TPU v7x, 512 devices: a whole 4x4x16 slice. The times are simulated.
512 devices in a mesh: state: 4 (over y), aux: 32 (over z, x_hi), cond: 4 (over x_lo, core).
Axes of the slice: x: 4 (x_hi: 2, x_lo: 2; x = x_hi * 2 + x_lo), y: 4, z: 16, core: 2. Of those that a mesh axis runs over, the one named last changes fastest.
Arguments:
- cond_pairs: float32 [128, 1024, 1024], P('aux', 'cond', 'state'), may hold values from -0.1875 to 0.1875
- val_pairs: float32 [128, 512, 512], P('aux', 'state', 'cond'), may hold values from -0.25 to 0.25
- screened: float32 [128, 128], replicated, may hold values from -0.046875 to 0.046875
- trials: float32 [8, 1024, 512], P('state', 'cond'), may hold values from -6 to 6
Outputs:
- response: float32 [8, 1024, 512], P('state', 'cond')
All inputs are finite; a program needn't handle non-finite values.
Results may differ from a plain program's by a relative error of at most 0.0001.
Values sent between devices are 32-bit elements; how exact they have to be, the bound alone decides.
No kernel may reach another device: no remote copies, remote signals or barrier semaphores. Data moves between devices by JAX's collectives and lax.ppermute only.
A program may use at most 64 MiB of HBM per device.

v0:
```python
import jax
import jax.numpy as jnp
from jax import lax
from jax.sharding import PartitionSpec as P

highest = lax.Precision.HIGHEST


def per_device(cond_pairs, val_pairs, screened, trials):
    aux_dev = cond_pairs.shape[0]
    aux_first = lax.axis_index("aux") * aux_dev
    own_rows = lax.dynamic_slice_in_dim(screened, aux_first, aux_dev, 0)
    coupled = jnp.einsum(
        "pq,qab->pab",
        own_rows,
        lax.all_gather(val_pairs, "aux", axis=0, tiled=True),
        precision=highest,
    )
    n_state = lax.axis_size("state")
    n_cond = lax.axis_size("cond")
    rows_state = coupled.shape[1]
    cols_cond = coupled.shape[2]
    pieces = lax.all_gather(coupled[None], ("state", "cond"), axis=0, tiled=True)
    coupled_full = pieces.reshape(n_state, n_cond, aux_dev, rows_state, cols_cond)
    coupled_full = coupled_full.transpose(2, 0, 3, 1, 4).reshape(
        aux_dev, n_state * rows_state, n_cond * cols_cond
    )
    gathered = lax.all_gather(trials, "cond", axis=1, tiled=True)
    mixture = jnp.einsum(
        "pcd,ndv->pncv",
        lax.all_gather(cond_pairs, "state", axis=2, tiled=True),
        gathered,
        precision=highest,
    )
    partial_value = jnp.einsum("pncv,pvw->ncw", mixture, coupled_full, precision=highest)
    result = lax.psum(partial_value, "aux")
    return result


def solution(mesh):
    in_specs = (P("aux", "cond", "state"), P("aux", "state", "cond"), P(), P("state", "cond", None))
    out_specs = P("state", "cond", None)
    return jax.shard_map(
        per_device, mesh=mesh, in_specs=in_specs, out_specs=out_specs, check_vma=False
    )
```

profile of v0, /device:TPU:24, one launch (start us, length us, event | category | flops | bytes accessed | tf_op | source)
XLA Modules:
  0.0 708.1 jit_solution(9609853267463221620)
XLA Ops:
  6.5 0.0 copy-start
  6.5 0.0 all-gather.10.cloned.1.call-start
  6.5 0.7 all-gather.10.cloned.1.call-update
  7.3 0.0 all-gather.8.cloned.1.call-start
  7.3 0.7 all-gather.8.cloned.1.call-update
  8.0 0.0 all-gather.6.cloned.1.call-start
  8.1 0.7 all-gather.6.cloned.1.call-update
  8.7 0.0 all-gather.12.cloned.1.call-start
  8.8 197.7 %all-gather.10.cloned.1.call-done = f32[128,128,128]{2,1,0:T(8,128)} async-done(((f32[4,128,128]{2,1,0:T(8,128)}), f32[128,128,128]{2,1,0:T(8,128)}) %all-gather.10.cloned.1.call-update) | async-done | bytes 8388624 | tf_op jit(solution)/shard_map/all_gather | solution.py:16
  206.5 0.0 copy-done
  206.5 12.5 %fusion = f32[4,128,128]{2,0,1:T(4,128)S(1)} fusion(f32[128,128,128]{2,1,0:T(8,128)} %all-gather.10.cloned.1.call-done, f32[128,128]{1,0:T(8,128)S(1)} %copy-done, s32[]{:T(128)S(6)} %select_n.3), kind=kOutput, calls=%fused_computation | convolution fusion | flops 100663296 | bytes 8652804 | tf_op jit(solution)/shard_map/pq,qab->pab/dot_general | solution.py:13
  219.0 0.7 copy.8
  219.7 0.0 all-gather.12.cloned.1.call-update
  219.8 0.2 all-reduce.2.cloned.1.call-start
  220.0 37.5 %all-gather.8.cloned.1.call-done = f32[4,256,1024]{2,1,0:T(8,128)} async-done(((f32[4,256,256]{2,1,0:T(8,128)}), f32[4,256,1024]{2,1,0:T(8,128)}) %all-gather.8.cloned.1.call-update) | async-done | bytes 4194320 | tf_op jit(solution)/shard_map/all_gather | solution.py:31
  257.5 57.9 %all-gather.6.cloned.1.call-done = f32[2,1024,512]{2,1,0:T(8,128)} async-done(((f32[2,256,512]{2,1,0:T(8,128)}), f32[2,1024,512]{2,1,0:T(8,128)}) %all-gather.6.cloned.1.call-update) | async-done | bytes 4194320 | tf_op jit(solution)/shard_map/all_gather | solution.py:28
  315.4 17.7 %fusion.2 = f32[2,512,4,256]{1,3,2,0:T(8,128)} fusion(f32[2,1024,512]{2,1,0:T(8,128)} %all-gather.6.cloned.1.call-done, f32[4,256,1024]{2,1,0:T(8,128)} %all-gather.8.cloned.1.call-done), kind=kOutput, calls=%fused_computation.2 | convolution fusion | flops 12884901888 | bytes 12582912 | tf_op jit(solution)/shard_map/pcd,ndv->pncv/dot_general | solution.py:29
  333.1 29.9 %all-gather.12.cloned.1.call-done = f32[64,128,128]{2,1,0:T(8,128)} async-done(((f32[4,128,128]{2,1,0:T(8,128)}), f32[64,128,128]{2,1,0:T(8,128)}) %all-gather.12.cloned.1.call-update) | async-done | bytes 4194320 | tf_op jit(solution)/shard_map/all_gather | solution.py:23
  363.0 7.0 copy.15
  369.9 5.5 reshape.13
  375.4 10.2 %fusion.7 = f32[2,256,512]{2,1,0:T(8,128)} fusion(f32[4,512,512,1]{2,1,0,3:T(8,128)} %reshape.13, f32[2,512,4,256]{1,3,2,0:T(8,128)} %fusion.2), kind=kOutput, calls=%fused_computation.8 | convolution fusion | flops 6442450944 | bytes 9437184 | tf_op jit(solution)/shard_map/pncv,pvw->ncw/dot_general | solution.py:35
  385.7 0.0 all-reduce.2.cloned.1.call-update
  385.7 313.6 %all-reduce.2.cloned.1.call-done = f32[2,256,512]{2,1,0:T(8,128)} async-done(((f32[2,256,512]{2,1,0:T(8,128)}), f32[2,256,512]{2,1,0:T(8,128)}) %all-reduce.2.cloned.1.call-update) | async-done | bytes 1048592 | tf_op jit(solution)/shard_map/psum | solution.py:36
  699.3 2.3 copy.17
Async XLA Ops:
  6.5 200.0 %copy-start = (f32[128,128]{1,0:T(8,128)S(1)}, f32[128,128]{1,0:T(8,128)}, u32[]{:S(2)}) copy-start(f32[128,128]{1,0:T(8,128)} %param.6) | copy-start | bytes 196612
  6.5 200.0 %all-gather.10.cloned.1.call-start = ((), (), s32[]{:S(2)}) async-start(), calls=%async_computation.2 | async-start | bytes 8650752 | tf_op jit(solution)/shard_map/all_gather | solution.py:16
  7.3 250.3 %all-gather.8.cloned.1.call-start = ((), (), s32[]{:S(2)}) async-start(), calls=%async_computation.1 | async-start | bytes 5242880 | tf_op jit(solution)/shard_map/all_gather | solution.py:31
  8.0 307.4 %all-gather.6.cloned.1.call-start = ((), (), s32[]{:S(2)}) async-start(), calls=%async_computation | async-start | bytes 5242880 | tf_op jit(solution)/shard_map/all_gather | solution.py:28
  8.7 354.3 %all-gather.12.cloned.1.call-start = ((), (), s32[]{:S(2)}) async-start(), calls=%async_computation.4 | async-start | bytes 4456448 | tf_op jit(solution)/shard_map/all_gather | solution.py:23
  219.8 479.5 %all-reduce.2.cloned.1.call-start = ((), (), s32[]{:S(2)}) async-start(), calls=%async_computation.3 | async-start | bytes 2097152 | tf_op jit(solution)/shard_map/psum | solution.py:36
Sparse Core Ops, SparseCore 0:
  10.4 196.0 all-gather.9
  208.6 48.8 all-gather.7
  259.6 55.7 all-gather.5
  317.4 45.5 all-gather.11
  385.8 313.4 all-reduce.1
where the time goes:
time: 708 us
  waiting for transfers between devices  639 us (90%)
  matrix products  40.4 us (6%)
  local copies, waits for them, and re-layouts  15.4 us (2%)
  between operations  13.1 us (2%)
    psum x1, waiting for transfers between devices, per_device(): result = lax.psum(partial_value, 'aux')  314 us
    all_gather x1, waiting for transfers between devices, per_device(): lax.all_gather(val_pairs, 'aux', axis=0, tiled=True)  198 us
    all_gather x1, waiting for transfers between devices, per_device(): gathered = lax.all_gather(trials, 'cond', axis=1, tiled=True)  57.9 us
    all_gather x1, waiting for transfers between devices, per_device(): lax.all_gather(cond_pairs, 'state', axis=2, tiled=True)  37.5 us
    all_gather x1, waiting for transfers between devices, per_device(): lax.all_gather(coupled[None], ('state', 'cond'), axis=0, tiled=True)  29.9 us
    dot_general x1, matrix products, per_device(): jnp.einsum('pcd,ndv->pncv', lax.all_gather(cond_pairs, 'state', axis=2, t...  17.7 us
  transfers between devices with their start and end apart: 5, of which 5 were waited for; matrix products, arithmetic and copies ran while one was open for 4% of the time, Pallas kernels for 0%

commit v1 on v0

v1 whole, which is shorter than its diff:
```python
import jax
import jax.numpy as jnp
from jax import lax
from jax.experimental import pallas as pl
from jax.experimental.pallas import tpu as pltpu
from jax.sharding import PartitionSpec as P


AXES = ("state", "aux", "cond")
SHIFTS = (0, 1, -1, 2)
highest = lax.Precision.HIGHEST
f32, bf16 = jnp.float32, jnp.bfloat16


def split(value):
    upper = value.astype(bf16)
    return upper, (value - upper.astype(f32)).astype(bf16)


def dot3(a, b):
    (ah, al), (bh, bl) = a, b
    dot = lambda x, y: jnp.dot(x, y, preferred_element_type=f32)
    return dot(ah, bh) + (dot(ah, bl) + dot(al, bh))


def mix_kernel(*refs):
    slabs, pieces, (mh, ml), (b_all, x_all, bh, bl, xh, xl, sems) = refs[:4], refs[4:8], refs[8:10], refs[10:]
    n_p, _, width = slabs[0].shape
    n_n = pieces[0].shape[0]
    s, k = lax.axis_index("state"), lax.axis_index("cond")
    copies = []
    for i, shift in enumerate(SHIFTS):
        start = pl.multiple_of(lax.rem(s + 4 - shift, 4) * width, width)
        copies.append(pltpu.make_async_copy(slabs[i], b_all.at[:, :, pl.ds(start, width)], sems.at[i]))
    for i in range(4):
        copies.append(pltpu.make_async_copy(pieces[i], x_all.at[jnp.bitwise_xor(k, i)], sems.at[4 + i]))
    for copy in copies:
        copy.start()
    for copy in copies[4:]:
        copy.wait()

    @pl.loop(0, 4)
    def _(j):
        for n in range(n_n):
            at = pl.ds(pl.multiple_of(j * width, width), width)
            xh[n, at, :], xl[n, at, :] = split(x_all[j, n])

    for copy in copies[:4]:
        copy.wait()

    @pl.loop(0, n_p)
    def _(p):
        bh[...], bl[...] = split(b_all[p])

        @pl.loop(0, n_n)
        def _(n):
            mh[n, p], ml[n, p] = split(dot3((bh[...], bl[...]), (xh[n], xl[n])))


def mix(slabs, pieces):
    n_p, rows, width = slabs[0].shape
    n_n, _, cols = pieces[0].shape
    any_spec = pl.BlockSpec(memory_space=pl.ANY)
    vmem = pl.BlockSpec(memory_space=pltpu.VMEM)
    shape = jax.ShapeDtypeStruct((n_n, n_p, rows, cols), bf16)
    return pl.pallas_call(
        mix_kernel,
        name="mix",
        out_shape=(shape, shape),
        in_specs=[any_spec] * 8,
        out_specs=(vmem, vmem),
        scratch_shapes=[
            pltpu.VMEM((n_p, rows, 4 * width), f32),
            pltpu.VMEM((4, n_n, width, cols), f32),
            pltpu.VMEM((rows, 4 * width), bf16),
            pltpu.VMEM((rows, 4 * width), bf16),
            pltpu.VMEM((n_n, 4 * width, cols), bf16),
            pltpu.VMEM((n_n, 4 * width, cols), bf16),
            pltpu.SemaphoreType.DMA((8,)),
        ],
        cost_estimate=pl.CostEstimate(flops=3 * 2 * n_n * n_p * rows * 4 * width * cols, transcendentals=0, bytes_accessed=1 << 24),
    )(*slabs, *pieces)


def product_into(out, m_pair, c_pair, n):
    mh, ml = m_pair
    ch, cl = c_pair
    out[...] = jnp.zeros_like(out)

    @pl.loop(0, mh.shape[1])
    def _(p):
        out[...] += dot3((mh[n, p], ml[n, p]), (ch[p], cl[p]))


def theirs_kernel(*refs):
    mh, ml, bands, mates, (out, ch, cl), (c_all, sems) = refs[0], refs[1], refs[2:6], refs[6:10], refs[10:13], refs[13:]
    n_x, n_p, v1, v2 = bands[0].shape
    s, half, core = lax.axis_index("state"), lax.rem(lax.axis_index("aux"), 2), lax.rem(lax.axis_index("cond"), 2)
    copies = []
    for i, shift in enumerate(SHIFTS):
        row = pl.multiple_of(lax.rem(s + 4 - shift, 4) * v1, v1)
        for x in range(n_x):
            for band, at in ((bands[i], core), (mates[i], 1 - core)):
                col = pl.multiple_of((2 * x + at) * v2, v2)
                target = c_all.at[:, pl.ds(row, v1), pl.ds(col, v2)]
                copies.append(pltpu.make_async_copy(band.at[x], target, sems.at[len(copies)]))
    for copy in copies:
        copy.start()
    for copy in copies:
        copy.wait()

    @pl.loop(0, n_p)
    def _(p):
        ch[p], cl[p] = split(c_all[p])

    product_into(out, (mh, ml), (ch, cl), 1 - half)


def mine_kernel(mh, ml, ch, cl, out):
    product_into(out, (mh, ml), (ch, cl), lax.rem(lax.axis_index("aux"), 2))


def respond(m_pair, bands, mates):
    _, n_p, rows, cols = m_pair[0].shape
    any_spec = pl.BlockSpec(memory_space=pl.ANY)
    vmem = pl.BlockSpec(memory_space=pltpu.VMEM)
    part = jax.ShapeDtypeStruct((rows, cols), f32)
    full = jax.ShapeDtypeStruct((n_p, cols, cols), bf16)
    cost = pl.CostEstimate(flops=3 * 2 * n_p * rows * cols * cols, transcendentals=0, bytes_accessed=1 << 23)
    theirs, ch, cl = pl.pallas_call(
        theirs_kernel,
        name="theirs",
        out_shape=(part, full, full),
        in_specs=[vmem] * 2 + [any_spec] * 8,
        out_specs=(vmem,) * 3,
        scratch_shapes=[pltpu.VMEM((n_p, cols, cols), f32), pltpu.SemaphoreType.DMA((16,))],
        cost_estimate=cost,
    )(*m_pair, *bands, *mates)
    mine = pl.pallas_call(
        mine_kernel, name="mine", out_shape=part, in_specs=[vmem] * 4, out_specs=vmem, cost_estimate=cost
    )(*m_pair, ch, cl)
    return theirs, mine


def moves(mesh, step):
    n_state, n_aux, n_cond = (mesh.shape[name] for name in AXES)

    def number(y, z, x, core):
        n_z = n_aux // 2
        y, z, x, core = y % n_state, z % n_z, x % 4, core % 2
        return (y * n_aux + z * 2 + x // 2) * n_cond + (x % 2) * 2 + core

    places = [
        (y, z, x, core)
        for y in range(n_state)
        for z in range(n_aux // 2)
        for x in range(4)
        for core in range(2)
    ]
    return [(number(*place), number(*step(*place))) for place in places]


def solution(mesh):
    to_core = moves(mesh, lambda y, z, x, c: (y, z, x, 1 - c))
    to_x = {d: moves(mesh, lambda y, z, x, c, d=d: (y, z, x + d, c)) for d in (1, -1, 2)}
    to_pair = moves(mesh, lambda y, z, x, c: (y, z, x ^ 1, c))
    to_y = {d: moves(mesh, lambda y, z, x, c, d=d: (y + d, z, x, c)) for d in (1, -1, 2)}
    n_z = mesh.shape["aux"] // 2
    along_z = [[2 * z + half for z in range(n_z)] for half in range(2)]

    def send(value, pairs):
        return lax.ppermute(value, AXES, pairs)

    def per_device(cond_pairs, val_pairs, screened, trials):
        n_p, rows, _ = cond_pairs.shape
        half = lax.axis_index("aux") % 2
        x_lo = lax.axis_index("cond") // 2

        slabs = [cond_pairs]
        for d in SHIFTS[1:]:
            slabs.append(send(cond_pairs, to_y[d]))
        far = jnp.stack([send(trials[0], to_x[1]), send(trials[1], to_x[-1])])
        pieces = [trials, send(trials, to_core), far, send(far, to_core)]

        qb, v1, v2 = val_pairs.shape
        spread = val_pairs.reshape(qb, n_z, v1 // n_z, v2).transpose(1, 0, 2, 3)
        spread = lax.all_to_all(spread, "aux", 0, 0, axis_index_groups=along_z)
        w = screened.reshape(n_z, 2, n_p, n_z, 2, qb)
        w = lax.dynamic_index_in_dim(w, half, 4, keepdims=False)
        w_own = lax.dynamic_index_in_dim(w, half, 1, keepdims=False)
        w_other = lax.dynamic_index_in_dim(w, 1 - half, 1, keepdims=False)
        product = lambda m: jnp.einsum("apzq,zqrv->aprv", m, spread, precision=highest)
        swapped = send(product(w_other), to_x[2])
        block = product(w_own) + swapped
        block = lax.all_to_all(block, "aux", 0, 0, axis_index_groups=along_z)
        block = block.transpose(1, 0, 2, 3).reshape(n_p, v1, v2)

        other = send(block, to_pair)
        two = jnp.stack([jnp.where(x_lo == 0, block, other), jnp.where(x_lo == 0, other, block)])
        bands = [two]
        for d in SHIFTS[1:]:
            bands.append(send(two, to_y[d]))
        mates = [send(band, to_core) for band in bands]

        theirs, mine = respond(mix(slabs, pieces), bands, mates)

        mine = mine + send(theirs, to_x[2])
        parts = mine.reshape(n_z, rows // n_z, mine.shape[1])
        parts = lax.all_to_all(parts, "aux", 0, 0, axis_index_groups=along_z)
        total = jnp.sum(parts, axis=0)
        total = lax.all_gather(total, "aux", axis=0, tiled=True, axis_index_groups=along_z)
        opposite = send(total, to_x[2])
        return jnp.stack([jnp.where(half == 0, total, opposite), jnp.where(half == 0, opposite, total)])

    in_specs = (P("aux", "cond", "state"), P("aux", "state", "cond"), P(), P("state", "cond", None))
    return jax.shard_map(per_device, mesh=mesh, in_specs=in_specs, out_specs=P("state", "cond", None), check_vma=False)
```

time: 708 us -> 280 us (0.40)
  waiting for transfers between devices: 639 us -> 80.2 us
  starting transfers between devices: 0.34 us -> 78.5 us
  blocking collectives: 0 us -> 73.7 us
  matrix products: 40.4 us -> 1.13 us
  Pallas kernels: 0 us -> 30.3 us
  between operations: 13.1 us -> 0.5 us
    all_gather x4 -> x0, waiting for transfers between devices: 323 us -> none  [the longest x1 198 us: per_device(): lax.all_gather(val_pairs, 'aux', axis=0, tiled=True)]
    psum x1 -> x0, waiting for transfers between devices: 314 us -> none  [per_device(): result = lax.psum(partial_value, 'aux')]
    ppermute x0 -> x18, waiting for transfers between devices: none -> 66.1 us  [send(): return lax.ppermute(value, AXES, pairs)]
    ppermute x0 -> x18, starting transfers between devices: none -> 56 us  [send(): return lax.ppermute(value, AXES, pairs)]
    all_to_all x0 -> x1, blocking collectives: none -> 40 us  [per_device(): parts = lax.all_to_all(parts, 'aux', 0, 0, axis_index_groups=along_z)]
    dot_general x3 -> x2, matrix products: 40.4 us -> 1.13 us  [per_device(): jnp.einsum('apzq,zqrv->aprv', m, spread, precision=highest)]
    all_gather x0 -> x1, blocking collectives: none -> 33.6 us  [per_device(): lax.all_gather(total, 'aux', axis=0, tiled=True, axis_index_groups=along_z)]
    pallas_call x0 -> x3, Pallas kernels: none -> 30.3 us  [the longest x1 14.6 us: mix(): pl.pallas_call(mix_kernel, name='mix', out_shape=(shape, shape), in_specs...]
  transfers between devices with their start and end apart: 5 -> 20, of which waited for: 5 -> 8; matrix products, arithmetic and copies ran while one was open for 4% -> 3% of each run, Pallas kernels for 0% -> 8%
where the time goes in v1:
time: 280 us; the launch traced here: 277 us
  waiting for transfers between devices  80.2 us (29%)
  starting transfers between devices  78.5 us (28%)
  blocking collectives  73.7 us (26%)
  Pallas kernels  30.3 us (11%)
  local copies, waits for them, and re-layouts  9.12 us (3%)
  other arithmetic  3.48 us (1%)
    ppermute x18, waiting for transfers between devices, send(): return lax.ppermute(value, AXES, pairs)  66.1 us
    ppermute x18, starting transfers between devices, send(): return lax.ppermute(value, AXES, pairs)  56 us
    all_to_all x1, blocking collectives, per_device(): parts = lax.all_to_all(parts, 'aux', 0, 0, axis_index_groups=along_z)  40 us
    all_gather x1, blocking collectives, per_device(): lax.all_gather(total, 'aux', axis=0, tiled=True, axis_index_groups=along_z)  33.6 us
    all_to_all x1, starting transfers between devices, per_device(): spread = lax.all_to_all(spread, 'aux', 0, 0, axis_index_groups=along_z)  15.2 us
    pallas_call x1, Pallas kernels, mix(): pl.pallas_call(mix_kernel, name='mix', out_shape=(shape, shape), in_specs...  14.6 us
    all_to_all x1, waiting for transfers between devices, per_device(): spread = lax.all_to_all(spread, 'aux', 0, 0, axis_index_groups=along_z)  12.5 us
    pallas_call x1, Pallas kernels, respond(): pl.pallas_call(theirs_kernel, name='theirs', out_shape=(part, full, full)...  9 us
  transfers between devices with their start and end apart: 20, of which 8 were waited for; matrix products, arithmetic and copies ran while one was open for 3% of the time, Pallas kernels for 8%

profile of v1, /device:TPU:24, one launch (start us, length us, event | category | flops | bytes accessed | tf_op | source)
XLA Modules:
  0.0 276.9 jit_solution(14391096222410381993)
XLA Ops:
  1.8 15.2 %all-to-all-start = ((f32[16,4,8,128]{3,1,2,0:T(4,128)}), f32[16,4,8,128]{3,1,2,0:T(4,128)S(1)}, u32[]{:S(2)}, u32[]{:S(2)}) async-start(f32[16,4,8,128]{3,1,2,0:T(4,128)} %copy.13), calls=%async_computation | async-start | bytes 524288 | tf_op jit(solution)/shard_map/all_to_all | solution.py:187
  17.1 4.1 %reshape.16 = f32[16,2,4,16,2,4]{5,4,3,2,1,0:T(2,128)S(1)} reshape(f32[128,128]{1,0:T(8,128)} %param.6) | data formatting | bytes 131072 | tf_op jit(solution)/shard_map/reshape | solution.py:188
  22.9 12.5 %all-to-all-done = f32[16,4,8,128]{3,1,2,0:T(4,128)S(1)} async-done(((f32[16,4,8,128]{3,1,2,0:T(4,128)}), f32[16,4,8,128]{3,1,2,0:T(4,128)S(1)}, u32[]{:S(2)}, u32[]{:S(2)}) %all-to-all-start) | async-done | bytes 262176 | tf_op jit(solution)/shard_map/all_to_all | solution.py:187
  36.0 4.9 %collective-permute-start.7 = (f32[16,4,8,128]{3,0,2,1:T(8,128)S(1)}, f32[16,4,8,128]{3,0,2,1:T(8,128)S(1)}, u32[]{:S(2)}, u32[]{:S(2)}) collective-permute-start(f32[16,4,8,128]{3,0,2,1:T(8,128)S(1)} %convolution_bitcast_fusion), channel_id=1, source_target_pairs={{0,4},{1,5},{2,6},{3,7},{4,0},{5,1},{6,2},{7,3},{8,12},{9,13},{10,... | collective-permute-start | bytes 786440 | tf_op jit(solution)/shard_map/ppermute | solution.py:172
  41.5 4.2 %collective-permute-done.7 = f32[16,4,8,128]{3,0,2,1:T(8,128)S(1)} collective-permute-done((f32[16,4,8,128]{3,0,2,1:T(8,128)S(1)}, f32[16,4,8,128]{3,0,2,1:T(8,128)S(1)}, u32[]{:S(2)}, u32[]{:S(2)}) %collective-permute-start.7) | collective-permute-done | bytes 262176 | tf_op jit(solution)/shard_map/ppermute | solution.py:172
  47.1 7.4 %all-to-all-start.1 = ((f32[16,4,8,128]{3,2,1,0:T(8,128)}), f32[16,4,8,128]{3,2,1,0:T(8,128)S(1)}, u32[]{:S(2)}, u32[]{:S(2)}) async-start(f32[16,4,8,128]{3,2,1,0:T(8,128)} %copy.17), calls=%async_computation.1 | async-start | bytes 524288 | tf_op jit(solution)/shard_map/all_to_all | solution.py:195
  54.6 3.4 %collective-permute-start.4 = (f32[256,512]{1,0:T(8,128)S(1)}, f32[256,512]{1,0:T(8,128)S(1)}, u32[]{:S(2)}, u32[]{:S(2)}) collective-permute-start(f32[256,512]{1,0:T(8,128)S(1)} %get-tuple-element.19), channel_id=1, source_target_pairs={{0,2},{1,3},{2,4},{3,5},{4,6},{5,7},{6,0},{7,1},{8,10},{9,11},{10,... | collective-permute-start | bytes 1572872 | tf_op jit(solution)/shard_map/ppermute | solution.py:172
  58.0 3.7 %collective-permute-start.5 = (f32[256,512]{1,0:T(8,128)S(1)}, f32[256,512]{1,0:T(8,128)}, u32[]{:S(2)}, u32[]{:S(2)}) collective-permute-start(f32[256,512]{1,0:T(8,128)S(1)} %get-tuple-element.20), channel_id=1, source_target_pairs={{0,6},{1,7},{2,0},{3,1},{4,2},{5,3},{6,4},{7,5},{8,14},{9,15},{10,... | collective-permute-start | bytes 1572872 | tf_op jit(solution)/shard_map/ppermute | solution.py:172
  61.6 1.9 collective-permute-start.3
  63.6 2.7 collective-permute-start.1
  66.2 4.4 %collective-permute-start = (f32[4,256,256]{2,1,0:T(8,128)}, f32[4,256,256]{2,1,0:T(8,128)}, u32[]{:S(2)}, u32[]{:S(2)}) collective-permute-start(f32[4,256,256]{2,1,0:T(8,128)} %refs_0_.1), channel_id=1, source_target_pairs={{0,128},{1,129},{2,130},{3,131},{4,132},{5,133},{6,134},{7,135},{8... | collective-permute-start | bytes 3145736 | tf_op jit(solution)/shard_map/ppermute | solution.py:172
  72.3 3.4 %collective-permute-start.8 = (f32[4,128,128]{2,1,0:T(8,128)S(1)}, f32[4,128,128]{2,1,0:T(8,128)S(1)}, u32[]{:S(2)}, u32[]{:S(2)}) collective-permute-start(f32[4,128,128]{2,1,0:T(8,128)S(1)} %copy_bitcast_fusion), channel_id=1, source_target_pairs={{0,2},{1,3},{2,0},{3,1},{4,6},{5,7},{6,4},{7,5},{8,10},{9,11},{10,... | collective-permute-start | bytes 786440 | tf_op jit(solution)/shard_map/ppermute | solution.py:172
  75.7 3.1 %collective-permute-start.2 = (f32[4,256,256]{2,1,0:T(8,128)}, f32[4,256,256]{2,1,0:T(8,128)}, u32[]{:S(2)}, u32[]{:S(2)}) collective-permute-start(f32[4,256,256]{2,1,0:T(8,128)} %refs_0_.1), channel_id=1, source_target_pairs={{0,256},{1,257},{2,258},{3,259},{4,260},{5,261},{6,262},{7,263},{8... | collective-permute-start | bytes 3145736 | tf_op jit(solution)/shard_map/ppermute | solution.py:172
  80.7 1.9 collective-permute-start.6
  82.8 3.4 %collective-permute-start.11 = (f32[2,4,128,128]{3,2,1,0:T(8,128)S(1)}, f32[2,4,128,128]{3,2,1,0:T(8,128)S(1)}, u32[]{:S(2)}, u32[]{:S(2)}) collective-permute-start(f32[2,4,128,128]{3,2,1,0:T(8,128)S(1)} %pad_maximum_fusion.2.refs_2_), channel_id=1, source_target_pairs={{0,256},{1,257},{2,258},{3,259},{4,260},{5,261},{6,262},{7,263},{8... | collective-permute-start | bytes 1572872 | tf_op jit(solution)/shard_map/ppermute | solution.py:172
  86.2 40.0 %collective-permute-done.1.refs_2_ = f32[4,256,256]{2,1,0:T(8,128)} collective-permute-done((f32[4,256,256]{2,1,0:T(8,128)}, f32[4,256,256]{2,1,0:T(8,128)}, u32[]{:S(2)}, u32[]{:S(2)}) %collective-permute-start.1) | collective-permute-done | bytes 1048608 | tf_op jit(solution)/shard_map/ppermute | solution.py:172
  126.3 1.9 collective-permute-start.10
  128.2 5.1 %collective-permute-start.9 = (f32[2,4,128,128]{3,2,1,0:T(8,128)S(1)}, f32[2,4,128,128]{3,2,1,0:T(8,128)S(1)}, u32[]{:S(2)}, u32[]{:S(2)}) collective-permute-start(f32[2,4,128,128]{3,2,1,0:T(8,128)S(1)} %pad_maximum_fusion.2.refs_2_), channel_id=1, source_target_pairs={{0,128},{1,129},{2,130},{3,131},{4,132},{5,133},{6,134},{7,135},{8... | collective-permute-start | bytes 1572872 | tf_op jit(solution)/shard_map/ppermute | solution.py:172
  133.3 1.9 collective-permute-start.12
  135.3 2.4 collective-permute-start.15
  137.7 5.1 %collective-permute-done.10.refs_4_ = f32[2,4,128,128]{3,2,1,0:T(8,128)S(1)} collective-permute-done((f32[2,4,128,128]{3,2,1,0:T(8,128)S(1)}, f32[2,4,128,128]{3,2,1,0:T(8,128)S(1)}, u32[]{:S(2)}, u32[]{:S(2)}) %collective-permute-start.10) | collective-permute-done | bytes 524320 | tf_op jit(solution)/shard_map/ppermute | solution.py:172
  142.8 1.9 collective-permute-start.14
  144.8 2.4 collective-permute-start.13
  147.2 14.6 %mix.1 = (bf16[2,4,256,512]{3,2,1,0:T(8,128)(2,1)}, bf16[2,4,256,512]{3,2,1,0:T(8,128)(2,1)}) custom-call(f32[4,256,256]{2,1,0:T(8,128)} %refs_0_.1, f32[4,256,256]{2,1,0:T(8,128)} %collective-permute-done.refs_1_, f32[4,256,256]{2,1,0:T(8,128)} %collective-permute-done.1.refs_2_, f32[4,256,256]{2,1,0:T(8,128)} %collective-permute-done.2.refs_3_, ...), custom_call_target="tpu_custom_call" | custom-call | flops 6442450944 | bytes 16777216 | tf_op jit(solution)/shard_map/mix/pallas_call | solution.py:66
  161.9 9.0 %theirs.1 = (f32[256,512]{1,0:T(8,128)}, bf16[4,512,512]{2,1,0:T(8,128)(2,1)}, bf16[4,512,512]{2,1,0:T(8,128)(2,1)}) custom-call(bf16[2,4,256,512]{3,2,1,0:T(8,128)(2,1)} %get-tuple-element.10.refs_0_.mh, bf16[2,4,256,512]{3,2,1,0:T(8,128)(2,1)} %get-tuple-element.11.refs_1_.ml, f32[2,4,128,128]{3,2,1,0:T(8,128)} %copy-done, f32[2,4,128,128]{3,2,1,0:T(8,128)} %copy-done.5, ...), custom_call_target="tpu_custom_call" | custom-call | flops 1610612736 | bytes 8388608 | tf_op jit(solution)/shard_map/theirs/pallas_call | solution.py:130
  170.9 3.7 %collective-permute-start.16 = (f32[256,512]{1,0:T(8,128)}, f32[256,512]{1,0:T(8,128)S(1)}, u32[]{:S(2)}, u32[]{:S(2)}) collective-permute-start(f32[256,512]{1,0:T(8,128)} %get-tuple-element.14), channel_id=1, source_target_pairs={{0,4},{1,5},{2,6},{3,7},{4,0},{5,1},{6,2},{7,3},{8,12},{9,13},{10,... | collective-permute-start | bytes 1572872 | tf_op jit(solution)/shard_map/ppermute | solution.py:172
  174.7 6.7 %mine.1 = f32[256,512]{1,0:T(8,128)} custom-call(bf16[2,4,256,512]{3,2,1,0:T(8,128)(2,1)} %get-tuple-element.10.refs_0_.mh, bf16[2,4,256,512]{3,2,1,0:T(8,128)(2,1)} %get-tuple-element.11.refs_1_.ml, bf16[4,512,512]{2,1,0:T(8,128)(2,1)} %get-tuple-element.12.ch, bf16[4,512,512]{2,1,0:T(8,128)(2,1)} %get-tuple-element.13.cl), custom_call_target="tpu_custom_call" | custom-call | flops 1610612736 | bytes 8388608 | tf_op jit(solution)/shard_map/mine/pallas_call | solution.py:139
  181.3 7.1 %collective-permute-done.16 = f32[256,512]{1,0:T(8,128)S(1)} collective-permute-done((f32[256,512]{1,0:T(8,128)}, f32[256,512]{1,0:T(8,128)S(1)}, u32[]{:S(2)}, u32[]{:S(2)}) %collective-permute-start.16) | collective-permute-done | bytes 524320 | tf_op jit(solution)/shard_map/ppermute | solution.py:172
  189.5 40.0 %all_to_all.15 = f32[16,16,512]{2,1,0:T(8,128)S(1)} all-to-all(f32[16,16,512]{2,1,0:T(8,128)S(1)} %bitcast.57), channel_id=1, replica_groups={{0,8,16,24,32,40,48,56,64,72,80,88,96,104,112,120},{4,12,20,28,36,44,52..., dimensions={0} | all-to-all | bytes 1048576 | tf_op jit(solution)/shard_map/all_to_all | solution.py:209
  229.6 33.6 %all_gather.3 = f32[256,512]{1,0:T(8,128)S(1)} all-gather(f32[16,512]{1,0:T(8,128)S(1)} %reduce_sum.9), channel_id=1, replica_groups={{0,8,16,24,32,40,48,56,64,72,80,88,96,104,112,120},{4,12,20,28,36,44,52..., dimensions={0}, use_global_device_ids=true | all-gather | bytes 557056 | tf_op jit(solution)/shard_map/all_gather | solution.py:211
  263.2 3.7 %collective-permute-start.17 = (f32[256,512]{1,0:T(8,128)S(1)}, f32[256,512]{1,0:T(8,128)S(1)}, u32[]{:S(2)}, u32[]{:S(2)}) collective-permute-start(f32[256,512]{1,0:T(8,128)S(1)} %all_gather.3), channel_id=1, source_target_pairs={{0,4},{1,5},{2,6},{3,7},{4,0},{5,1},{6,2},{7,3},{8,12},{9,13},{10,... | collective-permute-start | bytes 1572872 | tf_op jit(solution)/shard_map/ppermute | solution.py:172
  266.9 8.8 %collective-permute-done.17 = f32[256,512]{1,0:T(8,128)S(1)} collective-permute-done((f32[256,512]{1,0:T(8,128)S(1)}, f32[256,512]{1,0:T(8,128)S(1)}, u32[]{:S(2)}, u32[]{:S(2)}) %collective-permute-start.17) | collective-permute-done | bytes 524320 | tf_op jit(solution)/shard_map/ppermute | solution.py:172
  (42 shorter events, 12.1 us)
Async XLA Ops:
  1.8 33.6 %all-to-all-start = ((f32[16,4,8,128]{3,1,2,0:T(4,128)}), f32[16,4,8,128]{3,1,2,0:T(4,128)S(1)}, u32[]{:S(2)}, u32[]{:S(2)}) async-start(f32[16,4,8,128]{3,1,2,0:T(4,128)} %copy.13), calls=%async_computation | async-start | bytes 524288 | tf_op jit(solution)/shard_map/all_to_all | solution.py:187
  22.2 32.3 %copy-start.1 = (f32[2,256,512]{2,1,0:T(8,128)S(1)}, f32[2,256,512]{2,1,0:T(8,128)}, u32[]{:S(2)}) copy-start(f32[2,256,512]{2,1,0:T(8,128)} %refs_4_.1) | copy-start | bytes 3145732
  36.0 9.8 %collective-permute-start.7 = (f32[16,4,8,128]{3,0,2,1:T(8,128)S(1)}, f32[16,4,8,128]{3,0,2,1:T(8,128)S(1)}, u32[]{:S(2)}, u32[]{:S(2)}) collective-permute-start(f32[16,4,8,128]{3,0,2,1:T(8,128)S(1)} %convolution_bitcast_fusion), channel_id=1, source_target_pairs={{0,4},{1,5},{2,6},{3,7},{4,0},{5,1},{6,2},{7,3},{8,12},{9,13},{10,... | collective-permute-start | bytes 786440 | tf_op jit(solution)/shard_map/ppermute | solution.py:172
  47.1 25.1 %all-to-all-start.1 = ((f32[16,4,8,128]{3,2,1,0:T(8,128)}), f32[16,4,8,128]{3,2,1,0:T(8,128)S(1)}, u32[]{:S(2)}, u32[]{:S(2)}) async-start(f32[16,4,8,128]{3,2,1,0:T(8,128)} %copy.17), calls=%async_computation.1 | async-start | bytes 524288 | tf_op jit(solution)/shard_map/all_to_all | solution.py:195
  54.6 17.7 %collective-permute-start.4 = (f32[256,512]{1,0:T(8,128)S(1)}, f32[256,512]{1,0:T(8,128)S(1)}, u32[]{:S(2)}, u32[]{:S(2)}) collective-permute-start(f32[256,512]{1,0:T(8,128)S(1)} %get-tuple-element.19), channel_id=1, source_target_pairs={{0,2},{1,3},{2,4},{3,5},{4,6},{5,7},{6,0},{7,1},{8,10},{9,11},{10,... | collective-permute-start | bytes 1572872 | tf_op jit(solution)/shard_map/ppermute | solution.py:172
  58.0 17.7 %collective-permute-start.5 = (f32[256,512]{1,0:T(8,128)S(1)}, f32[256,512]{1,0:T(8,128)}, u32[]{:S(2)}, u32[]{:S(2)}) collective-permute-start(f32[256,512]{1,0:T(8,128)S(1)} %get-tuple-element.20), channel_id=1, source_target_pairs={{0,6},{1,7},{2,0},{3,1},{4,2},{5,3},{6,4},{7,5},{8,14},{9,15},{10,... | collective-permute-start | bytes 1572872 | tf_op jit(solution)/shard_map/ppermute | solution.py:172
  61.6 21.1 %collective-permute-start.3 = (f32[2,256,512]{2,1,0:T(8,128)S(1)}, f32[2,256,512]{2,1,0:T(8,128)}, u32[]{:S(2)}, u32[]{:S(2)}) collective-permute-start(f32[2,256,512]{2,1,0:T(8,128)S(1)} %copy-done.1), channel_id=1, source_target_pairs={{0,1},{1,0},{2,3},{3,2},{4,5},{5,4},{6,7},{7,6},{8,9},{9,8},{10,11... | collective-permute-start | bytes 3145736 | tf_op jit(solution)/shard_map/ppermute | solution.py:172
  63.6 62.7 %collective-permute-start.1 = (f32[4,256,256]{2,1,0:T(8,128)}, f32[4,256,256]{2,1,0:T(8,128)}, u32[]{:S(2)}, u32[]{:S(2)}) collective-permute-start(f32[4,256,256]{2,1,0:T(8,128)} %refs_0_.1), channel_id=1, source_target_pairs={{0,384},{1,385},{2,386},{3,387},{4,388},{5,389},{6,390},{7,391},{8... | collective-permute-start | bytes 3145736 | tf_op jit(solution)/shard_map/ppermute | solution.py:172
  66.2 61.9 %collective-permute-start = (f32[4,256,256]{2,1,0:T(8,128)}, f32[4,256,256]{2,1,0:T(8,128)}, u32[]{:S(2)}, u32[]{:S(2)}) collective-permute-start(f32[4,256,256]{2,1,0:T(8,128)} %refs_0_.1), channel_id=1, source_target_pairs={{0,128},{1,129},{2,130},{3,131},{4,132},{5,133},{6,134},{7,135},{8... | collective-permute-start | bytes 3145736 | tf_op jit(solution)/shard_map/ppermute | solution.py:172
  72.3 8.5 %collective-permute-start.8 = (f32[4,128,128]{2,1,0:T(8,128)S(1)}, f32[4,128,128]{2,1,0:T(8,128)S(1)}, u32[]{:S(2)}, u32[]{:S(2)}) collective-permute-start(f32[4,128,128]{2,1,0:T(8,128)S(1)} %copy_bitcast_fusion), channel_id=1, source_target_pairs={{0,2},{1,3},{2,0},{3,1},{4,6},{5,7},{6,4},{7,5},{8,10},{9,11},{10,... | collective-permute-start | bytes 786440 | tf_op jit(solution)/shard_map/ppermute | solution.py:172
  75.7 57.7 %collective-permute-start.2 = (f32[4,256,256]{2,1,0:T(8,128)}, f32[4,256,256]{2,1,0:T(8,128)}, u32[]{:S(2)}, u32[]{:S(2)}) collective-permute-start(f32[4,256,256]{2,1,0:T(8,128)} %refs_0_.1), channel_id=1, source_target_pairs={{0,256},{1,257},{2,258},{3,259},{4,260},{5,261},{6,262},{7,263},{8... | collective-permute-start | bytes 3145736 | tf_op jit(solution)/shard_map/ppermute | solution.py:172
  79.9 67.3 %copy-start.2 = (f32[2,256,512]{2,1,0:T(8,128)}, f32[2,256,512]{2,1,0:T(8,128)S(1)}, u32[]{:S(2)}) copy-start(f32[2,256,512]{2,1,0:T(8,128)S(1)} %pad_maximum_fusion.refs_6_) | copy-start | bytes 3145732
  80.7 66.4 %collective-permute-start.6 = (f32[2,256,512]{2,1,0:T(8,128)S(1)}, f32[2,256,512]{2,1,0:T(8,128)}, u32[]{:S(2)}, u32[]{:S(2)}) collective-permute-start(f32[2,256,512]{2,1,0:T(8,128)S(1)} %pad_maximum_fusion.refs_6_), channel_id=1, source_target_pairs={{0,1},{1,0},{2,3},{3,2},{4,5},{5,4},{6,7},{7,6},{8,9},{9,8},{10,11... | collective-permute-start | bytes 3145736 | tf_op jit(solution)/shard_map/ppermute | solution.py:172
  82.8 79.1 %copy-start = (f32[2,4,128,128]{3,2,1,0:T(8,128)}, f32[2,4,128,128]{3,2,1,0:T(8,128)S(1)}, u32[]{:S(2)}) copy-start(f32[2,4,128,128]{3,2,1,0:T(8,128)S(1)} %pad_maximum_fusion.2.refs_2_) | copy-start | bytes 1572868
  82.8 52.5 %collective-permute-start.11 = (f32[2,4,128,128]{3,2,1,0:T(8,128)S(1)}, f32[2,4,128,128]{3,2,1,0:T(8,128)S(1)}, u32[]{:S(2)}, u32[]{:S(2)}) collective-permute-start(f32[2,4,128,128]{3,2,1,0:T(8,128)S(1)} %pad_maximum_fusion.2.refs_2_), channel_id=1, source_target_pairs={{0,256},{1,257},{2,258},{3,259},{4,260},{5,261},{6,262},{7,263},{8... | collective-permute-start | bytes 1572872 | tf_op jit(solution)/shard_map/ppermute | solution.py:172
  126.3 16.6 %collective-permute-start.10 = (f32[2,4,128,128]{3,2,1,0:T(8,128)S(1)}, f32[2,4,128,128]{3,2,1,0:T(8,128)S(1)}, u32[]{:S(2)}, u32[]{:S(2)}) collective-permute-start(f32[2,4,128,128]{3,2,1,0:T(8,128)S(1)} %pad_maximum_fusion.2.refs_2_), channel_id=1, source_target_pairs={{0,384},{1,385},{2,386},{3,387},{4,388},{5,389},{6,390},{7,391},{8... | collective-permute-start | bytes 1572872 | tf_op jit(solution)/shard_map/ppermute | solution.py:172
  128.2 16.6 %collective-permute-start.9 = (f32[2,4,128,128]{3,2,1,0:T(8,128)S(1)}, f32[2,4,128,128]{3,2,1,0:T(8,128)S(1)}, u32[]{:S(2)}, u32[]{:S(2)}) collective-permute-start(f32[2,4,128,128]{3,2,1,0:T(8,128)S(1)} %pad_maximum_fusion.2.refs_2_), channel_id=1, source_target_pairs={{0,128},{1,129},{2,130},{3,131},{4,132},{5,133},{6,134},{7,135},{8... | collective-permute-start | bytes 1572872 | tf_op jit(solution)/shard_map/ppermute | solution.py:172
  133.3 28.5 %collective-permute-start.12 = (f32[2,4,128,128]{3,2,1,0:T(8,128)S(1)}, f32[2,4,128,128]{3,2,1,0:T(8,128)}, u32[]{:S(2)}, u32[]{:S(2)}) collective-permute-start(f32[2,4,128,128]{3,2,1,0:T(8,128)S(1)} %pad_maximum_fusion.2.refs_2_), channel_id=1, source_target_pairs={{0,1},{1,0},{2,3},{3,2},{4,5},{5,4},{6,7},{7,6},{8,9},{9,8},{10,11... | collective-permute-start | bytes 1572872 | tf_op jit(solution)/shard_map/ppermute | solution.py:172
  135.3 26.6 %copy-start.3 = (f32[2,4,128,128]{3,2,1,0:T(8,128)}, f32[2,4,128,128]{3,2,1,0:T(8,128)S(1)}, u32[]{:S(2)}) copy-start(f32[2,4,128,128]{3,2,1,0:T(8,128)S(1)} %collective-permute-done.11.refs_5_) | copy-start | bytes 1572868
  135.3 26.6 %collective-permute-start.15 = (f32[2,4,128,128]{3,2,1,0:T(8,128)S(1)}, f32[2,4,128,128]{3,2,1,0:T(8,128)}, u32[]{:S(2)}, u32[]{:S(2)}) collective-permute-start(f32[2,4,128,128]{3,2,1,0:T(8,128)S(1)} %collective-permute-done.11.refs_5_), channel_id=1, source_target_pairs={{0,1},{1,0},{2,3},{3,2},{4,5},{5,4},{6,7},{7,6},{8,9},{9,8},{10,11... | collective-permute-start | bytes 1572872 | tf_op jit(solution)/shard_map/ppermute | solution.py:172
  142.8 19.0 %copy-start.4 = (f32[2,4,128,128]{3,2,1,0:T(8,128)}, f32[2,4,128,128]{3,2,1,0:T(8,128)S(1)}, u32[]{:S(2)}) copy-start(f32[2,4,128,128]{3,2,1,0:T(8,128)S(1)} %collective-permute-done.10.refs_4_) | copy-start | bytes 1572868
  142.8 19.1 %collective-permute-start.14 = (f32[2,4,128,128]{3,2,1,0:T(8,128)S(1)}, f32[2,4,128,128]{3,2,1,0:T(8,128)}, u32[]{:S(2)}, u32[]{:S(2)}) collective-permute-start(f32[2,4,128,128]{3,2,1,0:T(8,128)S(1)} %collective-permute-done.10.refs_4_), channel_id=1, source_target_pairs={{0,1},{1,0},{2,3},{3,2},{4,5},{5,4},{6,7},{7,6},{8,9},{9,8},{10,11... | collective-permute-start | bytes 1572872 | tf_op jit(solution)/shard_map/ppermute | solution.py:172
  144.8 17.1 %copy-start.5 = (f32[2,4,128,128]{3,2,1,0:T(8,128)}, f32[2,4,128,128]{3,2,1,0:T(8,128)S(1)}, u32[]{:S(2)}) copy-start(f32[2,4,128,128]{3,2,1,0:T(8,128)S(1)} %collective-permute-done.9.refs_3_) | copy-start | bytes 1572868
  144.8 17.1 %collective-permute-start.13 = (f32[2,4,128,128]{3,2,1,0:T(8,128)S(1)}, f32[2,4,128,128]{3,2,1,0:T(8,128)}, u32[]{:S(2)}, u32[]{:S(2)}) collective-permute-start(f32[2,4,128,128]{3,2,1,0:T(8,128)S(1)} %collective-permute-done.9.refs_3_), channel_id=1, source_target_pairs={{0,1},{1,0},{2,3},{3,2},{4,5},{5,4},{6,7},{7,6},{8,9},{9,8},{10,11... | collective-permute-start | bytes 1572872 | tf_op jit(solution)/shard_map/ppermute | solution.py:172
  170.9 17.4 %collective-permute-start.16 = (f32[256,512]{1,0:T(8,128)}, f32[256,512]{1,0:T(8,128)S(1)}, u32[]{:S(2)}, u32[]{:S(2)}) collective-permute-start(f32[256,512]{1,0:T(8,128)} %get-tuple-element.14), channel_id=1, source_target_pairs={{0,4},{1,5},{2,6},{3,7},{4,0},{5,1},{6,2},{7,3},{8,12},{9,13},{10,... | collective-permute-start | bytes 1572872 | tf_op jit(solution)/shard_map/ppermute | solution.py:172
  263.2 12.6 %collective-permute-start.17 = (f32[256,512]{1,0:T(8,128)S(1)}, f32[256,512]{1,0:T(8,128)S(1)}, u32[]{:S(2)}, u32[]{:S(2)}) collective-permute-start(f32[256,512]{1,0:T(8,128)S(1)} %all_gather.3), channel_id=1, source_target_pairs={{0,4},{1,5},{2,6},{3,7},{4,0},{5,1},{6,2},{7,3},{8,12},{9,13},{10,... | collective-permute-start | bytes 1572872 | tf_op jit(solution)/shard_map/ppermute | solution.py:172

commit v2 on v1

--- a/solution.py
+++ b/solution.py
@@ -78,24 +78,17 @@
             pltpu.VMEM((n_n, 4 * width, cols), bf16),
             pltpu.SemaphoreType.DMA((8,)),
         ],
-        cost_estimate=pl.CostEstimate(flops=3 * 2 * n_n * n_p * rows * 4 * width * cols, transcendentals=0, bytes_accessed=1 << 24),
+        compiler_params=pltpu.CompilerParams(vmem_limit_bytes=28 << 20),
+        cost_estimate=pl.CostEstimate(
+            flops=3 * 2 * n_n * n_p * rows * 4 * width * cols, transcendentals=0, bytes_accessed=1 << 24
+        ),
     )(*slabs, *pieces)
 
 
-def product_into(out, m_pair, c_pair, n):
-    mh, ml = m_pair
-    ch, cl = c_pair
-    out[...] = jnp.zeros_like(out)
-
-    @pl.loop(0, mh.shape[1])
-    def _(p):
-        out[...] += dot3((mh[n, p], ml[n, p]), (ch[p], cl[p]))
-
-
-def theirs_kernel(*refs):
-    mh, ml, bands, mates, (out, ch, cl), (c_all, sems) = refs[0], refs[1], refs[2:6], refs[6:10], refs[10:13], refs[13:]
+def respond_kernel(*refs):
+    mh, ml, bands, mates, (out, c_all, ch, cl, sems) = refs[0], refs[1], refs[2:6], refs[6:10], refs[10:]
     n_x, n_p, v1, v2 = bands[0].shape
-    s, half, core = lax.axis_index("state"), lax.rem(lax.axis_index("aux"), 2), lax.rem(lax.axis_index("cond"), 2)
+    s, core = lax.axis_index("state"), lax.rem(lax.axis_index("cond"), 2)
     copies = []
     for i, shift in enumerate(SHIFTS):
         row = pl.multiple_of(lax.rem(s + 4 - shift, 4) * v1, v1)
@@ -106,40 +99,40 @@
                 copies.append(pltpu.make_async_copy(band.at[x], target, sems.at[len(copies)]))
     for copy in copies:
         copy.start()
+    out[...] = jnp.zeros_like(out)
     for copy in copies:
         copy.wait()
 
     @pl.loop(0, n_p)
     def _(p):
-        ch[p], cl[p] = split(c_all[p])
-
-    product_into(out, (mh, ml), (ch, cl), 1 - half)
-
-
-def mine_kernel(mh, ml, ch, cl, out):
-    product_into(out, (mh, ml), (ch, cl), lax.rem(lax.axis_index("aux"), 2))
+        ch[...], cl[...] = split(c_all[p])
+
+        @pl.loop(0, out.shape[0])
+        def _(n):
+            out[n] += dot3((mh[n, p], ml[n, p]), (ch[...], cl[...]))
 
 
 def respond(m_pair, bands, mates):
-    _, n_p, rows, cols = m_pair[0].shape
+    n_n, n_p, rows, cols = m_pair[0].shape
     any_spec = pl.BlockSpec(memory_space=pl.ANY)
     vmem = pl.BlockSpec(memory_space=pltpu.VMEM)
-    part = jax.ShapeDtypeStruct((rows, cols), f32)
-    full = jax.ShapeDtypeStruct((n_p, cols, cols), bf16)
-    cost = pl.CostEstimate(flops=3 * 2 * n_p * rows * cols * cols, transcendentals=0, bytes_accessed=1 << 23)
-    theirs, ch, cl = pl.pallas_call(
-        theirs_kernel,
-        name="theirs",
-        out_shape=(part, full, full),
+    return pl.pallas_call(
+        respond_kernel,
+        name="respond",
+        out_shape=jax.ShapeDtypeStruct((n_n, rows, cols), f32),
         in_specs=[vmem] * 2 + [any_spec] * 8,
-        out_specs=(vmem,) * 3,
-        scratch_shapes=[pltpu.VMEM((n_p, cols, cols), f32), pltpu.SemaphoreType.DMA((16,))],
-        cost_estimate=cost,
+        out_specs=vmem,
+        scratch_shapes=[
+            pltpu.VMEM((n_p, cols, cols), f32),
+            pltpu.VMEM((cols, cols), bf16),
+            pltpu.VMEM((cols, cols), bf16),
+            pltpu.SemaphoreType.DMA((16,)),
+        ],
+        compiler_params=pltpu.CompilerParams(vmem_limit_bytes=28 << 20),
+        cost_estimate=pl.CostEstimate(
+            flops=3 * 2 * n_n * n_p * rows * cols * cols, transcendentals=0, bytes_accessed=1 << 24
+        ),
     )(*m_pair, *bands, *mates)
-    mine = pl.pallas_call(
-        mine_kernel, name="mine", out_shape=part, in_specs=[vmem] * 4, out_specs=vmem, cost_estimate=cost
-    )(*m_pair, ch, cl)
-    return theirs, mine
 
 
 def moves(mesh, step):
@@ -162,36 +155,42 @@
 
 def solution(mesh):
     to_core = moves(mesh, lambda y, z, x, c: (y, z, x, 1 - c))
-    to_x = {d: moves(mesh, lambda y, z, x, c, d=d: (y, z, x + d, c)) for d in (1, -1, 2)}
+    to_x = moves(mesh, lambda y, z, x, c: (y, z, x + 2, c))
     to_pair = moves(mesh, lambda y, z, x, c: (y, z, x ^ 1, c))
     to_y = {d: moves(mesh, lambda y, z, x, c, d=d: (y + d, z, x, c)) for d in (1, -1, 2)}
     n_z = mesh.shape["aux"] // 2
     along_z = [[2 * z + half for z in range(n_z)] for half in range(2)]
+    fours = [[4 * g + t for t in range(4)] for g in range(n_z // 2)]
+    along_fours = [[4 * g + t for g in range(n_z // 2)] for t in range(4)]
 
     def send(value, pairs):
         return lax.ppermute(value, AXES, pairs)
 
     def per_device(cond_pairs, val_pairs, screened, trials):
-        n_p, rows, _ = cond_pairs.shape
+        n_p, _, _ = cond_pairs.shape
         half = lax.axis_index("aux") % 2
         x_lo = lax.axis_index("cond") // 2
 
         slabs = [cond_pairs]
         for d in SHIFTS[1:]:
             slabs.append(send(cond_pairs, to_y[d]))
-        far = jnp.stack([send(trials[0], to_x[1]), send(trials[1], to_x[-1])])
-        pieces = [trials, send(trials, to_core), far, send(far, to_core)]
+        far = send(trials, to_pair)
+        pieces = [trials, send(trials, to_core), far]
+        pieces.append(send(far, to_core))
 
         qb, v1, v2 = val_pairs.shape
         spread = val_pairs.reshape(qb, n_z, v1 // n_z, v2).transpose(1, 0, 2, 3)
         spread = lax.all_to_all(spread, "aux", 0, 0, axis_index_groups=along_z)
-        w = screened.reshape(n_z, 2, n_p, n_z, 2, qb)
-        w = lax.dynamic_index_in_dim(w, half, 4, keepdims=False)
-        w_own = lax.dynamic_index_in_dim(w, half, 1, keepdims=False)
-        w_other = lax.dynamic_index_in_dim(w, 1 - half, 1, keepdims=False)
-        product = lambda m: jnp.einsum("apzq,zqrv->aprv", m, spread, precision=highest)
-        swapped = send(product(w_other), to_x[2])
-        block = product(w_own) + swapped
+        n_q = screened.shape[0]
+        q = lax.broadcasted_iota(jnp.int32, (n_q, n_q // 2), 0)
+        j = lax.broadcasted_iota(jnp.int32, (n_q, n_q // 2), 1)
+        picks = (q == (j // qb) * (2 * qb) + half * qb + j % qb).astype(f32)
+        columns = jnp.dot(screened, picks, precision=highest)
+        spread = spread.reshape(n_q // 2, v1 // n_z, v2)
+        product = jnp.einsum("pq,qrv->prv", columns, spread, precision=highest)
+        product = product.reshape(n_z, 2, n_p, v1 // n_z, v2)
+        swapped = send(lax.dynamic_index_in_dim(product, 1 - half, 1, keepdims=False), to_x)
+        block = lax.dynamic_index_in_dim(product, half, 1, keepdims=False) + swapped
         block = lax.all_to_all(block, "aux", 0, 0, axis_index_groups=along_z)
         block = block.transpose(1, 0, 2, 3).reshape(n_p, v1, v2)
 
@@ -202,15 +201,15 @@
             bands.append(send(two, to_y[d]))
         mates = [send(band, to_core) for band in bands]
 
-        theirs, mine = respond(mix(slabs, pieces), bands, mates)
-
-        mine = mine + send(theirs, to_x[2])
-        parts = mine.reshape(n_z, rows // n_z, mine.shape[1])
-        parts = lax.all_to_all(parts, "aux", 0, 0, axis_index_groups=along_z)
-        total = jnp.sum(parts, axis=0)
-        total = lax.all_gather(total, "aux", axis=0, tiled=True, axis_index_groups=along_z)
-        opposite = send(total, to_x[2])
-        return jnp.stack([jnp.where(half == 0, total, opposite), jnp.where(half == 0, opposite, total)])
+        m_pair = mix(slabs, pieces)
+        partial = respond(m_pair, bands, mates)
+
+        swap = lambda value, groups: lax.all_to_all(value, "aux", 0, 0, axis_index_groups=groups)
+        parts = jnp.sum(swap(partial.reshape(4, -1, partial.shape[2]), fours), axis=0)
+        parts = jnp.sum(swap(parts.reshape(n_z // 2, -1, parts.shape[1]), along_fours), axis=0)
+        total = lax.all_gather(parts, "aux", axis=0, tiled=True, axis_index_groups=along_fours)
+        total = swap(jnp.broadcast_to(total, (4, *total.shape)), fours)
+        return total.reshape(partial.shape)
 
     in_specs = (P("aux", "cond", "state"), P("aux", "state", "cond"), P(), P("state", "cond", None))
     return jax.shard_map(per_device, mesh=mesh, in_specs=in_specs, out_specs=P("state", "cond", None), check_vma=False)

time: 280 us -> 249 us (0.89)
  blocking collectives: 73.7 us -> 93.9 us
  starting transfers between devices: 78.5 us -> 63.5 us
  waiting for transfers between devices: 80.2 us -> 66 us
  Pallas kernels: 30.3 us -> 17.9 us
  local copies, waits for them, and re-layouts: 9.12 us -> 3.95 us
    all_to_all x1 -> x3, blocking collectives: 40 us -> 65.3 us  [per_device(): lax.all_to_all(value, 'aux', 0, 0, axis_index_groups=groups)]
    ppermute x18 -> x15, waiting for transfers between devices: 66.1 us -> 42.8 us  [send(): return lax.ppermute(value, AXES, pairs)]
    ppermute x18 -> x15, starting transfers between devices: 56 us -> 40.9 us  [send(): return lax.ppermute(value, AXES, pairs)]
    pallas_call x2 -> x1, Pallas kernels: 15.7 us -> 5.96 us  [respond(): pl.pallas_call(respond_kernel, name='respond', out_shape=jax.ShapeDtypeSt...]
    all_to_all x1, waiting for transfers between devices: 12.5 us -> 17.9 us  [per_device(): spread = lax.all_to_all(spread, 'aux', 0, 0, axis_index_groups=along_z)]
    all_gather x1, blocking collectives: 33.6 us -> 28.6 us  [per_device(): lax.all_gather(parts, 'aux', axis=0, tiled=True, axis_index_groups=along_...]
    reshape x1 -> x0, local copies, waits for them, and re-layouts: 4.07 us -> none  [per_device(): w = screened.reshape(n_z, 2, n_p, n_z, 2, qb)]
    all_to_all x1, waiting for transfers between devices: 1.57 us -> 5.3 us  [per_device(): block = lax.all_to_all(block, 'aux', 0, 0, axis_index_groups=along_z)]
  transfers between devices with their start and end apart: 20 -> 17, of which waited for: 8 -> 9; matrix products, arithmetic and copies ran while one was open for 3% -> 1% of each run, Pallas kernels for 8% -> 5%
where the time goes in v2:
time: 249 us; the launch traced here: 248 us
  blocking collectives  93.9 us (38%)
  waiting for transfers between devices  66 us (27%)
  starting transfers between devices  63.5 us (26%)
  Pallas kernels  17.9 us (7%)
  local copies, waits for them, and re-layouts  3.95 us (2%)
    all_to_all x3, blocking collectives, per_device(): lax.all_to_all(value, 'aux', 0, 0, axis_index_groups=groups)  65.3 us
    ppermute x15, waiting for transfers between devices, send(): return lax.ppermute(value, AXES, pairs)  42.8 us
    ppermute x15, starting transfers between devices, send(): return lax.ppermute(value, AXES, pairs)  40.9 us
    all_gather x1, blocking collectives, per_device(): lax.all_gather(parts, 'aux', axis=0, tiled=True, axis_index_groups=along_...  28.6 us
    all_to_all x1, waiting for transfers between devices, per_device(): spread = lax.all_to_all(spread, 'aux', 0, 0, axis_index_groups=along_z)  17.9 us
    all_to_all x1, starting transfers between devices, per_device(): spread = lax.all_to_all(spread, 'aux', 0, 0, axis_index_groups=along_z)  15.2 us
    pallas_call x1, Pallas kernels, mix(): pl.pallas_call(mix_kernel, name='mix', out_shape=(shape, shape), in_specs...  11.9 us
    all_to_all x1, starting transfers between devices, per_device(): block = lax.all_to_all(block, 'aux', 0, 0, axis_index_groups=along_z)  7.39 us
  transfers between devices with their start and end apart: 17, of which 9 were waited for; matrix products, arithmetic and copies ran while one was open for 1% of the time, Pallas kernels for 5%

profile of v2, /device:TPU:24, one launch (start us, length us, event | category | flops | bytes accessed | tf_op | source)
XLA Modules:
  0.0 248.4 jit_solution(10361479386804092139)
XLA Ops:
  0.0 1.9 copy.21
  1.9 15.2 %all-to-all-start = ((f32[16,4,8,128]{3,1,2,0:T(4,128)}), f32[16,4,8,128]{3,1,2,0:T(4,128)S(1)}, u32[]{:S(2)}, u32[]{:S(2)}) async-start(f32[16,4,8,128]{3,1,2,0:T(4,128)} %bitcast.4), calls=%async_computation | async-start | bytes 524288 | tf_op jit(solution)/shard_map/all_to_all | solution.py:183
  17.5 17.9 %all-to-all-done = f32[16,4,8,128]{3,1,2,0:T(4,128)S(1)} async-done(((f32[16,4,8,128]{3,1,2,0:T(4,128)}), f32[16,4,8,128]{3,1,2,0:T(4,128)S(1)}, u32[]{:S(2)}, u32[]{:S(2)}) %all-to-all-start) | async-done | bytes 262176 | tf_op jit(solution)/shard_map/all_to_all | solution.py:183
  36.2 4.9 %collective-permute-start.6 = (f32[16,4,8,128]{3,2,1,0:T(8,128)S(1)}, f32[16,4,8,128]{3,2,1,0:T(8,128)S(1)}, u32[]{:S(2)}, u32[]{:S(2)}) collective-permute-start(f32[16,4,8,128]{3,2,1,0:T(8,128)S(1)} %bitcast.42), channel_id=1, source_target_pairs={{0,4},{1,5},{2,6},{3,7},{4,0},{5,1},{6,2},{7,3},{8,12},{9,13},{10,... | collective-permute-start | bytes 786440 | tf_op jit(solution)/shard_map/ppermute | solution.py:167
  41.2 4.8 %collective-permute-done.6 = f32[16,4,8,128]{3,2,1,0:T(8,128)S(1)} collective-permute-done((f32[16,4,8,128]{3,2,1,0:T(8,128)S(1)}, f32[16,4,8,128]{3,2,1,0:T(8,128)S(1)}, u32[]{:S(2)}, u32[]{:S(2)}) %collective-permute-start.6) | collective-permute-done | bytes 262176 | tf_op jit(solution)/shard_map/ppermute | solution.py:167
  46.8 7.4 %all-to-all-start.1 = ((f32[16,4,8,128]{3,2,1,0:T(8,128)}), f32[16,4,8,128]{3,2,1,0:T(8,128)S(1)}, u32[]{:S(2)}, u32[]{:S(2)}) async-start(f32[16,4,8,128]{3,2,1,0:T(8,128)} %bitcast_add_fusion), calls=%async_computation.1 | async-start | bytes 524288 | tf_op jit(solution)/shard_map/all_to_all | solution.py:194
  54.2 3.4 %collective-permute-start.4 = (f32[2,256,512]{2,1,0:T(8,128)S(1)}, f32[2,256,512]{2,1,0:T(8,128)S(1)}, u32[]{:S(2)}, u32[]{:S(2)}) collective-permute-start(f32[2,256,512]{2,1,0:T(8,128)S(1)} %copy-done.2), channel_id=1, source_target_pairs={{0,2},{1,3},{2,0},{3,1},{4,6},{5,7},{6,4},{7,5},{8,10},{9,11},{10,... | collective-permute-start | bytes 3145736 | tf_op jit(solution)/shard_map/ppermute | solution.py:167
  57.6 2.1 collective-permute-start
  59.7 3.7 %collective-permute-start.1 = (f32[4,256,256]{2,1,0:T(8,128)S(1)}, f32[4,256,256]{2,1,0:T(8,128)}, u32[]{:S(2)}, u32[]{:S(2)}) collective-permute-start(f32[4,256,256]{2,1,0:T(8,128)S(1)} %copy-done.1), channel_id=1, source_target_pairs={{0,384},{1,385},{2,386},{3,387},{4,388},{5,389},{6,390},{7,391},{8... | collective-permute-start | bytes 3145736 | tf_op jit(solution)/shard_map/ppermute | solution.py:167
  63.4 3.1 %collective-permute-start.2 = (f32[4,256,256]{2,1,0:T(8,128)S(1)}, f32[4,256,256]{2,1,0:T(8,128)}, u32[]{:S(2)}, u32[]{:S(2)}) collective-permute-start(f32[4,256,256]{2,1,0:T(8,128)S(1)} %copy-done.1), channel_id=1, source_target_pairs={{0,256},{1,257},{2,258},{3,259},{4,260},{5,261},{6,262},{7,263},{8... | collective-permute-start | bytes 3145736 | tf_op jit(solution)/shard_map/ppermute | solution.py:167
  66.6 5.3 %all-to-all-done.1 = f32[16,4,8,128]{3,2,1,0:T(8,128)S(1)} async-done(((f32[16,4,8,128]{3,2,1,0:T(8,128)}), f32[16,4,8,128]{3,2,1,0:T(8,128)S(1)}, u32[]{:S(2)}, u32[]{:S(2)}) %all-to-all-start.1) | async-done | bytes 262176 | tf_op jit(solution)/shard_map/all_to_all | solution.py:194
  71.9 3.4 %collective-permute-start.7 = (f32[4,128,128]{2,1,0:T(8,128)S(1)}, f32[4,128,128]{2,1,0:T(8,128)S(1)}, u32[]{:S(2)}, u32[]{:S(2)}) collective-permute-start(f32[4,128,128]{2,1,0:T(8,128)S(1)} %copy_bitcast_fusion), channel_id=1, source_target_pairs={{0,2},{1,3},{2,0},{3,1},{4,6},{5,7},{6,4},{7,5},{8,10},{9,11},{10,... | collective-permute-start | bytes 786440 | tf_op jit(solution)/shard_map/ppermute | solution.py:167
  75.3 6.8 %collective-permute-done.4.refs_6_ = f32[2,256,512]{2,1,0:T(8,128)S(1)} collective-permute-done((f32[2,256,512]{2,1,0:T(8,128)S(1)}, f32[2,256,512]{2,1,0:T(8,128)S(1)}, u32[]{:S(2)}, u32[]{:S(2)}) %collective-permute-start.4) | collective-permute-done | bytes 1048608 | tf_op jit(solution)/shard_map/ppermute | solution.py:167
  82.1 1.9 collective-permute-start.3
  86.1 1.9 collective-permute-start.5
  89.1 2.1 collective-permute-start.8
  91.2 15.1 %collective-permute-done.1.refs_2_ = f32[4,256,256]{2,1,0:T(8,128)} collective-permute-done((f32[4,256,256]{2,1,0:T(8,128)S(1)}, f32[4,256,256]{2,1,0:T(8,128)}, u32[]{:S(2)}, u32[]{:S(2)}) %collective-permute-start.1) | collective-permute-done | bytes 1048608 | tf_op jit(solution)/shard_map/ppermute | solution.py:167
  106.3 1.9 collective-permute-start.9
  108.2 3.1 %collective-permute-done.2.refs_3_ = f32[4,256,256]{2,1,0:T(8,128)} collective-permute-done((f32[4,256,256]{2,1,0:T(8,128)S(1)}, f32[4,256,256]{2,1,0:T(8,128)}, u32[]{:S(2)}, u32[]{:S(2)}) %collective-permute-start.2) | collective-permute-done | bytes 1048608 | tf_op jit(solution)/shard_map/ppermute | solution.py:167
  111.3 4.2 %collective-permute-start.10 = (f32[2,4,128,128]{3,2,1,0:T(8,128)S(1)}, f32[2,4,128,128]{3,2,1,0:T(8,128)S(1)}, u32[]{:S(2)}, u32[]{:S(2)}) collective-permute-start(f32[2,4,128,128]{3,2,1,0:T(8,128)S(1)} %pad_maximum_fusion.refs_2_), channel_id=1, source_target_pairs={{0,256},{1,257},{2,258},{3,259},{4,260},{5,261},{6,262},{7,263},{8... | collective-permute-start | bytes 1572872 | tf_op jit(solution)/shard_map/ppermute | solution.py:167
  115.5 1.9 collective-permute-start.11
  117.4 1.8 collective-permute-done.8.refs_3_
  119.3 1.9 collective-permute-start.12
  121.2 9.8 %collective-permute-done.9.refs_4_ = f32[2,4,128,128]{3,2,1,0:T(8,128)S(1)} collective-permute-done((f32[2,4,128,128]{3,2,1,0:T(8,128)S(1)}, f32[2,4,128,128]{3,2,1,0:T(8,128)S(1)}, u32[]{:S(2)}, u32[]{:S(2)}) %collective-permute-start.9) | collective-permute-done | bytes 524320 | tf_op jit(solution)/shard_map/ppermute | solution.py:167
  131.0 1.9 collective-permute-start.13
  132.9 2.4 collective-permute-start.14
  135.3 11.9 %mix.1 = (bf16[2,4,256,512]{3,2,1,0:T(8,128)(2,1)S(1)}, bf16[2,4,256,512]{3,2,1,0:T(8,128)(2,1)S(1)}) custom-call(f32[4,256,256]{2,1,0:T(8,128)S(1)} %copy-done.1, f32[4,256,256]{2,1,0:T(8,128)} %collective-permute-done.refs_1_, f32[4,256,256]{2,1,0:T(8,128)} %collective-permute-done.1.refs_2_, f32[4,256,256]{2,1,0:T(8,128)} %collective-permute-done.2.refs_3_, ...), custom_call_target="tpu_custom_call" | custom-call | flops 6442450944 | bytes 16777216 | tf_op jit(solution)/shard_map/mix/pallas_call | solution.py:66
  147.3 6.0 %respond.1 = f32[2,256,512]{2,1,0:T(8,128)S(1)} custom-call(bf16[2,4,256,512]{3,2,1,0:T(8,128)(2,1)S(1)} %get-tuple-element.7.refs_0_, bf16[2,4,256,512]{3,2,1,0:T(8,128)(2,1)S(1)} %get-tuple-element.8.refs_1_, f32[2,4,128,128]{3,2,1,0:T(8,128)S(1)} %pad_maximum_fusion.refs_2_, f32[2,4,128,128]{3,2,1,0:T(8,128)S(1)} %collective-permute-done.8.refs_3_, ...), custom_call_target="tpu_custom_call" | custom-call | flops 3221225472 | bytes 16777216 | tf_op jit(solution)/shard_map/respond/pallas_call | solution.py:119
  153.3 20.7 %all_to_all.25 = f32[4,128,512]{2,1,0:T(8,128)S(1)} all-to-all(f32[4,128,512]{2,1,0:T(8,128)S(1)} %bitcast.38), channel_id=1, replica_groups={{0,4,8,12},{16,20,24,28},{32,36,40,44},{48,52,56,60},{64,68,72,76},{80,..., dimensions={0} | all-to-all | bytes 2097152 | tf_op jit(solution)/shard_map/all_to_all | solution.py:207
  174.1 30.7 %all_to_all.26 = f32[8,16,512]{2,1,0:T(8,128)S(1)} all-to-all(f32[8,16,512]{2,1,0:T(8,128)S(1)} %bitcast.40), channel_id=1, replica_groups={{0,16,32,48,64,80,96,112},{4,20,36,52,68,84,100,116},{8,24,40,56,72,88,..., dimensions={0} | all-to-all | bytes 524288 | tf_op jit(solution)/shard_map/all_to_all | solution.py:207
  204.8 28.6 %all_gather.3 = f32[128,512]{1,0:T(8,128)S(1)} all-gather(f32[16,512]{1,0:T(8,128)S(1)} %reduce_sum.19), channel_id=1, replica_groups={{0,16,32,48,64,80,96,112},{4,20,36,52,68,84,100,116},{8,24,40,56,72,88,..., dimensions={0}, use_global_device_ids=true | all-gather | bytes 294912 | tf_op jit(solution)/shard_map/all_gather | solution.py:210
  233.5 13.9 %all_to_all.27 = f32[4,128,512]{2,1,0:T(8,128)S(1)} all-to-all(f32[4,128,512]{2,1,0:T(8,128)S(1)} %broadcast_in_dim.3), channel_id=1, replica_groups={{0,4,8,12},{16,20,24,28},{32,36,40,44},{48,52,56,60},{64,68,72,76},{80,..., dimensions={0} | all-to-all | bytes 2097152 | tf_op jit(solution)/shard_map/all_to_all | solution.py:207
  (34 shorter events, 6.2 us)
Async XLA Ops:
  0.0 17.1 %copy-start = (f32[128,128]{1,0:T(8,128)S(1)}, f32[128,128]{1,0:T(8,128)}, u32[]{:S(2)}) copy-start(f32[128,128]{1,0:T(8,128)} %param.6) | copy-start | bytes 196612
  1.9 33.6 %all-to-all-start = ((f32[16,4,8,128]{3,1,2,0:T(4,128)}), f32[16,4,8,128]{3,1,2,0:T(4,128)S(1)}, u32[]{:S(2)}, u32[]{:S(2)}) async-start(f32[16,4,8,128]{3,1,2,0:T(4,128)} %bitcast.4), calls=%async_computation | async-start | bytes 524288 | tf_op jit(solution)/shard_map/all_to_all | solution.py:183
  17.5 36.7 %copy-start.2 = (f32[2,256,512]{2,1,0:T(8,128)S(1)}, f32[2,256,512]{2,1,0:T(8,128)}, u32[]{:S(2)}) copy-start(f32[2,256,512]{2,1,0:T(8,128)} %refs_4_.1) | copy-start | bytes 3145732
  17.5 40.1 %copy-start.1 = (f32[4,256,256]{2,1,0:T(8,128)S(1)}, f32[4,256,256]{2,1,0:T(8,128)}, u32[]{:S(2)}) copy-start(f32[4,256,256]{2,1,0:T(8,128)} %refs_0_.1) | copy-start | bytes 3145732
  36.2 9.8 %collective-permute-start.6 = (f32[16,4,8,128]{3,2,1,0:T(8,128)S(1)}, f32[16,4,8,128]{3,2,1,0:T(8,128)S(1)}, u32[]{:S(2)}, u32[]{:S(2)}) collective-permute-start(f32[16,4,8,128]{3,2,1,0:T(8,128)S(1)} %bitcast.42), channel_id=1, source_target_pairs={{0,4},{1,5},{2,6},{3,7},{4,0},{5,1},{6,2},{7,3},{8,12},{9,13},{10,... | collective-permute-start | bytes 786440 | tf_op jit(solution)/shard_map/ppermute | solution.py:167
  46.8 25.1 %all-to-all-start.1 = ((f32[16,4,8,128]{3,2,1,0:T(8,128)}), f32[16,4,8,128]{3,2,1,0:T(8,128)S(1)}, u32[]{:S(2)}, u32[]{:S(2)}) async-start(f32[16,4,8,128]{3,2,1,0:T(8,128)} %bitcast_add_fusion), calls=%async_computation.1 | async-start | bytes 524288 | tf_op jit(solution)/shard_map/all_to_all | solution.py:194
  54.2 27.9 %collective-permute-start.4 = (f32[2,256,512]{2,1,0:T(8,128)S(1)}, f32[2,256,512]{2,1,0:T(8,128)S(1)}, u32[]{:S(2)}, u32[]{:S(2)}) collective-permute-start(f32[2,256,512]{2,1,0:T(8,128)S(1)} %copy-done.2), channel_id=1, source_target_pairs={{0,2},{1,3},{2,0},{3,1},{4,6},{5,7},{6,4},{7,5},{8,10},{9,11},{10,... | collective-permute-start | bytes 3145736 | tf_op jit(solution)/shard_map/ppermute | solution.py:167
  57.6 31.5 %collective-permute-start = (f32[4,256,256]{2,1,0:T(8,128)S(1)}, f32[4,256,256]{2,1,0:T(8,128)}, u32[]{:S(2)}, u32[]{:S(2)}) collective-permute-start(f32[4,256,256]{2,1,0:T(8,128)S(1)} %copy-done.1), channel_id=1, source_target_pairs={{0,128},{1,129},{2,130},{3,131},{4,132},{5,133},{6,134},{7,135},{8... | collective-permute-start | bytes 3145736 | tf_op jit(solution)/shard_map/ppermute | solution.py:167
  59.7 46.5 %collective-permute-start.1 = (f32[4,256,256]{2,1,0:T(8,128)S(1)}, f32[4,256,256]{2,1,0:T(8,128)}, u32[]{:S(2)}, u32[]{:S(2)}) collective-permute-start(f32[4,256,256]{2,1,0:T(8,128)S(1)} %copy-done.1), channel_id=1, source_target_pairs={{0,384},{1,385},{2,386},{3,387},{4,388},{5,389},{6,390},{7,391},{8... | collective-permute-start | bytes 3145736 | tf_op jit(solution)/shard_map/ppermute | solution.py:167
  63.4 47.8 %collective-permute-start.2 = (f32[4,256,256]{2,1,0:T(8,128)S(1)}, f32[4,256,256]{2,1,0:T(8,128)}, u32[]{:S(2)}, u32[]{:S(2)}) collective-permute-start(f32[4,256,256]{2,1,0:T(8,128)S(1)} %copy-done.1), channel_id=1, source_target_pairs={{0,256},{1,257},{2,258},{3,259},{4,260},{5,261},{6,262},{7,263},{8... | collective-permute-start | bytes 3145736 | tf_op jit(solution)/shard_map/ppermute | solution.py:167
  71.9 13.5 %collective-permute-start.7 = (f32[4,128,128]{2,1,0:T(8,128)S(1)}, f32[4,128,128]{2,1,0:T(8,128)S(1)}, u32[]{:S(2)}, u32[]{:S(2)}) collective-permute-start(f32[4,128,128]{2,1,0:T(8,128)S(1)} %copy_bitcast_fusion), channel_id=1, source_target_pairs={{0,2},{1,3},{2,0},{3,1},{4,6},{5,7},{6,4},{7,5},{8,10},{9,11},{10,... | collective-permute-start | bytes 786440 | tf_op jit(solution)/shard_map/ppermute | solution.py:167
  82.1 33.4 %collective-permute-start.3 = (f32[2,256,512]{2,1,0:T(8,128)S(1)}, f32[2,256,512]{2,1,0:T(8,128)}, u32[]{:S(2)}, u32[]{:S(2)}) collective-permute-start(f32[2,256,512]{2,1,0:T(8,128)S(1)} %copy-done.2), channel_id=1, source_target_pairs={{0,1},{1,0},{2,3},{3,2},{4,5},{5,4},{6,7},{7,6},{8,9},{9,8},{10,11... | collective-permute-start | bytes 3145736 | tf_op jit(solution)/shard_map/ppermute | solution.py:167
  85.4 0.7 copy-start.3
  86.1 49.2 %collective-permute-start.5 = (f32[2,256,512]{2,1,0:T(8,128)S(1)}, f32[2,256,512]{2,1,0:T(8,128)}, u32[]{:S(2)}, u32[]{:S(2)}) collective-permute-start(f32[2,256,512]{2,1,0:T(8,128)S(1)} %collective-permute-done.4.refs_6_), channel_id=1, source_target_pairs={{0,1},{1,0},{2,3},{3,2},{4,5},{5,4},{6,7},{7,6},{8,9},{9,8},{10,11... | collective-permute-start | bytes 3145736 | tf_op jit(solution)/shard_map/ppermute | solution.py:167
  89.1 30.2 %collective-permute-start.8 = (f32[2,4,128,128]{3,2,1,0:T(8,128)S(1)}, f32[2,4,128,128]{3,2,1,0:T(8,128)S(1)}, u32[]{:S(2)}, u32[]{:S(2)}) collective-permute-start(f32[2,4,128,128]{3,2,1,0:T(8,128)S(1)} %pad_maximum_fusion.refs_2_), channel_id=1, source_target_pairs={{0,128},{1,129},{2,130},{3,131},{4,132},{5,133},{6,134},{7,135},{8... | collective-permute-start | bytes 1572872 | tf_op jit(solution)/shard_map/ppermute | solution.py:167
  106.3 24.7 %collective-permute-start.9 = (f32[2,4,128,128]{3,2,1,0:T(8,128)S(1)}, f32[2,4,128,128]{3,2,1,0:T(8,128)S(1)}, u32[]{:S(2)}, u32[]{:S(2)}) collective-permute-start(f32[2,4,128,128]{3,2,1,0:T(8,128)S(1)} %pad_maximum_fusion.refs_2_), channel_id=1, source_target_pairs={{0,384},{1,385},{2,386},{3,387},{4,388},{5,389},{6,390},{7,391},{8... | collective-permute-start | bytes 1572872 | tf_op jit(solution)/shard_map/ppermute | solution.py:167
  111.3 21.6 %collective-permute-start.10 = (f32[2,4,128,128]{3,2,1,0:T(8,128)S(1)}, f32[2,4,128,128]{3,2,1,0:T(8,128)S(1)}, u32[]{:S(2)}, u32[]{:S(2)}) collective-permute-start(f32[2,4,128,128]{3,2,1,0:T(8,128)S(1)} %pad_maximum_fusion.refs_2_), channel_id=1, source_target_pairs={{0,256},{1,257},{2,258},{3,259},{4,260},{5,261},{6,262},{7,263},{8... | collective-permute-start | bytes 1572872 | tf_op jit(solution)/shard_map/ppermute | solution.py:167
  115.5 31.8 %collective-permute-start.11 = (f32[2,4,128,128]{3,2,1,0:T(8,128)S(1)}, f32[2,4,128,128]{3,2,1,0:T(8,128)S(1)}, u32[]{:S(2)}, u32[]{:S(2)}) collective-permute-start(f32[2,4,128,128]{3,2,1,0:T(8,128)S(1)} %pad_maximum_fusion.refs_2_), channel_id=1, source_target_pairs={{0,1},{1,0},{2,3},{3,2},{4,5},{5,4},{6,7},{7,6},{8,9},{9,8},{10,11... | collective-permute-start | bytes 1572872 | tf_op jit(solution)/shard_map/ppermute | solution.py:167
  119.3 28.0 %collective-permute-start.12 = (f32[2,4,128,128]{3,2,1,0:T(8,128)S(1)}, f32[2,4,128,128]{3,2,1,0:T(8,128)S(1)}, u32[]{:S(2)}, u32[]{:S(2)}) collective-permute-start(f32[2,4,128,128]{3,2,1,0:T(8,128)S(1)} %collective-permute-done.8.refs_3_), channel_id=1, source_target_pairs={{0,1},{1,0},{2,3},{3,2},{4,5},{5,4},{6,7},{7,6},{8,9},{9,8},{10,11... | collective-permute-start | bytes 1572872 | tf_op jit(solution)/shard_map/ppermute | solution.py:167
  131.0 16.3 %collective-permute-start.13 = (f32[2,4,128,128]{3,2,1,0:T(8,128)S(1)}, f32[2,4,128,128]{3,2,1,0:T(8,128)S(1)}, u32[]{:S(2)}, u32[]{:S(2)}) collective-permute-start(f32[2,4,128,128]{3,2,1,0:T(8,128)S(1)} %collective-permute-done.9.refs_4_), channel_id=1, source_target_pairs={{0,1},{1,0},{2,3},{3,2},{4,5},{5,4},{6,7},{7,6},{8,9},{9,8},{10,11... | collective-permute-start | bytes 1572872 | tf_op jit(solution)/shard_map/ppermute | solution.py:167
  132.9 14.4 %collective-permute-start.14 = (f32[2,4,128,128]{3,2,1,0:T(8,128)S(1)}, f32[2,4,128,128]{3,2,1,0:T(8,128)S(1)}, u32[]{:S(2)}, u32[]{:S(2)}) collective-permute-start(f32[2,4,128,128]{3,2,1,0:T(8,128)S(1)} %collective-permute-done.10.refs_5_), channel_id=1, source_target_pairs={{0,1},{1,0},{2,3},{3,2},{4,5},{5,4},{6,7},{7,6},{8,9},{9,8},{10,11... | collective-permute-start | bytes 1572872 | tf_op jit(solution)/shard_map/ppermute | solution.py:167

commit v3 on v2

--- a/solution.py
+++ b/solution.py
@@ -155,7 +155,7 @@
 
 def solution(mesh):
     to_core = moves(mesh, lambda y, z, x, c: (y, z, x, 1 - c))
-    to_x = moves(mesh, lambda y, z, x, c: (y, z, x + 2, c))
+    to_x = {d: moves(mesh, lambda y, z, x, c, d=d: (y, z, x + d, c)) for d in (1, -1, 2)}
     to_pair = moves(mesh, lambda y, z, x, c: (y, z, x ^ 1, c))
     to_y = {d: moves(mesh, lambda y, z, x, c, d=d: (y + d, z, x, c)) for d in (1, -1, 2)}
     n_z = mesh.shape["aux"] // 2
@@ -174,7 +174,7 @@
         slabs = [cond_pairs]
         for d in SHIFTS[1:]:
             slabs.append(send(cond_pairs, to_y[d]))
-        far = send(trials, to_pair)
+        far = jnp.stack([send(trials[0], to_x[1]), send(trials[1], to_x[-1])])
         pieces = [trials, send(trials, to_core), far]
         pieces.append(send(far, to_core))
 
@@ -189,7 +189,7 @@
         spread = spread.reshape(n_q // 2, v1 // n_z, v2)
         product = jnp.einsum("pq,qrv->prv", columns, spread, precision=highest)
         product = product.reshape(n_z, 2, n_p, v1 // n_z, v2)
-        swapped = send(lax.dynamic_index_in_dim(product, 1 - half, 1, keepdims=False), to_x)
+        swapped = send(lax.dynamic_index_in_dim(product, 1 - half, 1, keepdims=False), to_x[2])
         block = lax.dynamic_index_in_dim(product, half, 1, keepdims=False) + swapped
         block = lax.all_to_all(block, "aux", 0, 0, axis_index_groups=along_z)
         block = block.transpose(1, 0, 2, 3).reshape(n_p, v1, v2)
@@ -207,8 +207,9 @@
         swap = lambda value, groups: lax.all_to_all(value, "aux", 0, 0, axis_index_groups=groups)
         parts = jnp.sum(swap(partial.reshape(4, -1, partial.shape[2]), fours), axis=0)
         parts = jnp.sum(swap(parts.reshape(n_z // 2, -1, parts.shape[1]), along_fours), axis=0)
-        total = lax.all_gather(parts, "aux", axis=0, tiled=True, axis_index_groups=along_fours)
-        total = swap(jnp.broadcast_to(total, (4, *total.shape)), fours)
+        copies = lambda value, count: jnp.broadcast_to(value, (count, *value.shape))
+        total = swap(copies(parts, n_z // 2), along_fours).reshape(-1, parts.shape[1])
+        total = swap(copies(total, 4), fours)
         return total.reshape(partial.shape)
 
     in_specs = (P("aux", "cond", "state"), P("aux", "state", "cond"), P(), P("state", "cond", None))

time: 249 us -> 250 us (level); the launches traced: 248 us -> 247 us
  blocking collectives: 93.9 us -> 87.7 us
  starting transfers between devices: 63.5 us -> 66.9 us
    all_gather x1 -> x0, blocking collectives: 28.6 us -> none  [per_device(): lax.all_gather(parts, 'aux', axis=0, tiled=True, axis_index_groups=along_...]
    all_to_all x3 -> x4, blocking collectives: 65.3 us -> 87.7 us  [per_device(): lax.all_to_all(value, 'aux', 0, 0, axis_index_groups=groups)]
    all_to_all x1, waiting for transfers between devices: 5.3 us -> 1.07 us  [per_device(): block = lax.all_to_all(block, 'aux', 0, 0, axis_index_groups=along_z)]
    ppermute x15 -> x16, starting transfers between devices: 40.9 us -> 44.3 us  [send(): return lax.ppermute(value, AXES, pairs)]
    ppermute x15 -> x16, waiting for transfers between devices: 42.8 us -> 45.6 us  [send(): return lax.ppermute(value, AXES, pairs)]
  transfers between devices with their start and end apart: 17 -> 18, of which waited for: 9 -> 9; matrix products, arithmetic and copies ran while one was open for 1% -> 1% of each run, Pallas kernels for 5% -> 5%
where the time goes in v3:
time: 250 us; the launch traced here: 247 us
  blocking collectives  87.7 us (35%)
  starting transfers between devices  66.9 us (27%)
  waiting for transfers between devices  64.6 us (26%)
  Pallas kernels  17.9 us (7%)
  local copies, waits for them, and re-layouts  5.01 us (2%)
  other arithmetic  3.2 us (1%)
    all_to_all x4, blocking collectives, per_device(): lax.all_to_all(value, 'aux', 0, 0, axis_index_groups=groups)  87.7 us
    ppermute x16, waiting for transfers between devices, send(): return lax.ppermute(value, AXES, pairs)  45.6 us
    ppermute x16, starting transfers between devices, send(): return lax.ppermute(value, AXES, pairs)  44.3 us
    all_to_all x1, waiting for transfers between devices, per_device(): spread = lax.all_to_all(spread, 'aux', 0, 0, axis_index_groups=along_z)  18 us
    all_to_all x1, starting transfers between devices, per_device(): spread = lax.all_to_all(spread, 'aux', 0, 0, axis_index_groups=along_z)  15.2 us
    pallas_call x1, Pallas kernels, mix(): pl.pallas_call(mix_kernel, name='mix', out_shape=(shape, shape), in_specs...  11.9 us
    all_to_all x1, starting transfers between devices, per_device(): block = lax.all_to_all(block, 'aux', 0, 0, axis_index_groups=along_z)  7.39 us
    pallas_call x1, Pallas kernels, respond(): pl.pallas_call(respond_kernel, name='respond', out_shape=jax.ShapeDtypeSt...  5.96 us
  transfers between devices with their start and end apart: 18, of which 9 were waited for; matrix products, arithmetic and copies ran while one was open for 1% of the time, Pallas kernels for 5%

profile of v3, /device:TPU:24, one launch (start us, length us, event | category | flops | bytes accessed | tf_op | source)
XLA Modules:
  0.0 246.6 jit_solution(5953175474131483825)
XLA Ops:
  0.0 1.9 copy.21
  1.9 15.2 %all-to-all-start = ((f32[16,4,8,128]{3,1,2,0:T(4,128)}), f32[16,4,8,128]{3,1,2,0:T(4,128)S(1)}, u32[]{:S(2)}, u32[]{:S(2)}) async-start(f32[16,4,8,128]{3,1,2,0:T(4,128)} %bitcast.8), calls=%async_computation | async-start | bytes 524288 | tf_op jit(solution)/shard_map/all_to_all | solution.py:183
  17.5 18.0 %all-to-all-done = f32[16,4,8,128]{3,1,2,0:T(4,128)S(1)} async-done(((f32[16,4,8,128]{3,1,2,0:T(4,128)}), f32[16,4,8,128]{3,1,2,0:T(4,128)S(1)}, u32[]{:S(2)}, u32[]{:S(2)}) %all-to-all-start) | async-done | bytes 262176 | tf_op jit(solution)/shard_map/all_to_all | solution.py:183
  36.2 5.1 %collective-permute-start.7 = (f32[16,4,8,128]{3,2,1,0:T(8,128)S(1)}, f32[16,4,8,128]{3,2,1,0:T(8,128)S(1)}, u32[]{:S(2)}, u32[]{:S(2)}) collective-permute-start(f32[16,4,8,128]{3,2,1,0:T(8,128)S(1)} %bitcast.52), channel_id=1, source_target_pairs={{0,4},{1,5},{2,6},{3,7},{4,0},{5,1},{6,2},{7,3},{8,12},{9,13},{10,... | collective-permute-start | bytes 786440 | tf_op jit(solution)/shard_map/ppermute | solution.py:167
  41.3 4.8 %collective-permute-done.7 = f32[16,4,8,128]{3,2,1,0:T(8,128)S(1)} collective-permute-done((f32[16,4,8,128]{3,2,1,0:T(8,128)S(1)}, f32[16,4,8,128]{3,2,1,0:T(8,128)S(1)}, u32[]{:S(2)}, u32[]{:S(2)}) %collective-permute-start.7) | collective-permute-done | bytes 262176 | tf_op jit(solution)/shard_map/ppermute | solution.py:167
  46.9 7.4 %all-to-all-start.1 = ((f32[16,4,8,128]{3,2,1,0:T(8,128)}), f32[16,4,8,128]{3,2,1,0:T(8,128)S(1)}, u32[]{:S(2)}, u32[]{:S(2)}) async-start(f32[16,4,8,128]{3,2,1,0:T(8,128)} %bitcast_add_fusion), calls=%async_computation.1 | async-start | bytes 524288 | tf_op jit(solution)/shard_map/all_to_all | solution.py:194
  55.3 4.7 %collective-permute-start.5 = (f32[256,512]{1,0:T(8,128)}, f32[256,512]{1,0:T(8,128)S(1)}, u32[]{:S(2)}, u32[]{:S(2)}) collective-permute-start(f32[256,512]{1,0:T(8,128)} %get-tuple-element.10), channel_id=1, source_target_pairs={{0,6},{1,7},{2,0},{3,1},{4,2},{5,3},{6,4},{7,5},{8,14},{9,15},{10,... | collective-permute-start | bytes 1572872 | tf_op jit(solution)/shard_map/ppermute | solution.py:167
  60.0 1.9 collective-permute-start.4
  61.9 2.1 collective-permute-start
  64.1 3.7 %collective-permute-start.1 = (f32[4,256,256]{2,1,0:T(8,128)S(1)}, f32[4,256,256]{2,1,0:T(8,128)}, u32[]{:S(2)}, u32[]{:S(2)}) collective-permute-start(f32[4,256,256]{2,1,0:T(8,128)S(1)} %copy-done.2), channel_id=1, source_target_pairs={{0,384},{1,385},{2,386},{3,387},{4,388},{5,389},{6,390},{7,391},{8... | collective-permute-start | bytes 3145736 | tf_op jit(solution)/shard_map/ppermute | solution.py:167
  67.8 3.1 %collective-permute-start.2 = (f32[4,256,256]{2,1,0:T(8,128)S(1)}, f32[4,256,256]{2,1,0:T(8,128)}, u32[]{:S(2)}, u32[]{:S(2)}) collective-permute-start(f32[4,256,256]{2,1,0:T(8,128)S(1)} %copy-done.2), channel_id=1, source_target_pairs={{0,256},{1,257},{2,258},{3,259},{4,260},{5,261},{6,262},{7,263},{8... | collective-permute-start | bytes 3145736 | tf_op jit(solution)/shard_map/ppermute | solution.py:167
  72.1 3.4 %collective-permute-start.8 = (f32[4,128,128]{2,1,0:T(8,128)S(1)}, f32[4,128,128]{2,1,0:T(8,128)S(1)}, u32[]{:S(2)}, u32[]{:S(2)}) collective-permute-start(f32[4,128,128]{2,1,0:T(8,128)S(1)} %copy_bitcast_fusion), channel_id=1, source_target_pairs={{0,2},{1,3},{2,0},{3,1},{4,6},{5,7},{6,4},{7,5},{8,10},{9,11},{10,... | collective-permute-start | bytes 786440 | tf_op jit(solution)/shard_map/ppermute | solution.py:167
  75.5 1.9 collective-permute-start.3
  81.0 1.9 collective-permute-start.6
  84.0 6.0 %collective-permute-done.refs_1_ = f32[4,256,256]{2,1,0:T(8,128)} collective-permute-done((f32[4,256,256]{2,1,0:T(8,128)S(1)}, f32[4,256,256]{2,1,0:T(8,128)}, u32[]{:S(2)}, u32[]{:S(2)}) %collective-permute-start) | collective-permute-done | bytes 1048608 | tf_op jit(solution)/shard_map/ppermute | solution.py:167
  90.0 2.2 collective-permute-start.9
  92.2 18.4 %collective-permute-done.1.refs_2_ = f32[4,256,256]{2,1,0:T(8,128)} collective-permute-done((f32[4,256,256]{2,1,0:T(8,128)S(1)}, f32[4,256,256]{2,1,0:T(8,128)}, u32[]{:S(2)}, u32[]{:S(2)}) %collective-permute-start.1) | collective-permute-done | bytes 1048608 | tf_op jit(solution)/shard_map/ppermute | solution.py:167
  110.6 1.9 collective-permute-start.10
  112.5 3.1 %collective-permute-done.2.refs_3_ = f32[4,256,256]{2,1,0:T(8,128)} collective-permute-done((f32[4,256,256]{2,1,0:T(8,128)S(1)}, f32[4,256,256]{2,1,0:T(8,128)}, u32[]{:S(2)}, u32[]{:S(2)}) %collective-permute-start.2) | collective-permute-done | bytes 1048608 | tf_op jit(solution)/shard_map/ppermute | solution.py:167
  115.6 4.2 %collective-permute-start.11 = (f32[2,4,128,128]{3,2,1,0:T(8,128)S(1)}, f32[2,4,128,128]{3,2,1,0:T(8,128)S(1)}, u32[]{:S(2)}, u32[]{:S(2)}) collective-permute-start(f32[2,4,128,128]{3,2,1,0:T(8,128)S(1)} %pad_maximum_fusion.1.refs_2_), channel_id=1, source_target_pairs={{0,256},{1,257},{2,258},{3,259},{4,260},{5,261},{6,262},{7,263},{8... | collective-permute-start | bytes 1572872 | tf_op jit(solution)/shard_map/ppermute | solution.py:167
  119.9 1.9 collective-permute-start.12
  121.8 1.8 collective-permute-done.9.refs_3_
  123.6 1.9 collective-permute-start.13
  125.5 9.8 %collective-permute-done.10.refs_4_ = f32[2,4,128,128]{3,2,1,0:T(8,128)S(1)} collective-permute-done((f32[2,4,128,128]{3,2,1,0:T(8,128)S(1)}, f32[2,4,128,128]{3,2,1,0:T(8,128)S(1)}, u32[]{:S(2)}, u32[]{:S(2)}) %collective-permute-start.10) | collective-permute-done | bytes 524320 | tf_op jit(solution)/shard_map/ppermute | solution.py:167
  135.3 1.9 collective-permute-start.14
  137.3 2.4 collective-permute-start.15
  139.7 11.9 %mix.1 = (bf16[2,4,256,512]{3,2,1,0:T(8,128)(2,1)S(1)}, bf16[2,4,256,512]{3,2,1,0:T(8,128)(2,1)S(1)}) custom-call(f32[4,256,256]{2,1,0:T(8,128)S(1)} %copy-done.2, f32[4,256,256]{2,1,0:T(8,128)} %collective-permute-done.refs_1_, f32[4,256,256]{2,1,0:T(8,128)} %collective-permute-done.1.refs_2_, f32[4,256,256]{2,1,0:T(8,128)} %collective-permute-done.2.refs_3_, ...), custom_call_target="tpu_custom_call" | custom-call | flops 6442450944 | bytes 16777216 | tf_op jit(solution)/shard_map/mix/pallas_call | solution.py:66
  151.7 6.0 %respond.1 = f32[2,256,512]{2,1,0:T(8,128)S(1)} custom-call(bf16[2,4,256,512]{3,2,1,0:T(8,128)(2,1)S(1)} %get-tuple-element.7.refs_0_, bf16[2,4,256,512]{3,2,1,0:T(8,128)(2,1)S(1)} %get-tuple-element.8.refs_1_, f32[2,4,128,128]{3,2,1,0:T(8,128)S(1)} %pad_maximum_fusion.1.refs_2_, f32[2,4,128,128]{3,2,1,0:T(8,128)S(1)} %collective-permute-done.9.refs_3_, ...), custom_call_target="tpu_custom_call" | custom-call | flops 3221225472 | bytes 16777216 | tf_op jit(solution)/shard_map/respond/pallas_call | solution.py:119
  157.6 20.0 %all_to_all.30 = f32[4,128,512]{2,1,0:T(8,128)S(1)} all-to-all(f32[4,128,512]{2,1,0:T(8,128)S(1)} %bitcast.45), channel_id=1, replica_groups={{0,4,8,12},{16,20,24,28},{32,36,40,44},{48,52,56,60},{64,68,72,76},{80,..., dimensions={0} | all-to-all | bytes 2097152 | tf_op jit(solution)/shard_map/all_to_all | solution.py:207
  177.7 30.7 %all_to_all.31 = f32[8,16,512]{2,1,0:T(8,128)S(1)} all-to-all(f32[8,16,512]{2,1,0:T(8,128)S(1)} %bitcast.47), channel_id=1, replica_groups={{0,16,32,48,64,80,96,112},{4,20,36,52,68,84,100,116},{8,24,40,56,72,88,..., dimensions={0} | all-to-all | bytes 524288 | tf_op jit(solution)/shard_map/all_to_all | solution.py:207
  208.4 22.7 %all_to_all.32 = f32[8,16,512]{2,1,0:T(8,128)S(1)} all-to-all(f32[8,16,512]{2,1,0:T(8,128)S(1)} %broadcast_in_dim.6), channel_id=1, replica_groups={{0,16,32,48,64,80,96,112},{4,20,36,52,68,84,100,116},{8,24,40,56,72,88,..., dimensions={0} | all-to-all | bytes 524288 | tf_op jit(solution)/shard_map/all_to_all | solution.py:207
  231.3 14.3 %all_to_all.33 = f32[4,128,512]{2,1,0:T(8,128)S(1)} all-to-all(f32[4,128,512]{2,1,0:T(8,128)S(1)} %broadcast_in_dim.7), channel_id=1, replica_groups={{0,4,8,12},{16,20,24,28},{32,36,40,44},{48,52,56,60},{64,68,72,76},{80,..., dimensions={0} | all-to-all | bytes 2097152 | tf_op jit(solution)/shard_map/all_to_all | solution.py:207
  (43 shorter events, 9.9 us)
Async XLA Ops:
  0.0 17.1 %copy-start = (f32[128,128]{1,0:T(8,128)S(1)}, f32[128,128]{1,0:T(8,128)}, u32[]{:S(2)}) copy-start(f32[128,128]{1,0:T(8,128)} %param.6) | copy-start | bytes 196612
  1.9 33.6 %all-to-all-start = ((f32[16,4,8,128]{3,1,2,0:T(4,128)}), f32[16,4,8,128]{3,1,2,0:T(4,128)S(1)}, u32[]{:S(2)}, u32[]{:S(2)}) async-start(f32[16,4,8,128]{3,1,2,0:T(4,128)} %bitcast.8), calls=%async_computation | async-start | bytes 524288 | tf_op jit(solution)/shard_map/all_to_all | solution.py:183
  17.5 36.8 %copy-start.1 = (f32[2,256,512]{2,1,0:T(8,128)S(1)}, f32[2,256,512]{2,1,0:T(8,128)}, u32[]{:S(2)}) copy-start(f32[2,256,512]{2,1,0:T(8,128)} %refs_4_.1) | copy-start | bytes 3145732
  36.1 25.8 %copy-start.2 = (f32[4,256,256]{2,1,0:T(8,128)S(1)}, f32[4,256,256]{2,1,0:T(8,128)}, u32[]{:S(2)}) copy-start(f32[4,256,256]{2,1,0:T(8,128)} %refs_0_.1) | copy-start | bytes 3145732
  36.2 9.9 %collective-permute-start.7 = (f32[16,4,8,128]{3,2,1,0:T(8,128)S(1)}, f32[16,4,8,128]{3,2,1,0:T(8,128)S(1)}, u32[]{:S(2)}, u32[]{:S(2)}) collective-permute-start(f32[16,4,8,128]{3,2,1,0:T(8,128)S(1)} %bitcast.52), channel_id=1, source_target_pairs={{0,4},{1,5},{2,6},{3,7},{4,0},{5,1},{6,2},{7,3},{8,12},{9,13},{10,... | collective-permute-start | bytes 786440 | tf_op jit(solution)/shard_map/ppermute | solution.py:167
  46.9 25.1 %all-to-all-start.1 = ((f32[16,4,8,128]{3,2,1,0:T(8,128)}), f32[16,4,8,128]{3,2,1,0:T(8,128)S(1)}, u32[]{:S(2)}, u32[]{:S(2)}) async-start(f32[16,4,8,128]{3,2,1,0:T(8,128)} %bitcast_add_fusion), calls=%async_computation.1 | async-start | bytes 524288 | tf_op jit(solution)/shard_map/all_to_all | solution.py:194
  55.3 16.7 %collective-permute-start.5 = (f32[256,512]{1,0:T(8,128)}, f32[256,512]{1,0:T(8,128)S(1)}, u32[]{:S(2)}, u32[]{:S(2)}) collective-permute-start(f32[256,512]{1,0:T(8,128)} %get-tuple-element.10), channel_id=1, source_target_pairs={{0,6},{1,7},{2,0},{3,1},{4,2},{5,3},{6,4},{7,5},{8,14},{9,15},{10,... | collective-permute-start | bytes 1572872 | tf_op jit(solution)/shard_map/ppermute | solution.py:167
  60.0 15.5 %collective-permute-start.4 = (f32[256,512]{1,0:T(8,128)}, f32[256,512]{1,0:T(8,128)S(1)}, u32[]{:S(2)}, u32[]{:S(2)}) collective-permute-start(f32[256,512]{1,0:T(8,128)} %get-tuple-element.9), channel_id=1, source_target_pairs={{0,2},{1,3},{2,4},{3,5},{4,6},{5,7},{6,0},{7,1},{8,10},{9,11},{10,... | collective-permute-start | bytes 1572872 | tf_op jit(solution)/shard_map/ppermute | solution.py:167
  61.9 28.0 %collective-permute-start = (f32[4,256,256]{2,1,0:T(8,128)S(1)}, f32[4,256,256]{2,1,0:T(8,128)}, u32[]{:S(2)}, u32[]{:S(2)}) collective-permute-start(f32[4,256,256]{2,1,0:T(8,128)S(1)} %copy-done.2), channel_id=1, source_target_pairs={{0,128},{1,129},{2,130},{3,131},{4,132},{5,133},{6,134},{7,135},{8... | collective-permute-start | bytes 3145736 | tf_op jit(solution)/shard_map/ppermute | solution.py:167
  64.1 46.6 %collective-permute-start.1 = (f32[4,256,256]{2,1,0:T(8,128)S(1)}, f32[4,256,256]{2,1,0:T(8,128)}, u32[]{:S(2)}, u32[]{:S(2)}) collective-permute-start(f32[4,256,256]{2,1,0:T(8,128)S(1)} %copy-done.2), channel_id=1, source_target_pairs={{0,384},{1,385},{2,386},{3,387},{4,388},{5,389},{6,390},{7,391},{8... | collective-permute-start | bytes 3145736 | tf_op jit(solution)/shard_map/ppermute | solution.py:167
  67.8 47.8 %collective-permute-start.2 = (f32[4,256,256]{2,1,0:T(8,128)S(1)}, f32[4,256,256]{2,1,0:T(8,128)}, u32[]{:S(2)}, u32[]{:S(2)}) collective-permute-start(f32[4,256,256]{2,1,0:T(8,128)S(1)} %copy-done.2), channel_id=1, source_target_pairs={{0,256},{1,257},{2,258},{3,259},{4,260},{5,261},{6,262},{7,263},{8... | collective-permute-start | bytes 3145736 | tf_op jit(solution)/shard_map/ppermute | solution.py:167
  72.1 5.4 %copy-start.3 = (f32[256,512]{1,0:T(8,128)}, f32[256,512]{1,0:T(8,128)S(1)}, u32[]{:S(2)}) copy-start(f32[256,512]{1,0:T(8,128)S(1)} %collective-permute-done.5) | copy-start | bytes 1572868
  72.1 8.3 %collective-permute-start.8 = (f32[4,128,128]{2,1,0:T(8,128)S(1)}, f32[4,128,128]{2,1,0:T(8,128)S(1)}, u32[]{:S(2)}, u32[]{:S(2)}) collective-permute-start(f32[4,128,128]{2,1,0:T(8,128)S(1)} %copy_bitcast_fusion), channel_id=1, source_target_pairs={{0,2},{1,3},{2,0},{3,1},{4,6},{5,7},{6,4},{7,5},{8,10},{9,11},{10,... | collective-permute-start | bytes 786440 | tf_op jit(solution)/shard_map/ppermute | solution.py:167
  75.5 1.9 copy-start.4
  75.5 44.3 %collective-permute-start.3 = (f32[2,256,512]{2,1,0:T(8,128)S(1)}, f32[2,256,512]{2,1,0:T(8,128)}, u32[]{:S(2)}, u32[]{:S(2)}) collective-permute-start(f32[2,256,512]{2,1,0:T(8,128)S(1)} %copy-done.1), channel_id=1, source_target_pairs={{0,1},{1,0},{2,3},{3,2},{4,5},{5,4},{6,7},{7,6},{8,9},{9,8},{10,11... | collective-permute-start | bytes 3145736 | tf_op jit(solution)/shard_map/ppermute | solution.py:167
  80.3 0.7 copy-start.5
  81.0 58.6 %collective-permute-start.6 = (f32[2,256,512]{2,1,0:T(8,128)S(1)}, f32[2,256,512]{2,1,0:T(8,128)}, u32[]{:S(2)}, u32[]{:S(2)}) collective-permute-start(f32[2,256,512]{2,1,0:T(8,128)S(1)} %pad_maximum_fusion.refs_6_), channel_id=1, source_target_pairs={{0,1},{1,0},{2,3},{3,2},{4,5},{5,4},{6,7},{7,6},{8,9},{9,8},{10,11... | collective-permute-start | bytes 3145736 | tf_op jit(solution)/shard_map/ppermute | solution.py:167
  90.0 33.6 %collective-permute-start.9 = (f32[2,4,128,128]{3,2,1,0:T(8,128)S(1)}, f32[2,4,128,128]{3,2,1,0:T(8,128)S(1)}, u32[]{:S(2)}, u32[]{:S(2)}) collective-permute-start(f32[2,4,128,128]{3,2,1,0:T(8,128)S(1)} %pad_maximum_fusion.1.refs_2_), channel_id=1, source_target_pairs={{0,128},{1,129},{2,130},{3,131},{4,132},{5,133},{6,134},{7,135},{8... | collective-permute-start | bytes 1572872 | tf_op jit(solution)/shard_map/ppermute | solution.py:167
  110.6 24.7 %collective-permute-start.10 = (f32[2,4,128,128]{3,2,1,0:T(8,128)S(1)}, f32[2,4,128,128]{3,2,1,0:T(8,128)S(1)}, u32[]{:S(2)}, u32[]{:S(2)}) collective-permute-start(f32[2,4,128,128]{3,2,1,0:T(8,128)S(1)} %pad_maximum_fusion.1.refs_2_), channel_id=1, source_target_pairs={{0,384},{1,385},{2,386},{3,387},{4,388},{5,389},{6,390},{7,391},{8... | collective-permute-start | bytes 1572872 | tf_op jit(solution)/shard_map/ppermute | solution.py:167
  115.6 21.6 %collective-permute-start.11 = (f32[2,4,128,128]{3,2,1,0:T(8,128)S(1)}, f32[2,4,128,128]{3,2,1,0:T(8,128)S(1)}, u32[]{:S(2)}, u32[]{:S(2)}) collective-permute-start(f32[2,4,128,128]{3,2,1,0:T(8,128)S(1)} %pad_maximum_fusion.1.refs_2_), channel_id=1, source_target_pairs={{0,256},{1,257},{2,258},{3,259},{4,260},{5,261},{6,262},{7,263},{8... | collective-permute-start | bytes 1572872 | tf_op jit(solution)/shard_map/ppermute | solution.py:167
  119.9 31.8 %collective-permute-start.12 = (f32[2,4,128,128]{3,2,1,0:T(8,128)S(1)}, f32[2,4,128,128]{3,2,1,0:T(8,128)S(1)}, u32[]{:S(2)}, u32[]{:S(2)}) collective-permute-start(f32[2,4,128,128]{3,2,1,0:T(8,128)S(1)} %pad_maximum_fusion.1.refs_2_), channel_id=1, source_target_pairs={{0,1},{1,0},{2,3},{3,2},{4,5},{5,4},{6,7},{7,6},{8,9},{9,8},{10,11... | collective-permute-start | bytes 1572872 | tf_op jit(solution)/shard_map/ppermute | solution.py:167
  123.6 28.0 %collective-permute-start.13 = (f32[2,4,128,128]{3,2,1,0:T(8,128)S(1)}, f32[2,4,128,128]{3,2,1,0:T(8,128)S(1)}, u32[]{:S(2)}, u32[]{:S(2)}) collective-permute-start(f32[2,4,128,128]{3,2,1,0:T(8,128)S(1)} %collective-permute-done.9.refs_3_), channel_id=1, source_target_pairs={{0,1},{1,0},{2,3},{3,2},{4,5},{5,4},{6,7},{7,6},{8,9},{9,8},{10,11... | collective-permute-start | bytes 1572872 | tf_op jit(solution)/shard_map/ppermute | solution.py:167
  135.3 16.3 %collective-permute-start.14 = (f32[2,4,128,128]{3,2,1,0:T(8,128)S(1)}, f32[2,4,128,128]{3,2,1,0:T(8,128)S(1)}, u32[]{:S(2)}, u32[]{:S(2)}) collective-permute-start(f32[2,4,128,128]{3,2,1,0:T(8,128)S(1)} %collective-permute-done.10.refs_4_), channel_id=1, source_target_pairs={{0,1},{1,0},{2,3},{3,2},{4,5},{5,4},{6,7},{7,6},{8,9},{9,8},{10,11... | collective-permute-start | bytes 1572872 | tf_op jit(solution)/shard_map/ppermute | solution.py:167
  137.3 14.4 %collective-permute-start.15 = (f32[2,4,128,128]{3,2,1,0:T(8,128)S(1)}, f32[2,4,128,128]{3,2,1,0:T(8,128)S(1)}, u32[]{:S(2)}, u32[]{:S(2)}) collective-permute-start(f32[2,4,128,128]{3,2,1,0:T(8,128)S(1)} %collective-permute-done.11.refs_5_), channel_id=1, source_target_pairs={{0,1},{1,0},{2,3},{3,2},{4,5},{5,4},{6,7},{7,6},{8,9},{9,8},{10,11... | collective-permute-start | bytes 1572872 | tf_op jit(solution)/shard_map/ppermute | solution.py:167

commit v4 on v3

--- a/solution.py
+++ b/solution.py
@@ -24,7 +24,7 @@
 
 
 def mix_kernel(*refs):
-    slabs, pieces, (mh, ml), (b_all, x_all, bh, bl, xh, xl, sems) = refs[:4], refs[4:8], refs[8:10], refs[10:]
+    slabs, pieces, (m, mh, ml), (b_all, x_all, bh, bl, xh, xl, sems) = refs[:4], refs[4:8], refs[8:11], refs[11:]
     n_p, _, width = slabs[0].shape
     n_n = pieces[0].shape[0]
     s, k = lax.axis_index("state"), lax.axis_index("cond")
@@ -54,7 +54,9 @@
 
         @pl.loop(0, n_n)
         def _(n):
-            mh[n, p], ml[n, p] = split(dot3((bh[...], bl[...]), (xh[n], xl[n])))
+            whole = dot3((bh[...], bl[...]), (xh[n], xl[n]))
+            m[n, p] = whole
+            mh[n, p], ml[n, p] = split(whole)
 
 
 def mix(slabs, pieces):
@@ -62,13 +64,14 @@
     n_n, _, cols = pieces[0].shape
     any_spec = pl.BlockSpec(memory_space=pl.ANY)
     vmem = pl.BlockSpec(memory_space=pltpu.VMEM)
-    shape = jax.ShapeDtypeStruct((n_n, n_p, rows, cols), bf16)
+    shape = (n_n, n_p, rows, cols)
+    half = jax.ShapeDtypeStruct(shape, bf16)
     return pl.pallas_call(
         mix_kernel,
         name="mix",
-        out_shape=(shape, shape),
+        out_shape=(jax.ShapeDtypeStruct(shape, f32), half, half),
         in_specs=[any_spec] * 8,
-        out_specs=(vmem, vmem),
+        out_specs=(vmem,) * 3,
         scratch_shapes=[
             pltpu.VMEM((n_p, rows, 4 * width), f32),
             pltpu.VMEM((4, n_n, width, cols), f32),
@@ -85,18 +88,40 @@
     )(*slabs, *pieces)
 
 
+def halves_kernel(m, mh, ml):
+    @pl.loop(0, m.shape[0])
+    def _(n):
+        @pl.loop(0, m.shape[1])
+        def _(p):
+            mh[n, p], ml[n, p] = split(m[n, p])
+
+
+def halves(m):
+    half = jax.ShapeDtypeStruct(m.shape, bf16)
+    vmem = pl.BlockSpec(memory_space=pltpu.VMEM)
+    return pl.pallas_call(
+        halves_kernel,
+        name="halves",
+        out_shape=(half, half),
+        in_specs=[vmem],
+        out_specs=(vmem, vmem),
+        compiler_params=pltpu.CompilerParams(vmem_limit_bytes=16 << 20),
+        cost_estimate=pl.CostEstimate(flops=4 * m.size, transcendentals=0, bytes_accessed=8 * m.size),
+    )(m)
+
+
 def respond_kernel(*refs):
-    mh, ml, bands, mates, (out, c_all, ch, cl, sems) = refs[0], refs[1], refs[2:6], refs[6:10], refs[10:]
-    n_x, n_p, v1, v2 = bands[0].shape
-    s, core = lax.axis_index("state"), lax.rem(lax.axis_index("cond"), 2)
+    own, partner, blocks, others, (out, c_all, ch, cl, sems) = refs[:2], refs[2:4], refs[4:8], refs[8:12], refs[12:]
+    n_n, n_p, rows, _ = own[0].shape
+    _, v1, v2 = blocks[0].shape
+    s, k = lax.axis_index("state"), lax.axis_index("cond")
+    x_lo, core = lax.div(k, 2), lax.rem(k, 2)
     copies = []
     for i, shift in enumerate(SHIFTS):
         row = pl.multiple_of(lax.rem(s + 4 - shift, 4) * v1, v1)
-        for x in range(n_x):
-            for band, at in ((bands[i], core), (mates[i], 1 - core)):
-                col = pl.multiple_of((2 * x + at) * v2, v2)
-                target = c_all.at[:, pl.ds(row, v1), pl.ds(col, v2)]
-                copies.append(pltpu.make_async_copy(band.at[x], target, sems.at[len(copies)]))
+        for block, at in ((blocks[i], x_lo), (others[i], 1 - x_lo)):
+            target = c_all.at[:, pl.ds(row, v1), pl.ds(pl.multiple_of(at * v2, v2), v2)]
+            copies.append(pltpu.make_async_copy(block, target, sems.at[len(copies)]))
     for copy in copies:
         copy.start()
     out[...] = jnp.zeros_like(out)
@@ -107,32 +132,66 @@
     def _(p):
         ch[...], cl[...] = split(c_all[p])
 
-        @pl.loop(0, out.shape[0])
+        @pl.loop(0, n_n)
         def _(n):
-            out[n] += dot3((mh[n, p], ml[n, p]), (ch[...], cl[...]))
-
-
-def respond(m_pair, bands, mates):
-    n_n, n_p, rows, cols = m_pair[0].shape
+            for (mh, ml), at in ((own, core), (partner, 1 - core)):
+                part = dot3((mh[n, p], ml[n, p]), (ch[...], cl[...]))
+                for h in range(2):
+                    out[2 * n + h, at] += part[h * (rows // 2) : (h + 1) * (rows // 2)]
+
+
+def respond(own, partner, blocks, others):
+    n_n, n_p, rows, cols = own[0].shape
     any_spec = pl.BlockSpec(memory_space=pl.ANY)
     vmem = pl.BlockSpec(memory_space=pltpu.VMEM)
+    wide = 2 * blocks[0].shape[2]
     return pl.pallas_call(
         respond_kernel,
         name="respond",
-        out_shape=jax.ShapeDtypeStruct((n_n, rows, cols), f32),
-        in_specs=[vmem] * 2 + [any_spec] * 8,
+        out_shape=jax.ShapeDtypeStruct((2 * n_n, 2, rows // 2, wide), f32),
+        in_specs=[vmem] * 4 + [any_spec] * 8,
         out_specs=vmem,
         scratch_shapes=[
-            pltpu.VMEM((n_p, cols, cols), f32),
-            pltpu.VMEM((cols, cols), bf16),
-            pltpu.VMEM((cols, cols), bf16),
-            pltpu.SemaphoreType.DMA((16,)),
+            pltpu.VMEM((n_p, cols, wide), f32),
+            pltpu.VMEM((cols, wide), bf16),
+            pltpu.VMEM((cols, wide), bf16),
+            pltpu.SemaphoreType.DMA((8,)),
         ],
-        compiler_params=pltpu.CompilerParams(vmem_limit_bytes=28 << 20),
+        compiler_params=pltpu.CompilerParams(vmem_limit_bytes=24 << 20),
         cost_estimate=pl.CostEstimate(
             flops=3 * 2 * n_n * n_p * rows * cols * cols, transcendentals=0, bytes_accessed=1 << 24
         ),
-    )(*m_pair, *bands, *mates)
+    )(*own, *partner, *blocks, *others)
+
+
+def join_kernel(parts, out, sems):
+    copies = []
+    for i in range(parts.shape[0]):
+        t, core = divmod(i, 2)
+        for x in range(2):
+            v2 = parts.shape[2] // 2
+            source = parts.at[i, :, pl.ds(x * v2, v2)]
+            target = out.at[t, :, pl.ds((2 * x + core) * v2, v2)]
+            copies.append(pltpu.make_async_copy(source, target, sems.at[len(copies)]))
+    for copy in copies:
+        copy.start()
+    for copy in copies:
+        copy.wait()
+
+
+def join(parts):
+    n, rows, cols = parts.shape
+    any_spec = pl.BlockSpec(memory_space=pl.ANY)
+    return pl.pallas_call(
+        join_kernel,
+        name="join",
+        out_shape=jax.ShapeDtypeStruct((n // 2, rows, 2 * cols), f32),
+        in_specs=[any_spec],
+        out_specs=any_spec,
+        scratch_shapes=[pltpu.SemaphoreType.DMA((2 * n,))],
+        compiler_params=pltpu.CompilerParams(vmem_limit_bytes=1 << 20),
+        cost_estimate=pl.CostEstimate(flops=0, transcendentals=0, bytes_accessed=8 * parts.size),
+    )(parts)
 
 
 def moves(mesh, step):
@@ -161,6 +220,9 @@
     n_z = mesh.shape["aux"] // 2
     along_z = [[2 * z + half for z in range(n_z)] for half in range(2)]
     fours = [[4 * g + t for t in range(4)] for g in range(n_z // 2)]
+    eights = [
+        [(4 * g + t) * 4 + 2 * x + core for t in range(4) for core in range(2)] for g in range(n_z // 2) for x in range(2)
+    ]
     along_fours = [[4 * g + t for g in range(n_z // 2)] for t in range(4)]
 
     def send(value, pairs):
@@ -169,7 +231,6 @@
     def per_device(cond_pairs, val_pairs, screened, trials):
         n_p, _, _ = cond_pairs.shape
         half = lax.axis_index("aux") % 2
-        x_lo = lax.axis_index("cond") // 2
 
         slabs = [cond_pairs]
         for d in SHIFTS[1:]:
@@ -194,23 +255,28 @@
         block = lax.all_to_all(block, "aux", 0, 0, axis_index_groups=along_z)
         block = block.transpose(1, 0, 2, 3).reshape(n_p, v1, v2)
 
+        mixed, *own = mix(slabs, pieces)
+        mixed = send(mixed, to_core)
+
         other = send(block, to_pair)
-        two = jnp.stack([jnp.where(x_lo == 0, block, other), jnp.where(x_lo == 0, other, block)])
-        bands = [two]
+        blocks, others = [block], [other]
         for d in SHIFTS[1:]:
-            bands.append(send(two, to_y[d]))
-        mates = [send(band, to_core) for band in bands]
-
-        m_pair = mix(slabs, pieces)
-        partial = respond(m_pair, bands, mates)
-
-        swap = lambda value, groups: lax.all_to_all(value, "aux", 0, 0, axis_index_groups=groups)
-        parts = jnp.sum(swap(partial.reshape(4, -1, partial.shape[2]), fours), axis=0)
-        parts = jnp.sum(swap(parts.reshape(n_z // 2, -1, parts.shape[1]), along_fours), axis=0)
+            blocks.append(send(block, to_y[d]))
+        for d in SHIFTS[1:]:
+            others.append(send(other, to_y[d]))
+        partner = halves(mixed)
+        partial = respond(own, partner, blocks, others)
+
+        def swap(value, groups, axes="aux"):
+            return lax.all_to_all(value, axes, 0, 0, axis_index_groups=groups)
+
         copies = lambda value, count: jnp.broadcast_to(value, (count, *value.shape))
-        total = swap(copies(parts, n_z // 2), along_fours).reshape(-1, parts.shape[1])
-        total = swap(copies(total, 4), fours)
-        return total.reshape(partial.shape)
+        _, _, part_rows, cols = partial.shape
+        parts = jnp.sum(swap(partial.reshape(4, -1, cols), fours), axis=0)
+        parts = jnp.sum(swap(parts.reshape(n_z // 2, -1, cols), along_fours), axis=0)
+        total = swap(copies(parts, n_z // 2), along_fours).reshape(2, part_rows, cols)
+        total = swap(copies(total, 4).reshape(8, part_rows, cols), eights, ("aux", "cond"))
+        return join(total).reshape(trials.shape)
 
     in_specs = (P("aux", "cond", "state"), P("aux", "state", "cond"), P(), P("state", "cond", None))
     return jax.shard_map(per_device, mesh=mesh, in_specs=in_specs, out_specs=P("state", "cond", None), check_vma=False)

time: 250 us -> 270 us (1.080)
  blocking collectives: 87.7 us -> 110 us
  Pallas kernels: 17.9 us -> 21.6 us
  other arithmetic: 3.2 us -> 0.28 us
    all_to_all x4 -> x5, blocking collectives: 87.7 us -> 110 us  [the longest x4 84.2 us: swap(): return lax.all_to_all(value, axes, 0, 0, axis_index_groups=groups)]
    all_to_all x1 -> x0, starting transfers between devices: 7.39 us -> none  [per_device(): block = lax.all_to_all(block, 'aux', 0, 0, axis_index_groups=along_z)]
    ppermute x16, starting transfers between devices: 44.3 us -> 50.5 us  [send(): return lax.ppermute(value, AXES, pairs)]
    pallas_call x1 -> x3, Pallas kernels: 11.9 us -> 16.2 us  [the longest x1 12.1 us: mix(): pl.pallas_call(mix_kernel, name='mix', out_shape=(jax.ShapeDtypeStruct(sh...]
  transfers between devices with their start and end apart: 18 -> 17, of which waited for: 9 -> 7; matrix products, arithmetic and copies ran while one was open for 1% -> 1% of each run, Pallas kernels for 5% -> 1%
where the time goes in v4:
time: 270 us; the launch traced here: 267 us
  blocking collectives  110 us (41%)
  starting transfers between devices  65.7 us (24%)
  waiting for transfers between devices  64.2 us (24%)
  Pallas kernels  21.6 us (8%)
  local copies, waits for them, and re-layouts  4.1 us (2%)
    all_to_all x4, blocking collectives, swap(): return lax.all_to_all(value, axes, 0, 0, axis_index_groups=groups)  84.2 us
    ppermute x16, starting transfers between devices, send(): return lax.ppermute(value, AXES, pairs)  50.5 us
    ppermute x16, waiting for transfers between devices, send(): return lax.ppermute(value, AXES, pairs)  45.7 us
    all_to_all x1, blocking collectives, per_device(): block = lax.all_to_all(block, 'aux', 0, 0, axis_index_groups=along_z)  25.7 us
    all_to_all x1, waiting for transfers between devices, per_device(): spread = lax.all_to_all(spread, 'aux', 0, 0, axis_index_groups=along_z)  18.4 us
    all_to_all x1, starting transfers between devices, per_device(): spread = lax.all_to_all(spread, 'aux', 0, 0, axis_index_groups=along_z)  15.2 us
    pallas_call x1, Pallas kernels, mix(): pl.pallas_call(mix_kernel, name='mix', out_shape=(jax.ShapeDtypeStruct(sh...  12.1 us
    pallas_call x1, Pallas kernels, respond(): pl.pallas_call(respond_kernel, name='respond', out_shape=jax.ShapeDtypeSt...  5.41 us
  transfers between devices with their start and end apart: 17, of which 7 were waited for; matrix products, arithmetic and copies ran while one was open for 1% of the time, Pallas kernels for 1%

profile of v4, /device:TPU:24, one launch (start us, length us, event | category | flops | bytes accessed | tf_op | source)
XLA Modules:
  0.0 266.9 jit_solution(14556088868069686463)
XLA Ops:
  0.0 1.4 slice_bitcast_fusion.1
  1.4 4.7 %collective-permute-start.5 = (f32[256,512]{1,0:T(8,128)S(1)}, f32[256,512]{1,0:T(8,128)S(1)}, u32[]{:S(2)}, u32[]{:S(2)}) collective-permute-start(f32[256,512]{1,0:T(8,128)S(1)} %get-tuple-element.16), channel_id=1, source_target_pairs={{0,6},{1,7},{2,0},{3,1},{4,2},{5,3},{6,4},{7,5},{8,14},{9,15},{10,... | collective-permute-start | bytes 1572872 | tf_op jit(solution)/shard_map/ppermute | solution.py:229
  6.1 1.9 collective-permute-start.4
  8.0 6.7 %collective-permute-start = (f32[4,256,256]{2,1,0:T(8,128)S(1)}, f32[4,256,256]{2,1,0:T(8,128)S(1)}, u32[]{:S(2)}, u32[]{:S(2)}) collective-permute-start(f32[4,256,256]{2,1,0:T(8,128)S(1)} %copy-done.2), channel_id=1, source_target_pairs={{0,128},{1,129},{2,130},{3,131},{4,132},{5,133},{6,134},{7,135},{8... | collective-permute-start | bytes 3145736 | tf_op jit(solution)/shard_map/ppermute | solution.py:229
  14.8 1.9 collective-permute-start.1
  16.7 3.4 %collective-permute-start.2 = (f32[4,256,256]{2,1,0:T(8,128)S(1)}, f32[4,256,256]{2,1,0:T(8,128)S(1)}, u32[]{:S(2)}, u32[]{:S(2)}) collective-permute-start(f32[4,256,256]{2,1,0:T(8,128)S(1)} %copy-done.2), channel_id=1, source_target_pairs={{0,256},{1,257},{2,258},{3,259},{4,260},{5,261},{6,262},{7,263},{8... | collective-permute-start | bytes 3145736 | tf_op jit(solution)/shard_map/ppermute | solution.py:229
  20.1 1.9 collective-permute-start.3
  22.7 2.1 collective-permute-start.6
  24.7 11.2 %collective-permute-done.refs_1_ = f32[4,256,256]{2,1,0:T(8,128)S(1)} collective-permute-done((f32[4,256,256]{2,1,0:T(8,128)S(1)}, f32[4,256,256]{2,1,0:T(8,128)S(1)}, u32[]{:S(2)}, u32[]{:S(2)}) %collective-permute-start) | collective-permute-done | bytes 1048608 | tf_op jit(solution)/shard_map/ppermute | solution.py:229
  36.0 24.2 %collective-permute-done.1.refs_2_ = f32[4,256,256]{2,1,0:T(8,128)S(1)} collective-permute-done((f32[4,256,256]{2,1,0:T(8,128)S(1)}, f32[4,256,256]{2,1,0:T(8,128)S(1)}, u32[]{:S(2)}, u32[]{:S(2)}) %collective-permute-start.1) | collective-permute-done | bytes 1048608 | tf_op jit(solution)/shard_map/ppermute | solution.py:229
  60.2 12.1 %mix.1 = (f32[2,4,256,512]{3,2,1,0:T(8,128)}, bf16[2,4,256,512]{3,2,1,0:T(8,128)(2,1)S(1)}, bf16[2,4,256,512]{3,2,1,0:T(8,128)(2,1)S(1)}) custom-call(f32[4,256,256]{2,1,0:T(8,128)S(1)} %copy-done.2, f32[4,256,256]{2,1,0:T(8,128)S(1)} %collective-permute-done.refs_1_, f32[4,256,256]{2,1,0:T(8,128)S(1)} %collective-permute-done.1.refs_2_, ...), custom_call_target="tpu_custom_call" | custom-call | flops 6442450944 | bytes 16777216 | tf_op jit(solution)/shard_map/mix/pallas_call | solution.py:69
  72.3 1.4 copy-done.3
  73.7 1.9 collective-permute-start.7
  76.5 15.2 %all-to-all-start = ((f32[16,4,8,128]{3,1,2,0:T(4,128)}), f32[16,4,8,128]{3,1,2,0:T(4,128)S(1)}, u32[]{:S(2)}, u32[]{:S(2)}) async-start(f32[16,4,8,128]{3,1,2,0:T(4,128)} %bitcast.8), calls=%async_computation | async-start | bytes 524288 | tf_op jit(solution)/shard_map/all_to_all | solution.py:244
  92.2 18.4 %all-to-all-done = f32[16,4,8,128]{3,1,2,0:T(4,128)S(1)} async-done(((f32[16,4,8,128]{3,1,2,0:T(4,128)}), f32[16,4,8,128]{3,1,2,0:T(4,128)S(1)}, u32[]{:S(2)}, u32[]{:S(2)}) %all-to-all-start) | async-done | bytes 262176 | tf_op jit(solution)/shard_map/all_to_all | solution.py:244
  111.3 3.9 %collective-permute-start.8 = (f32[16,4,8,128]{3,2,1,0:T(8,128)S(1)}, f32[16,4,8,128]{3,2,1,0:T(8,128)S(1)}, u32[]{:S(2)}, u32[]{:S(2)}) collective-permute-start(f32[16,4,8,128]{3,2,1,0:T(8,128)S(1)} %bitcast.43), channel_id=1, source_target_pairs={{0,4},{1,5},{2,6},{3,7},{4,0},{5,1},{6,2},{7,3},{8,12},{9,13},{10,... | collective-permute-start | bytes 786440 | tf_op jit(solution)/shard_map/ppermute | solution.py:229
  115.3 5.9 %collective-permute-done.8 = f32[16,4,8,128]{3,2,1,0:T(8,128)S(1)} collective-permute-done((f32[16,4,8,128]{3,2,1,0:T(8,128)S(1)}, f32[16,4,8,128]{3,2,1,0:T(8,128)S(1)}, u32[]{:S(2)}, u32[]{:S(2)}) %collective-permute-start.8) | collective-permute-done | bytes 262176 | tf_op jit(solution)/shard_map/ppermute | solution.py:229
  121.2 25.7 %all_to_all.30 = f32[16,4,8,128]{3,2,1,0:T(8,128)S(1)} all-to-all(f32[16,4,8,128]{3,2,1,0:T(8,128)S(1)} %bitcast_add_fusion), channel_id=1, replica_groups={{0,8,16,24,32,40,48,56,64,72,80,88,96,104,112,120},{4,12,20,28,36,44,52..., dimensions={0} | all-to-all | bytes 524288 | tf_op jit(solution)/shard_map/all_to_all | solution.py:255
  147.0 2.8 %collective-permute-start.12 = (f32[4,128,128]{2,1,0:T(8,128)S(1)}, f32[4,128,128]{2,1,0:T(8,128)S(1)}, u32[]{:S(2)}, u32[]{:S(2)}) collective-permute-start(f32[4,128,128]{2,1,0:T(8,128)S(1)} %copy_bitcast_fusion.refs_4_), channel_id=1, source_target_pairs={{0,2},{1,3},{2,0},{3,1},{4,6},{5,7},{6,4},{7,5},{8,10},{9,11},{10,... | collective-permute-start | bytes 786440 | tf_op jit(solution)/shard_map/ppermute | solution.py:229
  149.7 1.9 collective-permute-start.9
  151.7 3.9 %collective-permute-start.10 = (f32[4,128,128]{2,1,0:T(8,128)S(1)}, f32[4,128,128]{2,1,0:T(8,128)S(1)}, u32[]{:S(2)}, u32[]{:S(2)}) collective-permute-start(f32[4,128,128]{2,1,0:T(8,128)S(1)} %copy_bitcast_fusion.refs_4_), channel_id=1, source_target_pairs={{0,384},{1,385},{2,386},{3,387},{4,388},{5,389},{6,390},{7,391},{8... | collective-permute-start | bytes 786440 | tf_op jit(solution)/shard_map/ppermute | solution.py:229
  155.6 3.9 %collective-permute-start.11 = (f32[4,128,128]{2,1,0:T(8,128)S(1)}, f32[4,128,128]{2,1,0:T(8,128)S(1)}, u32[]{:S(2)}, u32[]{:S(2)}) collective-permute-start(f32[4,128,128]{2,1,0:T(8,128)S(1)} %copy_bitcast_fusion.refs_4_), channel_id=1, source_target_pairs={{0,256},{1,257},{2,258},{3,259},{4,260},{5,261},{6,262},{7,263},{8... | collective-permute-start | bytes 786440 | tf_op jit(solution)/shard_map/ppermute | solution.py:229
  159.5 2.6 collective-permute-start.13
  162.1 3.2 %collective-permute-start.14 = (f32[4,128,128]{2,1,0:T(8,128)S(1)}, f32[4,128,128]{2,1,0:T(8,128)S(1)}, u32[]{:S(2)}, u32[]{:S(2)}) collective-permute-start(f32[4,128,128]{2,1,0:T(8,128)S(1)} %collective-permute-done.12.refs_8_), channel_id=1, source_target_pairs={{0,384},{1,385},{2,386},{3,387},{4,388},{5,389},{6,390},{7,391},{8... | collective-permute-start | bytes 786440 | tf_op jit(solution)/shard_map/ppermute | solution.py:229
  165.4 3.7 %collective-permute-start.15 = (f32[4,128,128]{2,1,0:T(8,128)S(1)}, f32[4,128,128]{2,1,0:T(8,128)S(1)}, u32[]{:S(2)}, u32[]{:S(2)}) collective-permute-start(f32[4,128,128]{2,1,0:T(8,128)S(1)} %collective-permute-done.12.refs_8_), channel_id=1, source_target_pairs={{0,256},{1,257},{2,258},{3,259},{4,260},{5,261},{6,262},{7,263},{8... | collective-permute-start | bytes 786440 | tf_op jit(solution)/shard_map/ppermute | solution.py:229
  169.1 2.9 %halves.1 = (bf16[2,4,256,512]{3,2,1,0:T(8,128)(2,1)S(1)}, bf16[2,4,256,512]{3,2,1,0:T(8,128)(2,1)S(1)}) custom-call(f32[2,4,256,512]{3,2,1,0:T(8,128)} %collective-permute-done.7.m), custom_call_target="tpu_custom_call" | custom-call | flops 4194304 | bytes 8388608 | tf_op jit(solution)/shard_map/halves/pallas_call | solution.py:102
  173.1 2.8 %collective-permute-done.15.refs_11_ = f32[4,128,128]{2,1,0:T(8,128)S(1)} collective-permute-done((f32[4,128,128]{2,1,0:T(8,128)S(1)}, f32[4,128,128]{2,1,0:T(8,128)S(1)}, u32[]{:S(2)}, u32[]{:S(2)}) %collective-permute-start.15) | collective-permute-done | bytes 262176 | tf_op jit(solution)/shard_map/ppermute | solution.py:229
  176.0 5.4 %respond.1 = f32[4,2,128,256]{3,2,1,0:T(8,128)S(1)} custom-call(bf16[2,4,256,512]{3,2,1,0:T(8,128)(2,1)S(1)} %get-tuple-element.10.refs_0_, bf16[2,4,256,512]{3,2,1,0:T(8,128)(2,1)S(1)} %copy-done.4, bf16[2,4,256,512]{3,2,1,0:T(8,128)(2,1)S(1)} %get-tuple-element.13.refs_2_, bf16[2,4,256,512]{3,2,1,0:T(8,128)(2,1)S(1)} %get-tuple-element.14.refs_3_, ...), custom_call_target="tpu_custom_call" | custom-call | flops 3221225472 | bytes 16777216 | tf_op jit(solution)/shard_map/respond/pallas_call | solution.py:148
  181.4 22.0 %all_to_all.31 = f32[4,256,256]{2,1,0:T(8,128)S(1)} all-to-all(f32[4,256,256]{2,1,0:T(8,128)S(1)} %bitcast.36), channel_id=1, replica_groups={{0,4,8,12},{16,20,24,28},{32,36,40,44},{48,52,56,60},{64,68,72,76},{80,..., dimensions={0} | all-to-all | bytes 2097152 | tf_op jit(solution)/shard_map/all_to_all | solution.py:271
  203.5 23.3 %all_to_all.32 = f32[8,32,256]{2,1,0:T(8,128)S(1)} all-to-all(f32[8,32,256]{2,1,0:T(8,128)S(1)} %bitcast.38), channel_id=1, replica_groups={{0,16,32,48,64,80,96,112},{4,20,36,52,68,84,100,116},{8,24,40,56,72,88,..., dimensions={0} | all-to-all | bytes 524288 | tf_op jit(solution)/shard_map/all_to_all | solution.py:271
  226.9 20.3 %all_to_all.33 = f32[8,32,256]{2,1,0:T(8,128)S(1)} all-to-all(f32[8,32,256]{2,1,0:T(8,128)S(1)} %broadcast_in_dim.6), channel_id=1, replica_groups={{0,16,32,48,64,80,96,112},{4,20,36,52,68,84,100,116},{8,24,40,56,72,88,..., dimensions={0} | all-to-all | bytes 524288 | tf_op jit(solution)/shard_map/all_to_all | solution.py:271
  247.2 18.5 %all_to_all.34.parts = f32[8,128,256]{2,1,0:T(8,128)S(1)} all-to-all(f32[8,128,256]{2,1,0:T(8,128)S(1)} %bitcast.37), channel_id=1, replica_groups={{0,1,4,5,8,9,12,13},{2,3,6,7,10,11,14,15},{16,17,20,21,24,25,28,29},{18..., dimensions={0} | all-to-all | bytes 2097152 | tf_op jit(solution)/shard_map/all_to_all | solution.py:271
  (41 shorter events, 5.1 us)
Async XLA Ops:
  0.0 91.8 %copy-start = (f32[128,128]{1,0:T(8,128)S(1)}, f32[128,128]{1,0:T(8,128)}, u32[]{:S(2)}) copy-start(f32[128,128]{1,0:T(8,128)} %param.6) | copy-start | bytes 196612
  0.0 20.1 %copy-start.1 = (f32[2,256,512]{2,1,0:T(8,128)S(1)}, f32[2,256,512]{2,1,0:T(8,128)}, u32[]{:S(2)}) copy-start(f32[2,256,512]{2,1,0:T(8,128)} %refs_4_.1) | copy-start | bytes 3145732
  0.0 8.0 %copy-start.2 = (f32[4,256,256]{2,1,0:T(8,128)S(1)}, f32[4,256,256]{2,1,0:T(8,128)}, u32[]{:S(2)}) copy-start(f32[4,256,256]{2,1,0:T(8,128)} %refs_0_.1) | copy-start | bytes 3145732
  1.4 18.7 %collective-permute-start.5 = (f32[256,512]{1,0:T(8,128)S(1)}, f32[256,512]{1,0:T(8,128)S(1)}, u32[]{:S(2)}, u32[]{:S(2)}) collective-permute-start(f32[256,512]{1,0:T(8,128)S(1)} %get-tuple-element.16), channel_id=1, source_target_pairs={{0,6},{1,7},{2,0},{3,1},{4,2},{5,3},{6,4},{7,5},{8,14},{9,15},{10,... | collective-permute-start | bytes 1572872 | tf_op jit(solution)/shard_map/ppermute | solution.py:229
  6.1 16.5 %collective-permute-start.4 = (f32[256,512]{1,0:T(8,128)S(1)}, f32[256,512]{1,0:T(8,128)S(1)}, u32[]{:S(2)}, u32[]{:S(2)}) collective-permute-start(f32[256,512]{1,0:T(8,128)S(1)} %get-tuple-element.15), channel_id=1, source_target_pairs={{0,2},{1,3},{2,4},{3,5},{4,6},{5,7},{6,0},{7,1},{8,10},{9,11},{10,... | collective-permute-start | bytes 1572872 | tf_op jit(solution)/shard_map/ppermute | solution.py:229
  8.0 27.9 %collective-permute-start = (f32[4,256,256]{2,1,0:T(8,128)S(1)}, f32[4,256,256]{2,1,0:T(8,128)S(1)}, u32[]{:S(2)}, u32[]{:S(2)}) collective-permute-start(f32[4,256,256]{2,1,0:T(8,128)S(1)} %copy-done.2), channel_id=1, source_target_pairs={{0,128},{1,129},{2,130},{3,131},{4,132},{5,133},{6,134},{7,135},{8... | collective-permute-start | bytes 3145736 | tf_op jit(solution)/shard_map/ppermute | solution.py:229
  14.8 45.4 %collective-permute-start.1 = (f32[4,256,256]{2,1,0:T(8,128)S(1)}, f32[4,256,256]{2,1,0:T(8,128)S(1)}, u32[]{:S(2)}, u32[]{:S(2)}) collective-permute-start(f32[4,256,256]{2,1,0:T(8,128)S(1)} %copy-done.2), channel_id=1, source_target_pairs={{0,384},{1,385},{2,386},{3,387},{4,388},{5,389},{6,390},{7,391},{8... | collective-permute-start | bytes 3145736 | tf_op jit(solution)/shard_map/ppermute | solution.py:229
  16.7 43.5 %collective-permute-start.2 = (f32[4,256,256]{2,1,0:T(8,128)S(1)}, f32[4,256,256]{2,1,0:T(8,128)S(1)}, u32[]{:S(2)}, u32[]{:S(2)}) collective-permute-start(f32[4,256,256]{2,1,0:T(8,128)S(1)} %copy-done.2), channel_id=1, source_target_pairs={{0,256},{1,257},{2,258},{3,259},{4,260},{5,261},{6,262},{7,263},{8... | collective-permute-start | bytes 3145736 | tf_op jit(solution)/shard_map/ppermute | solution.py:229
  20.1 40.1 %collective-permute-start.3 = (f32[2,256,512]{2,1,0:T(8,128)S(1)}, f32[2,256,512]{2,1,0:T(8,128)S(1)}, u32[]{:S(2)}, u32[]{:S(2)}) collective-permute-start(f32[2,256,512]{2,1,0:T(8,128)S(1)} %copy-done.1), channel_id=1, source_target_pairs={{0,1},{1,0},{2,3},{3,2},{4,5},{5,4},{6,7},{7,6},{8,9},{9,8},{10,11... | collective-permute-start | bytes 3145736 | tf_op jit(solution)/shard_map/ppermute | solution.py:229
  22.7 53.0 %copy-start.5 = (f32[4,128,128]{2,1,0:T(8,128)S(1)}, f32[4,128,128]{2,1,0:T(8,128)}, u32[]{:S(2)}) copy-start(f32[4,128,128]{2,1,0:T(8,128)} %param.5) | copy-start | bytes 786436
  22.7 37.5 %collective-permute-start.6 = (f32[2,256,512]{2,1,0:T(8,128)S(1)}, f32[2,256,512]{2,1,0:T(8,128)S(1)}, u32[]{:S(2)}, u32[]{:S(2)}) collective-permute-start(f32[2,256,512]{2,1,0:T(8,128)S(1)} %pad_maximum_fusion.refs_6_), channel_id=1, source_target_pairs={{0,1},{1,0},{2,3},{3,2},{4,5},{5,4},{6,7},{7,6},{8,9},{9,8},{10,11... | collective-permute-start | bytes 3145736 | tf_op jit(solution)/shard_map/ppermute | solution.py:229
  72.3 1.4 copy-start.3
  73.7 91.6 %collective-permute-start.7 = (f32[2,4,256,512]{3,2,1,0:T(8,128)}, f32[2,4,256,512]{3,2,1,0:T(8,128)}, u32[]{:S(2)}, u32[]{:S(2)}) collective-permute-start(f32[2,4,256,512]{3,2,1,0:T(8,128)} %get-tuple-element.12), channel_id=1, source_target_pairs={{0,1},{1,0},{2,3},{3,2},{4,5},{5,4},{6,7},{7,6},{8,9},{9,8},{10,11... | collective-permute-start | bytes 12582920 | tf_op jit(solution)/shard_map/ppermute | solution.py:229
  76.5 34.0 %all-to-all-start = ((f32[16,4,8,128]{3,1,2,0:T(4,128)}), f32[16,4,8,128]{3,1,2,0:T(4,128)S(1)}, u32[]{:S(2)}, u32[]{:S(2)}) async-start(f32[16,4,8,128]{3,1,2,0:T(4,128)} %bitcast.8), calls=%async_computation | async-start | bytes 524288 | tf_op jit(solution)/shard_map/all_to_all | solution.py:244
  111.3 9.8 %collective-permute-start.8 = (f32[16,4,8,128]{3,2,1,0:T(8,128)S(1)}, f32[16,4,8,128]{3,2,1,0:T(8,128)S(1)}, u32[]{:S(2)}, u32[]{:S(2)}) collective-permute-start(f32[16,4,8,128]{3,2,1,0:T(8,128)S(1)} %bitcast.43), channel_id=1, source_target_pairs={{0,4},{1,5},{2,6},{3,7},{4,0},{5,1},{6,2},{7,3},{8,12},{9,13},{10,... | collective-permute-start | bytes 786440 | tf_op jit(solution)/shard_map/ppermute | solution.py:229
  147.0 29.0 %copy-start.4 = (bf16[2,4,256,512]{3,2,1,0:T(8,128)(2,1)S(1)}, bf16[2,4,256,512]{3,2,1,0:T(8,128)(2,1)}, u32[]{:S(2)}) copy-start(bf16[2,4,256,512]{3,2,1,0:T(8,128)(2,1)} %copy-done.3) | copy-start | bytes 6291460
  147.0 12.5 %collective-permute-start.12 = (f32[4,128,128]{2,1,0:T(8,128)S(1)}, f32[4,128,128]{2,1,0:T(8,128)S(1)}, u32[]{:S(2)}, u32[]{:S(2)}) collective-permute-start(f32[4,128,128]{2,1,0:T(8,128)S(1)} %copy_bitcast_fusion.refs_4_), channel_id=1, source_target_pairs={{0,2},{1,3},{2,0},{3,1},{4,6},{5,7},{6,4},{7,5},{8,10},{9,11},{10,... | collective-permute-start | bytes 786440 | tf_op jit(solution)/shard_map/ppermute | solution.py:229
  149.7 12.4 %collective-permute-start.9 = (f32[4,128,128]{2,1,0:T(8,128)S(1)}, f32[4,128,128]{2,1,0:T(8,128)S(1)}, u32[]{:S(2)}, u32[]{:S(2)}) collective-permute-start(f32[4,128,128]{2,1,0:T(8,128)S(1)} %copy_bitcast_fusion.refs_4_), channel_id=1, source_target_pairs={{0,128},{1,129},{2,130},{3,131},{4,132},{5,133},{6,134},{7,135},{8... | collective-permute-start | bytes 786440 | tf_op jit(solution)/shard_map/ppermute | solution.py:229
  151.7 20.4 %collective-permute-start.10 = (f32[4,128,128]{2,1,0:T(8,128)S(1)}, f32[4,128,128]{2,1,0:T(8,128)S(1)}, u32[]{:S(2)}, u32[]{:S(2)}) collective-permute-start(f32[4,128,128]{2,1,0:T(8,128)S(1)} %copy_bitcast_fusion.refs_4_), channel_id=1, source_target_pairs={{0,384},{1,385},{2,386},{3,387},{4,388},{5,389},{6,390},{7,391},{8... | collective-permute-start | bytes 786440 | tf_op jit(solution)/shard_map/ppermute | solution.py:229
  155.6 16.5 %collective-permute-start.11 = (f32[4,128,128]{2,1,0:T(8,128)S(1)}, f32[4,128,128]{2,1,0:T(8,128)S(1)}, u32[]{:S(2)}, u32[]{:S(2)}) collective-permute-start(f32[4,128,128]{2,1,0:T(8,128)S(1)} %copy_bitcast_fusion.refs_4_), channel_id=1, source_target_pairs={{0,256},{1,257},{2,258},{3,259},{4,260},{5,261},{6,262},{7,263},{8... | collective-permute-start | bytes 786440 | tf_op jit(solution)/shard_map/ppermute | solution.py:229
  159.5 12.6 %collective-permute-start.13 = (f32[4,128,128]{2,1,0:T(8,128)S(1)}, f32[4,128,128]{2,1,0:T(8,128)S(1)}, u32[]{:S(2)}, u32[]{:S(2)}) collective-permute-start(f32[4,128,128]{2,1,0:T(8,128)S(1)} %collective-permute-done.12.refs_8_), channel_id=1, source_target_pairs={{0,128},{1,129},{2,130},{3,131},{4,132},{5,133},{6,134},{7,135},{8... | collective-permute-start | bytes 786440 | tf_op jit(solution)/shard_map/ppermute | solution.py:229
  162.1 11.0 %collective-permute-start.14 = (f32[4,128,128]{2,1,0:T(8,128)S(1)}, f32[4,128,128]{2,1,0:T(8,128)S(1)}, u32[]{:S(2)}, u32[]{:S(2)}) collective-permute-start(f32[4,128,128]{2,1,0:T(8,128)S(1)} %collective-permute-done.12.refs_8_), channel_id=1, source_target_pairs={{0,384},{1,385},{2,386},{3,387},{4,388},{5,389},{6,390},{7,391},{8... | collective-permute-start | bytes 786440 | tf_op jit(solution)/shard_map/ppermute | solution.py:229
  165.4 10.6 %collective-permute-start.15 = (f32[4,128,128]{2,1,0:T(8,128)S(1)}, f32[4,128,128]{2,1,0:T(8,128)S(1)}, u32[]{:S(2)}, u32[]{:S(2)}) collective-permute-start(f32[4,128,128]{2,1,0:T(8,128)S(1)} %collective-permute-done.12.refs_8_), channel_id=1, source_target_pairs={{0,256},{1,257},{2,258},{3,259},{4,260},{5,261},{6,262},{7,263},{8... | collective-permute-start | bytes 786440 | tf_op jit(solution)/shard_map/ppermute | solution.py:229

commit v5 on v3

--- a/solution.py
+++ b/solution.py
@@ -85,10 +85,24 @@
     )(*slabs, *pieces)
 
 
-def respond_kernel(*refs):
-    mh, ml, bands, mates, (out, c_all, ch, cl, sems) = refs[0], refs[1], refs[2:6], refs[6:10], refs[10:]
+def rows_of(m, t, p):
+    rows = m.shape[2] // 2
+    return m[lax.div(t, 2), p, pl.ds(pl.multiple_of(lax.rem(t, 2) * rows, rows), rows), :]
+
+
+def add_products(outs, places, mh, ml, p, c_pair):
+    both = [jnp.concatenate([rows_of(m, t, p) for t in places], axis=0) for m in (mh, ml)]
+    part = dot3(both, c_pair)
+    rows = part.shape[0] // 2
+    outs[0][...] += part[:rows]
+    outs[1][...] += part[rows:]
+
+
+def far_kernel(*refs):
+    mh, ml, bands, mates, (across, diagonal, ch, cl, c_all, sems) = refs[0], refs[1], refs[2:6], refs[6:10], refs[10:]
     n_x, n_p, v1, v2 = bands[0].shape
     s, core = lax.axis_index("state"), lax.rem(lax.axis_index("cond"), 2)
+    place = lax.rem(lax.axis_index("aux"), 4)
     copies = []
     for i, shift in enumerate(SHIFTS):
         row = pl.multiple_of(lax.rem(s + 4 - shift, 4) * v1, v1)
@@ -99,40 +113,60 @@
                 copies.append(pltpu.make_async_copy(band.at[x], target, sems.at[len(copies)]))
     for copy in copies:
         copy.start()
-    out[...] = jnp.zeros_like(out)
+    across[...] = jnp.zeros_like(across)
+    diagonal[...] = jnp.zeros_like(diagonal)
     for copy in copies:
         copy.wait()
+    places = [jnp.bitwise_xor(place, 1), jnp.bitwise_xor(place, 3)]
 
     @pl.loop(0, n_p)
     def _(p):
-        ch[...], cl[...] = split(c_all[p])
-
-        @pl.loop(0, out.shape[0])
-        def _(n):
-            out[n] += dot3((mh[n, p], ml[n, p]), (ch[...], cl[...]))
-
-
-def respond(m_pair, bands, mates):
-    n_n, n_p, rows, cols = m_pair[0].shape
+        ch[p], cl[p] = split(c_all[p])
+        add_products((across, diagonal), places, mh, ml, p, (ch[p], cl[p]))
+
+
+def near_kernel(mh, ml, ch, cl, beside, here):
+    place = lax.rem(lax.axis_index("aux"), 4)
+    places = [jnp.bitwise_xor(place, 2), place]
+    beside[...] = jnp.zeros_like(beside)
+    here[...] = jnp.zeros_like(here)
+
+    @pl.loop(0, mh.shape[1])
+    def _(p):
+        add_products((beside, here), places, mh, ml, p, (ch[p], cl[p]))
+
+
+def respond_far(m_pair, bands, mates):
+    _, n_p, rows, cols = m_pair[0].shape
     any_spec = pl.BlockSpec(memory_space=pl.ANY)
     vmem = pl.BlockSpec(memory_space=pltpu.VMEM)
+    part = jax.ShapeDtypeStruct((rows // 2, cols), f32)
+    full = jax.ShapeDtypeStruct((n_p, cols, cols), bf16)
     return pl.pallas_call(
-        respond_kernel,
-        name="respond",
-        out_shape=jax.ShapeDtypeStruct((n_n, rows, cols), f32),
+        far_kernel,
+        name="respond_far",
+        out_shape=(part, part, full, full),
         in_specs=[vmem] * 2 + [any_spec] * 8,
-        out_specs=vmem,
-        scratch_shapes=[
-            pltpu.VMEM((n_p, cols, cols), f32),
-            pltpu.VMEM((cols, cols), bf16),
-            pltpu.VMEM((cols, cols), bf16),
-            pltpu.SemaphoreType.DMA((16,)),
-        ],
+        out_specs=(vmem,) * 4,
+        scratch_shapes=[pltpu.VMEM((n_p, cols, cols), f32), pltpu.SemaphoreType.DMA((16,))],
         compiler_params=pltpu.CompilerParams(vmem_limit_bytes=28 << 20),
-        cost_estimate=pl.CostEstimate(
-            flops=3 * 2 * n_n * n_p * rows * cols * cols, transcendentals=0, bytes_accessed=1 << 24
-        ),
+        cost_estimate=pl.CostEstimate(flops=6 * n_p * rows * cols * cols, transcendentals=0, bytes_accessed=1 << 23),
     )(*m_pair, *bands, *mates)
+
+
+def respond_near(m_pair, c_pair):
+    _, n_p, rows, cols = m_pair[0].shape
+    vmem = pl.BlockSpec(memory_space=pltpu.VMEM)
+    part = jax.ShapeDtypeStruct((rows // 2, cols), f32)
+    return pl.pallas_call(
+        near_kernel,
+        name="respond_near",
+        out_shape=(part, part),
+        in_specs=[vmem] * 4,
+        out_specs=(vmem, vmem),
+        compiler_params=pltpu.CompilerParams(vmem_limit_bytes=28 << 20),
+        cost_estimate=pl.CostEstimate(flops=6 * n_p * rows * cols * cols, transcendentals=0, bytes_accessed=1 << 23),
+    )(*m_pair, *c_pair)
 
 
 def moves(mesh, step):
@@ -156,6 +190,8 @@
 def solution(mesh):
     to_core = moves(mesh, lambda y, z, x, c: (y, z, x, 1 - c))
     to_x = {d: moves(mesh, lambda y, z, x, c, d=d: (y, z, x + d, c)) for d in (1, -1, 2)}
+    to_beside = moves(mesh, lambda y, z, x, c: (y, z ^ 1, x, c))
+    to_diagonal = moves(mesh, lambda y, z, x, c: (y, z ^ 1, x + 2, c))
     to_pair = moves(mesh, lambda y, z, x, c: (y, z, x ^ 1, c))
     to_y = {d: moves(mesh, lambda y, z, x, c, d=d: (y + d, z, x, c)) for d in (1, -1, 2)}
     n_z = mesh.shape["aux"] // 2
@@ -202,15 +238,19 @@
         mates = [send(band, to_core) for band in bands]
 
         m_pair = mix(slabs, pieces)
-        partial = respond(m_pair, bands, mates)
-
+        across, diagonal, *c_pair = respond_far(m_pair, bands, mates)
+
+        across = send(across, to_x[2])
+        diagonal = send(diagonal, to_diagonal)
+        beside, here = respond_near(m_pair, c_pair)
+        beside = send(beside, to_beside)
+        parts = (here + beside) + (across + diagonal)
         swap = lambda value, groups: lax.all_to_all(value, "aux", 0, 0, axis_index_groups=groups)
-        parts = jnp.sum(swap(partial.reshape(4, -1, partial.shape[2]), fours), axis=0)
         parts = jnp.sum(swap(parts.reshape(n_z // 2, -1, parts.shape[1]), along_fours), axis=0)
         copies = lambda value, count: jnp.broadcast_to(value, (count, *value.shape))
         total = swap(copies(parts, n_z // 2), along_fours).reshape(-1, parts.shape[1])
         total = swap(copies(total, 4), fours)
-        return total.reshape(partial.shape)
+        return total.reshape(trials.shape)
 
     in_specs = (P("aux", "cond", "state"), P("aux", "state", "cond"), P(), P("state", "cond", None))
     return jax.shard_map(per_device, mesh=mesh, in_specs=in_specs, out_specs=P("state", "cond", None), check_vma=False)

time: 250 us -> 250 us (level)
  blocking collectives: 87.7 us -> 70.2 us
  starting transfers between devices: 66.9 us -> 77.6 us
  waiting for transfers between devices: 64.6 us -> 72 us
    all_to_all x4 -> x3, blocking collectives: 87.7 us -> 70.2 us  [per_device(): lax.all_to_all(value, 'aux', 0, 0, axis_index_groups=groups)]
    ppermute x16 -> x19, starting transfers between devices: 44.3 us -> 55 us  [send(): return lax.ppermute(value, AXES, pairs)]
    ppermute x16 -> x19, waiting for transfers between devices: 45.6 us -> 52.9 us  [send(): return lax.ppermute(value, AXES, pairs)]
    pallas_call x1 -> x2, Pallas kernels: 5.96 us -> 5.56 us  [the longest x1 3.24 us: respond_far(): pl.pallas_call(far_kernel, name='respond_far', out_shape=(part, part, ful...]
  transfers between devices with their start and end apart: 18 -> 21, of which waited for: 9 -> 11; matrix products, arithmetic and copies ran while one was open for 1% -> 1% of each run, Pallas kernels for 5% -> 6%
where the time goes in v5:
time: 250 us; the launch traced here: 247 us
  starting transfers between devices  77.6 us (31%)
  waiting for transfers between devices  72 us (29%)
  blocking collectives  70.2 us (28%)
  Pallas kernels  17.5 us (7%)
  local copies, waits for them, and re-layouts  5 us (2%)
  other arithmetic  3.2 us (1%)
    all_to_all x3, blocking collectives, per_device(): lax.all_to_all(value, 'aux', 0, 0, axis_index_groups=groups)  70.2 us
    ppermute x19, starting transfers between devices, send(): return lax.ppermute(value, AXES, pairs)  55 us
    ppermute x19, waiting for transfers between devices, send(): return lax.ppermute(value, AXES, pairs)  52.9 us
    all_to_all x1, waiting for transfers between devices, per_device(): spread = lax.all_to_all(spread, 'aux', 0, 0, axis_index_groups=along_z)  18 us
    all_to_all x1, starting transfers between devices, per_device(): spread = lax.all_to_all(spread, 'aux', 0, 0, axis_index_groups=along_z)  15.2 us
    pallas_call x1, Pallas kernels, mix(): pl.pallas_call(mix_kernel, name='mix', out_shape=(shape, shape), in_specs...  11.9 us
    all_to_all x1, starting transfers between devices, per_device(): block = lax.all_to_all(block, 'aux', 0, 0, axis_index_groups=along_z)  7.39 us
  transfers between devices with their start and end apart: 21, of which 11 were waited for; matrix products, arithmetic and copies ran while one was open for 1% of the time, Pallas kernels for 6%

profile of v5, /device:TPU:24, one launch (start us, length us, event | category | flops | bytes accessed | tf_op | source)
XLA Modules:
  0.0 246.8 jit_solution(17490320958690964698)
XLA Ops:
  1.9 15.2 %all-to-all-start = ((f32[16,4,8,128]{3,1,2,0:T(4,128)}), f32[16,4,8,128]{3,1,2,0:T(4,128)S(1)}, u32[]{:S(2)}, u32[]{:S(2)}) async-start(f32[16,4,8,128]{3,1,2,0:T(4,128)} %bitcast.8), calls=%async_computation | async-start | bytes 524288 | tf_op jit(solution)/shard_map/all_to_all | solution.py:219
  17.5 18.0 %all-to-all-done = f32[16,4,8,128]{3,1,2,0:T(4,128)S(1)} async-done(((f32[16,4,8,128]{3,1,2,0:T(4,128)}), f32[16,4,8,128]{3,1,2,0:T(4,128)S(1)}, u32[]{:S(2)}, u32[]{:S(2)}) %all-to-all-start) | async-done | bytes 262176 | tf_op jit(solution)/shard_map/all_to_all | solution.py:219
  36.2 5.1 %collective-permute-start.7 = (f32[16,4,8,128]{3,2,1,0:T(8,128)S(1)}, f32[16,4,8,128]{3,2,1,0:T(8,128)S(1)}, u32[]{:S(2)}, u32[]{:S(2)}) collective-permute-start(f32[16,4,8,128]{3,2,1,0:T(8,128)S(1)} %bitcast.50), channel_id=1, source_target_pairs={{0,4},{1,5},{2,6},{3,7},{4,0},{5,1},{6,2},{7,3},{8,12},{9,13},{10,... | collective-permute-start | bytes 786440 | tf_op jit(solution)/shard_map/ppermute | solution.py:203
  41.3 4.8 %collective-permute-done.7 = f32[16,4,8,128]{3,2,1,0:T(8,128)S(1)} collective-permute-done((f32[16,4,8,128]{3,2,1,0:T(8,128)S(1)}, f32[16,4,8,128]{3,2,1,0:T(8,128)S(1)}, u32[]{:S(2)}, u32[]{:S(2)}) %collective-permute-start.7) | collective-permute-done | bytes 262176 | tf_op jit(solution)/shard_map/ppermute | solution.py:203
  46.9 7.4 %all-to-all-start.1 = ((f32[16,4,8,128]{3,2,1,0:T(8,128)}), f32[16,4,8,128]{3,2,1,0:T(8,128)S(1)}, u32[]{:S(2)}, u32[]{:S(2)}) async-start(f32[16,4,8,128]{3,2,1,0:T(8,128)} %bitcast_add_fusion), calls=%async_computation.1 | async-start | bytes 524288 | tf_op jit(solution)/shard_map/all_to_all | solution.py:230
  55.3 4.7 %collective-permute-start.5 = (f32[256,512]{1,0:T(8,128)}, f32[256,512]{1,0:T(8,128)S(1)}, u32[]{:S(2)}, u32[]{:S(2)}) collective-permute-start(f32[256,512]{1,0:T(8,128)} %get-tuple-element.22), channel_id=1, source_target_pairs={{0,6},{1,7},{2,0},{3,1},{4,2},{5,3},{6,4},{7,5},{8,14},{9,15},{10,... | collective-permute-start | bytes 1572872 | tf_op jit(solution)/shard_map/ppermute | solution.py:203
  60.0 1.9 collective-permute-start.4
  61.9 2.1 collective-permute-start
  64.1 3.7 %collective-permute-start.1 = (f32[4,256,256]{2,1,0:T(8,128)S(1)}, f32[4,256,256]{2,1,0:T(8,128)}, u32[]{:S(2)}, u32[]{:S(2)}) collective-permute-start(f32[4,256,256]{2,1,0:T(8,128)S(1)} %copy-done.2), channel_id=1, source_target_pairs={{0,384},{1,385},{2,386},{3,387},{4,388},{5,389},{6,390},{7,391},{8... | collective-permute-start | bytes 3145736 | tf_op jit(solution)/shard_map/ppermute | solution.py:203
  67.8 3.1 %collective-permute-start.2 = (f32[4,256,256]{2,1,0:T(8,128)S(1)}, f32[4,256,256]{2,1,0:T(8,128)}, u32[]{:S(2)}, u32[]{:S(2)}) collective-permute-start(f32[4,256,256]{2,1,0:T(8,128)S(1)} %copy-done.2), channel_id=1, source_target_pairs={{0,256},{1,257},{2,258},{3,259},{4,260},{5,261},{6,262},{7,263},{8... | collective-permute-start | bytes 3145736 | tf_op jit(solution)/shard_map/ppermute | solution.py:203
  72.1 3.4 %collective-permute-start.8 = (f32[4,128,128]{2,1,0:T(8,128)S(1)}, f32[4,128,128]{2,1,0:T(8,128)S(1)}, u32[]{:S(2)}, u32[]{:S(2)}) collective-permute-start(f32[4,128,128]{2,1,0:T(8,128)S(1)} %copy_bitcast_fusion), channel_id=1, source_target_pairs={{0,2},{1,3},{2,0},{3,1},{4,6},{5,7},{6,4},{7,5},{8,10},{9,11},{10,... | collective-permute-start | bytes 786440 | tf_op jit(solution)/shard_map/ppermute | solution.py:203
  75.5 1.9 collective-permute-start.3
  81.0 1.9 collective-permute-start.6
  84.0 6.0 %collective-permute-done.refs_1_ = f32[4,256,256]{2,1,0:T(8,128)} collective-permute-done((f32[4,256,256]{2,1,0:T(8,128)S(1)}, f32[4,256,256]{2,1,0:T(8,128)}, u32[]{:S(2)}, u32[]{:S(2)}) %collective-permute-start) | collective-permute-done | bytes 1048608 | tf_op jit(solution)/shard_map/ppermute | solution.py:203
  90.0 2.2 collective-permute-start.9
  92.2 18.4 %collective-permute-done.1.refs_2_ = f32[4,256,256]{2,1,0:T(8,128)} collective-permute-done((f32[4,256,256]{2,1,0:T(8,128)S(1)}, f32[4,256,256]{2,1,0:T(8,128)}, u32[]{:S(2)}, u32[]{:S(2)}) %collective-permute-start.1) | collective-permute-done | bytes 1048608 | tf_op jit(solution)/shard_map/ppermute | solution.py:203
  112.5 3.1 %collective-permute-done.2.refs_3_ = f32[4,256,256]{2,1,0:T(8,128)} collective-permute-done((f32[4,256,256]{2,1,0:T(8,128)S(1)}, f32[4,256,256]{2,1,0:T(8,128)}, u32[]{:S(2)}, u32[]{:S(2)}) %collective-permute-start.2) | collective-permute-done | bytes 1048608 | tf_op jit(solution)/shard_map/ppermute | solution.py:203
  115.6 4.2 %collective-permute-start.11 = (f32[2,4,128,128]{3,2,1,0:T(8,128)S(1)}, f32[2,4,128,128]{3,2,1,0:T(8,128)S(1)}, u32[]{:S(2)}, u32[]{:S(2)}) collective-permute-start(f32[2,4,128,128]{3,2,1,0:T(8,128)S(1)} %pad_maximum_fusion.1.refs_2_), channel_id=1, source_target_pairs={{0,256},{1,257},{2,258},{3,259},{4,260},{5,261},{6,262},{7,263},{8... | collective-permute-start | bytes 1572872 | tf_op jit(solution)/shard_map/ppermute | solution.py:203
  119.9 1.9 collective-permute-start.12
  125.5 9.8 %collective-permute-done.10.refs_4_ = f32[2,4,128,128]{3,2,1,0:T(8,128)S(1)} collective-permute-done((f32[2,4,128,128]{3,2,1,0:T(8,128)S(1)}, f32[2,4,128,128]{3,2,1,0:T(8,128)S(1)}, u32[]{:S(2)}, u32[]{:S(2)}) %collective-permute-start.10) | collective-permute-done | bytes 524320 | tf_op jit(solution)/shard_map/ppermute | solution.py:203
  137.3 2.4 collective-permute-start.15
  139.7 11.9 %mix.1 = (bf16[2,4,256,512]{3,2,1,0:T(8,128)(2,1)S(1)}, bf16[2,4,256,512]{3,2,1,0:T(8,128)(2,1)S(1)}) custom-call(f32[4,256,256]{2,1,0:T(8,128)S(1)} %copy-done.2, f32[4,256,256]{2,1,0:T(8,128)} %collective-permute-done.refs_1_, f32[4,256,256]{2,1,0:T(8,128)} %collective-permute-done.1.refs_2_, f32[4,256,256]{2,1,0:T(8,128)} %collective-permute-done.2.refs_3_, ...), custom_call_target="tpu_custom_call" | custom-call | flops 6442450944 | bytes 16777216 | tf_op jit(solution)/shard_map/mix/pallas_call | solution.py:66
  151.7 3.2 %respond_far.1 = (f32[128,512]{1,0:T(8,128)S(1)}, f32[128,512]{1,0:T(8,128)S(1)}, bf16[4,512,512]{2,1,0:T(8,128)(2,1)S(1)}, bf16[4,512,512]{2,1,0:T(8,128)(2,1)S(1)}) custom-call(bf16[2,4,256,512]{3,2,1,0:T(8,128)(2,1)S(1)} %get-tuple-element.13.refs_0_.mh, bf16[2,4,256,512]{3,2,1,0:T(8,128)(2,1)S(1)} %get-tuple-element.14.refs_1_.ml, ...), custom_call_target="tpu_custom_call" | custom-call | flops 1610612736 | bytes 8388608 | tf_op jit(solution)/shard_map/respond_far/pallas_call | solution.py:145
  154.9 3.9 %collective-permute-start.17 = (f32[128,512]{1,0:T(8,128)S(1)}, f32[128,512]{1,0:T(8,128)S(1)}, u32[]{:S(2)}, u32[]{:S(2)}) collective-permute-start(f32[128,512]{1,0:T(8,128)S(1)} %get-tuple-element.19), channel_id=1, source_target_pairs={{0,4},{1,5},{2,6},{3,7},{4,0},{5,1},{6,2},{7,3},{8,12},{9,13},{10,... | collective-permute-start | bytes 786440 | tf_op jit(solution)/shard_map/ppermute | solution.py:203
  158.8 4.5 %collective-permute-start.18 = (f32[128,512]{1,0:T(8,128)S(1)}, f32[128,512]{1,0:T(8,128)S(1)}, u32[]{:S(2)}, u32[]{:S(2)}) collective-permute-start(f32[128,512]{1,0:T(8,128)S(1)} %get-tuple-element.20), channel_id=1, source_target_pairs={{0,12},{1,13},{2,14},{3,15},{4,8},{5,9},{6,10},{7,11},{8,4},{9,5},... | collective-permute-start | bytes 786440 | tf_op jit(solution)/shard_map/ppermute | solution.py:203
  163.4 2.3 respond_near.1
  165.7 2.3 collective-permute-start.16
  168.0 4.2 %collective-permute-done.17 = f32[128,512]{1,0:T(8,128)S(1)} collective-permute-done((f32[128,512]{1,0:T(8,128)S(1)}, f32[128,512]{1,0:T(8,128)S(1)}, u32[]{:S(2)}, u32[]{:S(2)}) %collective-permute-start.17) | collective-permute-done | bytes 262176 | tf_op jit(solution)/shard_map/ppermute | solution.py:203
  172.2 3.1 %collective-permute-done.16 = f32[128,512]{1,0:T(8,128)S(1)} collective-permute-done((f32[128,512]{1,0:T(8,128)S(1)}, f32[128,512]{1,0:T(8,128)S(1)}, u32[]{:S(2)}, u32[]{:S(2)}) %collective-permute-start.16) | collective-permute-done | bytes 262176 | tf_op jit(solution)/shard_map/ppermute | solution.py:203
  175.4 31.5 %all_to_all.25 = f32[8,16,512]{2,1,0:T(8,128)S(1)} all-to-all(f32[8,16,512]{2,1,0:T(8,128)S(1)} %bitcast.45), channel_id=1, replica_groups={{0,16,32,48,64,80,96,112},{4,20,36,52,68,84,100,116},{8,24,40,56,72,88,..., dimensions={0} | all-to-all | bytes 524288 | tf_op jit(solution)/shard_map/all_to_all | solution.py:248
  206.9 22.1 %all_to_all.26 = f32[8,16,512]{2,1,0:T(8,128)S(1)} all-to-all(f32[8,16,512]{2,1,0:T(8,128)S(1)} %broadcast_in_dim.6), channel_id=1, replica_groups={{0,16,32,48,64,80,96,112},{4,20,36,52,68,84,100,116},{8,24,40,56,72,88,..., dimensions={0} | all-to-all | bytes 524288 | tf_op jit(solution)/shard_map/all_to_all | solution.py:248
  229.1 16.7 %all_to_all.27 = f32[4,128,512]{2,1,0:T(8,128)S(1)} all-to-all(f32[4,128,512]{2,1,0:T(8,128)S(1)} %broadcast_in_dim.7), channel_id=1, replica_groups={{0,4,8,12},{16,20,24,28},{32,36,40,44},{48,52,56,60},{64,68,72,76},{80,..., dimensions={0} | all-to-all | bytes 2097152 | tf_op jit(solution)/shard_map/all_to_all | solution.py:248
  (49 shorter events, 19.3 us)
Async XLA Ops:
  0.0 17.1 %copy-start = (f32[128,128]{1,0:T(8,128)S(1)}, f32[128,128]{1,0:T(8,128)}, u32[]{:S(2)}) copy-start(f32[128,128]{1,0:T(8,128)} %param.6) | copy-start | bytes 196612
  1.9 33.6 %all-to-all-start = ((f32[16,4,8,128]{3,1,2,0:T(4,128)}), f32[16,4,8,128]{3,1,2,0:T(4,128)S(1)}, u32[]{:S(2)}, u32[]{:S(2)}) async-start(f32[16,4,8,128]{3,1,2,0:T(4,128)} %bitcast.8), calls=%async_computation | async-start | bytes 524288 | tf_op jit(solution)/shard_map/all_to_all | solution.py:219
  17.5 36.8 %copy-start.1 = (f32[2,256,512]{2,1,0:T(8,128)S(1)}, f32[2,256,512]{2,1,0:T(8,128)}, u32[]{:S(2)}) copy-start(f32[2,256,512]{2,1,0:T(8,128)} %refs_4_.1) | copy-start | bytes 3145732
  36.1 25.8 %copy-start.2 = (f32[4,256,256]{2,1,0:T(8,128)S(1)}, f32[4,256,256]{2,1,0:T(8,128)}, u32[]{:S(2)}) copy-start(f32[4,256,256]{2,1,0:T(8,128)} %refs_0_.1) | copy-start | bytes 3145732
  36.2 9.9 %collective-permute-start.7 = (f32[16,4,8,128]{3,2,1,0:T(8,128)S(1)}, f32[16,4,8,128]{3,2,1,0:T(8,128)S(1)}, u32[]{:S(2)}, u32[]{:S(2)}) collective-permute-start(f32[16,4,8,128]{3,2,1,0:T(8,128)S(1)} %bitcast.50), channel_id=1, source_target_pairs={{0,4},{1,5},{2,6},{3,7},{4,0},{5,1},{6,2},{7,3},{8,12},{9,13},{10,... | collective-permute-start | bytes 786440 | tf_op jit(solution)/shard_map/ppermute | solution.py:203
  46.9 25.1 %all-to-all-start.1 = ((f32[16,4,8,128]{3,2,1,0:T(8,128)}), f32[16,4,8,128]{3,2,1,0:T(8,128)S(1)}, u32[]{:S(2)}, u32[]{:S(2)}) async-start(f32[16,4,8,128]{3,2,1,0:T(8,128)} %bitcast_add_fusion), calls=%async_computation.1 | async-start | bytes 524288 | tf_op jit(solution)/shard_map/all_to_all | solution.py:230
  55.3 16.7 %collective-permute-start.5 = (f32[256,512]{1,0:T(8,128)}, f32[256,512]{1,0:T(8,128)S(1)}, u32[]{:S(2)}, u32[]{:S(2)}) collective-permute-start(f32[256,512]{1,0:T(8,128)} %get-tuple-element.22), channel_id=1, source_target_pairs={{0,6},{1,7},{2,0},{3,1},{4,2},{5,3},{6,4},{7,5},{8,14},{9,15},{10,... | collective-permute-start | bytes 1572872 | tf_op jit(solution)/shard_map/ppermute | solution.py:203
  60.0 15.5 %collective-permute-start.4 = (f32[256,512]{1,0:T(8,128)}, f32[256,512]{1,0:T(8,128)S(1)}, u32[]{:S(2)}, u32[]{:S(2)}) collective-permute-start(f32[256,512]{1,0:T(8,128)} %get-tuple-element.21), channel_id=1, source_target_pairs={{0,2},{1,3},{2,4},{3,5},{4,6},{5,7},{6,0},{7,1},{8,10},{9,11},{10,... | collective-permute-start | bytes 1572872 | tf_op jit(solution)/shard_map/ppermute | solution.py:203
  61.9 28.0 %collective-permute-start = (f32[4,256,256]{2,1,0:T(8,128)S(1)}, f32[4,256,256]{2,1,0:T(8,128)}, u32[]{:S(2)}, u32[]{:S(2)}) collective-permute-start(f32[4,256,256]{2,1,0:T(8,128)S(1)} %copy-done.2), channel_id=1, source_target_pairs={{0,128},{1,129},{2,130},{3,131},{4,132},{5,133},{6,134},{7,135},{8... | collective-permute-start | bytes 3145736 | tf_op jit(solution)/shard_map/ppermute | solution.py:203
  64.1 46.6 %collective-permute-start.1 = (f32[4,256,256]{2,1,0:T(8,128)S(1)}, f32[4,256,256]{2,1,0:T(8,128)}, u32[]{:S(2)}, u32[]{:S(2)}) collective-permute-start(f32[4,256,256]{2,1,0:T(8,128)S(1)} %copy-done.2), channel_id=1, source_target_pairs={{0,384},{1,385},{2,386},{3,387},{4,388},{5,389},{6,390},{7,391},{8... | collective-permute-start | bytes 3145736 | tf_op jit(solution)/shard_map/ppermute | solution.py:203
  67.8 47.8 %collective-permute-start.2 = (f32[4,256,256]{2,1,0:T(8,128)S(1)}, f32[4,256,256]{2,1,0:T(8,128)}, u32[]{:S(2)}, u32[]{:S(2)}) collective-permute-start(f32[4,256,256]{2,1,0:T(8,128)S(1)} %copy-done.2), channel_id=1, source_target_pairs={{0,256},{1,257},{2,258},{3,259},{4,260},{5,261},{6,262},{7,263},{8... | collective-permute-start | bytes 3145736 | tf_op jit(solution)/shard_map/ppermute | solution.py:203
  72.1 5.4 %copy-start.3 = (f32[256,512]{1,0:T(8,128)}, f32[256,512]{1,0:T(8,128)S(1)}, u32[]{:S(2)}) copy-start(f32[256,512]{1,0:T(8,128)S(1)} %collective-permute-done.5) | copy-start | bytes 1572868
  72.1 8.3 %collective-permute-start.8 = (f32[4,128,128]{2,1,0:T(8,128)S(1)}, f32[4,128,128]{2,1,0:T(8,128)S(1)}, u32[]{:S(2)}, u32[]{:S(2)}) collective-permute-start(f32[4,128,128]{2,1,0:T(8,128)S(1)} %copy_bitcast_fusion), channel_id=1, source_target_pairs={{0,2},{1,3},{2,0},{3,1},{4,6},{5,7},{6,4},{7,5},{8,10},{9,11},{10,... | collective-permute-start | bytes 786440 | tf_op jit(solution)/shard_map/ppermute | solution.py:203
  75.5 1.9 copy-start.4
  75.5 44.3 %collective-permute-start.3 = (f32[2,256,512]{2,1,0:T(8,128)S(1)}, f32[2,256,512]{2,1,0:T(8,128)}, u32[]{:S(2)}, u32[]{:S(2)}) collective-permute-start(f32[2,256,512]{2,1,0:T(8,128)S(1)} %copy-done.1), channel_id=1, source_target_pairs={{0,1},{1,0},{2,3},{3,2},{4,5},{5,4},{6,7},{7,6},{8,9},{9,8},{10,11... | collective-permute-start | bytes 3145736 | tf_op jit(solution)/shard_map/ppermute | solution.py:203
  80.3 0.7 copy-start.5
  81.0 58.6 %collective-permute-start.6 = (f32[2,256,512]{2,1,0:T(8,128)S(1)}, f32[2,256,512]{2,1,0:T(8,128)}, u32[]{:S(2)}, u32[]{:S(2)}) collective-permute-start(f32[2,256,512]{2,1,0:T(8,128)S(1)} %pad_maximum_fusion.refs_6_), channel_id=1, source_target_pairs={{0,1},{1,0},{2,3},{3,2},{4,5},{5,4},{6,7},{7,6},{8,9},{9,8},{10,11... | collective-permute-start | bytes 3145736 | tf_op jit(solution)/shard_map/ppermute | solution.py:203
  90.0 33.6 %collective-permute-start.9 = (f32[2,4,128,128]{3,2,1,0:T(8,128)S(1)}, f32[2,4,128,128]{3,2,1,0:T(8,128)S(1)}, u32[]{:S(2)}, u32[]{:S(2)}) collective-permute-start(f32[2,4,128,128]{3,2,1,0:T(8,128)S(1)} %pad_maximum_fusion.1.refs_2_), channel_id=1, source_target_pairs={{0,128},{1,129},{2,130},{3,131},{4,132},{5,133},{6,134},{7,135},{8... | collective-permute-start | bytes 1572872 | tf_op jit(solution)/shard_map/ppermute | solution.py:203
  110.6 24.7 %collective-permute-start.10 = (f32[2,4,128,128]{3,2,1,0:T(8,128)S(1)}, f32[2,4,128,128]{3,2,1,0:T(8,128)S(1)}, u32[]{:S(2)}, u32[]{:S(2)}) collective-permute-start(f32[2,4,128,128]{3,2,1,0:T(8,128)S(1)} %pad_maximum_fusion.1.refs_2_), channel_id=1, source_target_pairs={{0,384},{1,385},{2,386},{3,387},{4,388},{5,389},{6,390},{7,391},{8... | collective-permute-start | bytes 1572872 | tf_op jit(solution)/shard_map/ppermute | solution.py:203
  115.6 21.6 %collective-permute-start.11 = (f32[2,4,128,128]{3,2,1,0:T(8,128)S(1)}, f32[2,4,128,128]{3,2,1,0:T(8,128)S(1)}, u32[]{:S(2)}, u32[]{:S(2)}) collective-permute-start(f32[2,4,128,128]{3,2,1,0:T(8,128)S(1)} %pad_maximum_fusion.1.refs_2_), channel_id=1, source_target_pairs={{0,256},{1,257},{2,258},{3,259},{4,260},{5,261},{6,262},{7,263},{8... | collective-permute-start | bytes 1572872 | tf_op jit(solution)/shard_map/ppermute | solution.py:203
  119.9 31.8 %collective-permute-start.12 = (f32[2,4,128,128]{3,2,1,0:T(8,128)S(1)}, f32[2,4,128,128]{3,2,1,0:T(8,128)S(1)}, u32[]{:S(2)}, u32[]{:S(2)}) collective-permute-start(f32[2,4,128,128]{3,2,1,0:T(8,128)S(1)} %pad_maximum_fusion.1.refs_2_), channel_id=1, source_target_pairs={{0,1},{1,0},{2,3},{3,2},{4,5},{5,4},{6,7},{7,6},{8,9},{9,8},{10,11... | collective-permute-start | bytes 1572872 | tf_op jit(solution)/shard_map/ppermute | solution.py:203
  123.6 28.0 %collective-permute-start.13 = (f32[2,4,128,128]{3,2,1,0:T(8,128)S(1)}, f32[2,4,128,128]{3,2,1,0:T(8,128)S(1)}, u32[]{:S(2)}, u32[]{:S(2)}) collective-permute-start(f32[2,4,128,128]{3,2,1,0:T(8,128)S(1)} %collective-permute-done.9.refs_3_), channel_id=1, source_target_pairs={{0,1},{1,0},{2,3},{3,2},{4,5},{5,4},{6,7},{7,6},{8,9},{9,8},{10,11... | collective-permute-start | bytes 1572872 | tf_op jit(solution)/shard_map/ppermute | solution.py:203
  135.3 16.3 %collective-permute-start.14 = (f32[2,4,128,128]{3,2,1,0:T(8,128)S(1)}, f32[2,4,128,128]{3,2,1,0:T(8,128)S(1)}, u32[]{:S(2)}, u32[]{:S(2)}) collective-permute-start(f32[2,4,128,128]{3,2,1,0:T(8,128)S(1)} %collective-permute-done.10.refs_4_), channel_id=1, source_target_pairs={{0,1},{1,0},{2,3},{3,2},{4,5},{5,4},{6,7},{7,6},{8,9},{9,8},{10,11... | collective-permute-start | bytes 1572872 | tf_op jit(solution)/shard_map/ppermute | solution.py:203
  137.3 14.4 %collective-permute-start.15 = (f32[2,4,128,128]{3,2,1,0:T(8,128)S(1)}, f32[2,4,128,128]{3,2,1,0:T(8,128)S(1)}, u32[]{:S(2)}, u32[]{:S(2)}) collective-permute-start(f32[2,4,128,128]{3,2,1,0:T(8,128)S(1)} %collective-permute-done.11.refs_5_), channel_id=1, source_target_pairs={{0,1},{1,0},{2,3},{3,2},{4,5},{5,4},{6,7},{7,6},{8,9},{9,8},{10,11... | collective-permute-start | bytes 1572872 | tf_op jit(solution)/shard_map/ppermute | solution.py:203
  154.9 17.2 %collective-permute-start.17 = (f32[128,512]{1,0:T(8,128)S(1)}, f32[128,512]{1,0:T(8,128)S(1)}, u32[]{:S(2)}, u32[]{:S(2)}) collective-permute-start(f32[128,512]{1,0:T(8,128)S(1)} %get-tuple-element.19), channel_id=1, source_target_pairs={{0,4},{1,5},{2,6},{3,7},{4,0},{5,1},{6,2},{7,3},{8,12},{9,13},{10,... | collective-permute-start | bytes 786440 | tf_op jit(solution)/shard_map/ppermute | solution.py:203
  158.8 13.3 %collective-permute-start.18 = (f32[128,512]{1,0:T(8,128)S(1)}, f32[128,512]{1,0:T(8,128)S(1)}, u32[]{:S(2)}, u32[]{:S(2)}) collective-permute-start(f32[128,512]{1,0:T(8,128)S(1)} %get-tuple-element.20), channel_id=1, source_target_pairs={{0,12},{1,13},{2,14},{3,15},{4,8},{5,9},{6,10},{7,11},{8,4},{9,5},... | collective-permute-start | bytes 786440 | tf_op jit(solution)/shard_map/ppermute | solution.py:203
  165.7 9.6 %collective-permute-start.16 = (f32[128,512]{1,0:T(8,128)S(1)}, f32[128,512]{1,0:T(8,128)S(1)}, u32[]{:S(2)}, u32[]{:S(2)}) collective-permute-start(f32[128,512]{1,0:T(8,128)S(1)} %get-tuple-element.18), channel_id=1, source_target_pairs={{0,8},{1,9},{2,10},{3,11},{4,12},{5,13},{6,14},{7,15},{8,0},{9,1},... | collective-permute-start | bytes 786440 | tf_op jit(solution)/shard_map/ppermute | solution.py:203

commit v6 on v4

v6 whole, which is shorter than its diff:
```python
import functools

import jax
import jax.numpy as jnp
from jax import lax
from jax.experimental import pallas as pl
from jax.experimental.pallas import tpu as pltpu
from jax.sharding import PartitionSpec as P


AXES = ("state", "aux", "cond")
SHIFTS = (0, 1, -1, 2)
highest = lax.Precision.HIGHEST
f32, bf16 = jnp.float32, jnp.bfloat16


def split(value):
    upper = value.astype(bf16)
    return upper, (value - upper.astype(f32)).astype(bf16)


def dot3(a, b):
    (ah, al), (bh, bl) = a, b
    dot = lambda x, y: jnp.dot(x, y, preferred_element_type=f32)
    return dot(ah, bh) + (dot(ah, bl) + dot(al, bh))


any_spec = pl.BlockSpec(memory_space=pl.ANY)
vmem = pl.BlockSpec(memory_space=pltpu.VMEM)
hbm = pl.BlockSpec(memory_space=pltpu.HBM)


def cost(flops, size):
    return pl.CostEstimate(flops=flops, transcendentals=0, bytes_accessed=size)


def mix_trial(n, pieces, x_all, xh, xl, sems):
    k = lax.axis_index("cond")
    copies = []
    for i in range(4):
        copies.append(pltpu.make_async_copy(pieces[i].at[n], x_all.at[jnp.bitwise_xor(k, i)], sems.at[i]))
    for copy in copies:
        copy.start()
    for copy in copies:
        copy.wait()
    width = x_all.shape[1]

    @pl.loop(0, 4)
    def _(j):
        at = pl.ds(pl.multiple_of(j * width, width), width)
        xh[at, :], xl[at, :] = split(x_all[j])


def mix_first_kernel(*refs):
    slabs, pieces, (m, mh, ml, bh, bl), (b_all, x_all, xh, xl, sems) = refs[:4], refs[4:8], refs[8:13], refs[13:]
    width = slabs[0].shape[2]
    s = lax.axis_index("state")
    copies = []
    for i, shift in enumerate(SHIFTS):
        start = pl.multiple_of(lax.rem(s + 4 - shift, 4) * width, width)
        copies.append(pltpu.make_async_copy(slabs[i], b_all.at[:, :, pl.ds(start, width)], sems.at[4 + i]))
    for copy in copies:
        copy.start()
    mix_trial(0, pieces, x_all, xh, xl, sems)
    for copy in copies:
        copy.wait()

    @pl.loop(0, m.shape[0])
    def _(p):
        bh[p], bl[p] = split(b_all[p])
        whole = dot3((bh[p], bl[p]), (xh[...], xl[...]))
        m[p] = whole
        mh[p], ml[p] = split(whole)


def mix_next_kernel(n, bh, bl, *refs):
    pieces, (m, mh, ml), (x_all, xh, xl, sems) = refs[:4], refs[4:7], refs[7:]
    mix_trial(n, pieces, x_all, xh, xl, sems)

    @pl.loop(0, m.shape[0])
    def _(p):
        whole = dot3((bh[p], bl[p]), (xh[...], xl[...]))
        m[p] = whole
        mh[p], ml[p] = split(whole)


def mix(n, slabs, pieces, b_pair):
    n_p, rows, width = slabs[0].shape
    cols = pieces[0].shape[2]
    shape = (n_p, rows, cols)
    out = [jax.ShapeDtypeStruct(shape, f32)] + [jax.ShapeDtypeStruct(shape, bf16)] * 2
    scratch = [pltpu.VMEM((4, width, cols), f32)] + [pltpu.VMEM((4 * width, cols), bf16)] * 2
    scratch.append(pltpu.SemaphoreType.DMA((8,)))
    kernel, first, specs = functools.partial(mix_next_kernel, n), b_pair, [vmem] * 2
    if b_pair is None:
        kernel, first, specs = mix_first_kernel, slabs, [any_spec] * 4
        out += [jax.ShapeDtypeStruct((n_p, rows, 4 * width), bf16)] * 2
        scratch = [pltpu.VMEM((n_p, rows, 4 * width), f32)] + scratch
    return pl.pallas_call(
        kernel,
        out_shape=tuple(out),
        in_specs=specs + [any_spec] * 4,
        out_specs=(vmem,) * len(out),
        scratch_shapes=scratch,
        compiler_params=pltpu.CompilerParams(vmem_limit_bytes=22 << 20),
        cost_estimate=cost(6 * n_p * rows * 4 * width * cols, 1 << 23),
    )(*first, *pieces)


def halves_kernel(m, mh, ml):
    @pl.loop(0, m.shape[0])
    def _(p):
        mh[p], ml[p] = split(m[p])


def halves(m):
    half = jax.ShapeDtypeStruct(m.shape, bf16)
    return pl.pallas_call(
        halves_kernel,
        name="halves",
        out_shape=(half, half),
        in_specs=[vmem],
        out_specs=(vmem, vmem),
        compiler_params=pltpu.CompilerParams(vmem_limit_bytes=8 << 20),
        cost_estimate=cost(4 * m.size, 8 * m.size),
    )(m)


def bring(sides, h, held, sems):
    rows = held.shape[2]
    at = pl.ds(pl.multiple_of(h * rows, rows), rows)
    copies = [pltpu.make_async_copy(side.at[:, at, :], held.at[i], sems.at[i]) for i, side in enumerate(sides)]
    for copy in copies:
        copy.start()
    return copies


def products(held, p, c_pair):
    upper = jnp.concatenate([held[i, p] for i in range(0, 8, 2)], axis=0)
    lower = jnp.concatenate([held[i, p] for i in range(1, 8, 2)], axis=0)
    return dot3((upper, lower), c_pair)


def deal(total, outs):
    core, place = lax.rem(lax.axis_index("cond"), 2), lax.rem(lax.axis_index("aux"), 4)
    rows = total.shape[0] // 4
    for i, out in enumerate(outs):
        n = jnp.bitwise_xor(lax.div(place, 2), i)
        for side, at in ((0, core), (1, 1 - core)):
            out[at] = total[pl.ds(pl.multiple_of((2 * n + side) * rows, rows), rows), :]


def far_kernel(*refs):
    sides, got, (across, diagonal, ch, cl), (held, c_all, total, sems) = refs[:8], refs[8], refs[9:13], refs[13:]
    _, _, v1, v2 = got.shape
    copies = []
    for i in range(8):
        row, x = divmod(i, 2)
        target = c_all.at[:, pl.ds(row * v1, v1), pl.ds(x * v2, v2)]
        copies.append(pltpu.make_async_copy(got.at[i], target, sems.at[8 + i]))
    for copy in copies:
        copy.start()
    copies += bring(sides, 1 - lax.rem(lax.axis_index("aux"), 2), held, sems)
    total[...] = jnp.zeros_like(total)
    for copy in copies:
        copy.wait()

    @pl.loop(0, c_all.shape[0])
    def _(p):
        ch[p], cl[p] = split(c_all[p])
        total[...] += products(held, p, (ch[p], cl[p]))

    deal(total, (across, diagonal))


def near_kernel(*refs):
    sides, ch, cl, outs, (held, total, sems) = refs[:8], refs[8], refs[9], refs[10:12], refs[12:]
    copies = bring(sides, lax.rem(lax.axis_index("aux"), 2), held, sems)
    total[...] = jnp.zeros_like(total)
    for copy in copies:
        copy.wait()

    @pl.loop(0, ch.shape[0])
    def _(p):
        total[...] += products(held, p, (ch[p], cl[p]))

    deal(total, outs)


def respond_far(sides, got):
    n_p, rows, cols = sides[0].shape
    wide = 2 * got.shape[3]
    part = jax.ShapeDtypeStruct((2, rows // 2, wide), f32)
    full = jax.ShapeDtypeStruct((n_p, cols, wide), bf16)
    return pl.pallas_call(
        far_kernel,
        name="respond_far",
        out_shape=(part, part, full, full),
        in_specs=[hbm] * 8 + [any_spec],
        out_specs=(vmem,) * 4,
        scratch_shapes=[
            pltpu.VMEM((8, n_p, rows // 2, cols), bf16),
            pltpu.VMEM((n_p, cols, wide), f32),
            pltpu.VMEM((2 * rows, wide), f32),
            pltpu.SemaphoreType.DMA((16,)),
        ],
        compiler_params=pltpu.CompilerParams(vmem_limit_bytes=18 << 20),
        cost_estimate=cost(6 * n_p * rows * cols * cols, 1 << 23),
    )(*sides, got)


def respond_near(sides, c_pair):
    n_p, rows, cols = sides[0].shape
    wide = c_pair[0].shape[2]
    part = jax.ShapeDtypeStruct((2, rows // 2, wide), f32)
    return pl.pallas_call(
        near_kernel,
        name="respond_near",
        out_shape=(part, part),
        in_specs=[hbm] * 8 + [vmem] * 2,
        out_specs=(vmem, vmem),
        scratch_shapes=[
            pltpu.VMEM((8, n_p, rows // 2, cols), bf16),
            pltpu.VMEM((2 * rows, wide), f32),
            pltpu.SemaphoreType.DMA((8,)),
        ],
        compiler_params=pltpu.CompilerParams(vmem_limit_bytes=18 << 20),
        cost_estimate=cost(6 * n_p * rows * cols * cols, 1 << 23),
    )(*sides, *c_pair)


def join_kernel(parts, out, sems):
    copies = []
    for i in range(parts.shape[0]):
        t, core = divmod(i, 2)
        for x in range(2):
            v2 = parts.shape[2] // 2
            source = parts.at[i, :, pl.ds(x * v2, v2)]
            target = out.at[t, :, pl.ds((2 * x + core) * v2, v2)]
            copies.append(pltpu.make_async_copy(source, target, sems.at[len(copies)]))
    for copy in copies:
        copy.start()
    for copy in copies:
        copy.wait()


def join(parts):
    n, rows, cols = parts.shape
    return pl.pallas_call(
        join_kernel,
        name="join",
        out_shape=jax.ShapeDtypeStruct((n // 2, rows, 2 * cols), f32),
        in_specs=[any_spec],
        out_specs=any_spec,
        scratch_shapes=[pltpu.SemaphoreType.DMA((2 * n,))],
        compiler_params=pltpu.CompilerParams(vmem_limit_bytes=1 << 20),
        cost_estimate=cost(0, 8 * parts.size),
    )(parts)


def moves(mesh, step):
    n_state, n_aux, n_cond = (mesh.shape[name] for name in AXES)

    def number(y, z, x, core):
        n_z = n_aux // 2
        y, z, x, core = y % n_state, z % n_z, x % 4, core % 2
        return (y * n_aux + z * 2 + x // 2) * n_cond + (x % 2) * 2 + core

    places = [
        (y, z, x, core)
        for y in range(n_state)
        for z in range(n_aux // 2)
        for x in range(4)
        for core in range(2)
    ]
    return [(number(*place), number(*step(*place))) for place in places]


def solution(mesh):
    to_core = moves(mesh, lambda y, z, x, c: (y, z, x, 1 - c))
    to_x = {d: moves(mesh, lambda y, z, x, c, d=d: (y, z, x + d, c)) for d in (1, -1, 2)}
    to_beside = moves(mesh, lambda y, z, x, c: (y, z ^ 1, x, c))
    to_diagonal = moves(mesh, lambda y, z, x, c: (y, z ^ 1, x + 2, c))
    to_y = {d: moves(mesh, lambda y, z, x, c, d=d: (y + d, z, x, c)) for d in (1, -1, 2)}
    n_z = mesh.shape["aux"] // 2
    along_z = [[2 * z + half for z in range(n_z)] for half in range(2)]
    eights = [
        [(4 * g + t) * 4 + 2 * x + core for t in range(4) for core in range(2)] for g in range(n_z // 2) for x in range(2)
    ]
    sheets = [[4 * s + 2 * x + core for s in range(4) for x in range(2)] for core in range(2)]
    along_fours = [[4 * g + t for g in range(n_z // 2)] for t in range(4)]

    def send(value, pairs):
        return lax.ppermute(value, AXES, pairs)

    def per_device(cond_pairs, val_pairs, screened, trials):
        n_p, _, _ = cond_pairs.shape
        half = lax.axis_index("aux") % 2

        slabs = [cond_pairs]
        for d in SHIFTS[1:]:
            slabs.append(send(cond_pairs, to_y[d]))
        far = jnp.stack([send(trials[0], to_x[1]), send(trials[1], to_x[-1])])
        pieces = [trials, send(trials, to_core), far]
        pieces.append(send(far, to_core))

        qb, v1, v2 = val_pairs.shape
        spread = val_pairs.reshape(qb, n_z, v1 // n_z, v2).transpose(1, 0, 2, 3)
        spread = lax.all_to_all(spread, "aux", 0, 0, axis_index_groups=along_z)
        n_q = screened.shape[0]
        q = lax.broadcasted_iota(jnp.int32, (n_q, n_q // 2), 0)
        j = lax.broadcasted_iota(jnp.int32, (n_q, n_q // 2), 1)
        picks = (q == (j // qb) * (2 * qb) + half * qb + j % qb).astype(f32)
        columns = jnp.dot(screened, picks, precision=highest)
        spread = spread.reshape(n_q // 2, v1 // n_z, v2)
        product = jnp.einsum("pq,qrv->prv", columns, spread, precision=highest)
        product = product.reshape(n_z, 2, n_p, v1 // n_z, v2)
        swapped = send(lax.dynamic_index_in_dim(product, 1 - half, 1, keepdims=False), to_x[2])
        block = lax.dynamic_index_in_dim(product, half, 1, keepdims=False) + swapped
        block = lax.all_to_all(block, "aux", 0, 0, axis_index_groups=along_z)
        block = block.transpose(1, 0, 2, 3).reshape(n_p, v1, v2)

        copies = lambda value, count: jnp.broadcast_to(value, (count, *value.shape))
        swap = lambda value, groups, axes="aux": lax.all_to_all(value, axes, 0, 0, axis_index_groups=groups)

        got = swap(copies(block, 8), sheets, ("state", "cond"))

        own, partner, b_pair = [], [], None
        for n in range(trials.shape[0]):
            mixed, upper, lower, *b_new = mix(n, slabs, pieces, b_pair)
            b_pair = b_pair or b_new
            mixed = send(mixed, to_core)
            own, partner = [*own, (upper, lower)], [*partner, halves(mixed)]
        sides = [part for pair in zip(own, partner) for half_pair in pair for part in half_pair]
        sides = [pltpu.with_memory_space_constraint(side, pltpu.HBM) for side in sides]
        across, diagonal, *c_pair = respond_far(sides, got)

        across = send(across, to_x[2])
        diagonal = send(diagonal, to_diagonal)
        here, beside = respond_near(sides, c_pair)
        beside = send(beside, to_beside)
        parts = (here + beside) + (across + diagonal)
        shape = parts.shape
        parts = jnp.sum(swap(parts.reshape(n_z // 2, -1, shape[2]), along_fours), axis=0)
        total = swap(copies(parts, n_z // 2), along_fours).reshape(shape)
        total = swap(copies(total, 4).reshape(8, *shape[1:]), eights, ("aux", "cond"))
        return join(total).reshape(trials.shape)

    in_specs = (P("aux", "cond", "state"), P("aux", "state", "cond"), P(), P("state", "cond", None))
    return jax.shard_map(per_device, mesh=mesh, in_specs=in_specs, out_specs=P("state", "cond", None), check_vma=False)
```

time: 270 us -> 245 us (0.907)
  blocking collectives: 110 us -> 66.5 us
  local copies, waits for them, and re-layouts: 4.1 us -> 14.8 us
  waiting for transfers between devices: 64.2 us -> 55.8 us
  Pallas kernels: 21.6 us -> 29.5 us
  starting transfers between devices: 65.7 us -> 70.9 us
    all_to_all x5 -> x3, blocking collectives: 110 us -> 66.5 us  [per_device(): lax.all_to_all(value, axes, 0, 0, axis_index_groups=groups)]
    all_to_all x0 -> x2, waiting for transfers between devices: none -> 17.5 us  [the longest x1 17.5 us: per_device(): lax.all_to_all(value, axes, 0, 0, axis_index_groups=groups)]
    ppermute x16 -> x13, waiting for transfers between devices: 45.7 us -> 30.7 us  [send(): return lax.ppermute(value, AXES, pairs)]
    all_to_all x0 -> x2, starting transfers between devices: none -> 12.2 us  [the longest x1 7.65 us: per_device(): block = lax.all_to_all(block, 'aux', 0, 0, axis_index_groups=along_z)]
    all_to_all x1, waiting for transfers between devices: 18.4 us -> 7.64 us  [per_device(): spread = lax.all_to_all(spread, 'aux', 0, 0, axis_index_groups=along_z)]
    unnamed x13 -> x27, local copies, waits for them, and re-layouts: 2.29 us -> 9.72 us
    ppermute x16 -> x13, starting transfers between devices: 50.5 us -> 43.5 us  [send(): return lax.ppermute(value, AXES, pairs)]
    pallas_call x2 -> x4, Pallas kernels: 17.6 us -> 24.5 us  [the longest x2 15.1 us: mix(): pl.pallas_call(kernel, out_shape=tuple(out), in_specs=specs + [any_spec]...]
  transfers between devices with their start and end apart: 17 -> 16, of which waited for: 7 -> 5; matrix products, arithmetic and copies ran while one was open for 1% -> 3% of each run, Pallas kernels for 1% -> 10%
where the time goes in v6:
time: 245 us; the launch traced here: 242 us
  starting transfers between devices  70.9 us (29%)
  blocking collectives  66.5 us (27%)
  waiting for transfers between devices  55.8 us (23%)
  Pallas kernels  29.5 us (12%)
  local copies, waits for them, and re-layouts  14.8 us (6%)
    all_to_all x3, blocking collectives, per_device(): lax.all_to_all(value, axes, 0, 0, axis_index_groups=groups)  66.5 us
    ppermute x13, starting transfers between devices, send(): return lax.ppermute(value, AXES, pairs)  43.5 us
    ppermute x13, waiting for transfers between devices, send(): return lax.ppermute(value, AXES, pairs)  30.7 us
    all_to_all x1, waiting for transfers between devices, per_device(): lax.all_to_all(value, axes, 0, 0, axis_index_groups=groups)  17.5 us
    all_to_all x1, starting transfers between devices, per_device(): spread = lax.all_to_all(spread, 'aux', 0, 0, axis_index_groups=along_z)  15.2 us
    pallas_call x2, Pallas kernels, mix(): pl.pallas_call(kernel, out_shape=tuple(out), in_specs=specs + [any_spec]...  15.1 us
    unnamed x27, local copies, waits for them, and re-layouts  9.72 us
    all_to_all x1, starting transfers between devices, per_device(): block = lax.all_to_all(block, 'aux', 0, 0, axis_index_groups=along_z)  7.65 us
  transfers between devices with their start and end apart: 16, of which 5 were waited for; matrix products, arithmetic and copies ran while one was open for 3% of the time, Pallas kernels for 10%

profile of v6, /device:TPU:24, one launch (start us, length us, event | category | flops | bytes accessed | tf_op | source)
XLA Modules:
  0.0 241.5 jit_solution(10988146440489163445)
XLA Ops:
  0.0 1.9 copy.19
  1.9 15.2 %all-to-all-start = ((f32[16,4,8,128]{3,1,2,0:T(4,128)}), f32[16,4,8,128]{3,1,2,0:T(4,128)S(1)}, u32[]{:S(2)}, u32[]{:S(2)}) async-start(f32[16,4,8,128]{3,1,2,0:T(4,128)} %bitcast.8), calls=%async_computation | async-start | bytes 524288 | tf_op jit(solution)/shard_map/all_to_all | solution.py:309
  17.1 2.2 slice_bitcast_fusion.1
  19.3 4.8 %collective-permute-start.5 = (f32[256,512]{1,0:T(8,128)}, f32[256,512]{1,0:T(8,128)S(1)}, u32[]{:S(2)}, u32[]{:S(2)}) collective-permute-start(f32[256,512]{1,0:T(8,128)} %get-tuple-element.42), channel_id=1, source_target_pairs={{0,6},{1,7},{2,0},{3,1},{4,2},{5,3},{6,4},{7,5},{8,14},{9,15},{10,... | collective-permute-start | bytes 1572872 | tf_op jit(solution)/shard_map/ppermute | solution.py:294
  24.1 1.9 collective-permute-start.4
  27.8 7.6 %all-to-all-done = f32[16,4,8,128]{3,1,2,0:T(4,128)S(1)} async-done(((f32[16,4,8,128]{3,1,2,0:T(4,128)}), f32[16,4,8,128]{3,1,2,0:T(4,128)S(1)}, u32[]{:S(2)}, u32[]{:S(2)}) %all-to-all-start) | async-done | bytes 262176 | tf_op jit(solution)/shard_map/all_to_all | solution.py:309
  36.2 4.9 %collective-permute-start.9 = (f32[16,4,8,128]{3,2,1,0:T(8,128)S(1)}, f32[16,4,8,128]{3,2,1,0:T(8,128)S(1)}, u32[]{:S(2)}, u32[]{:S(2)}) collective-permute-start(f32[16,4,8,128]{3,2,1,0:T(8,128)S(1)} %bitcast.41), channel_id=1, source_target_pairs={{0,4},{1,5},{2,6},{3,7},{4,0},{5,1},{6,2},{7,3},{8,12},{9,13},{10,... | collective-permute-start | bytes 786440 | tf_op jit(solution)/shard_map/ppermute | solution.py:294
  41.2 2.1 collective-permute-start
  43.3 3.7 %collective-permute-start.1 = (f32[4,256,256]{2,1,0:T(8,128)S(1)}, f32[4,256,256]{2,1,0:T(8,128)}, u32[]{:S(2)}, u32[]{:S(2)}) collective-permute-start(f32[4,256,256]{2,1,0:T(8,128)S(1)} %copy-done.10), channel_id=1, source_target_pairs={{0,384},{1,385},{2,386},{3,387},{4,388},{5,389},{6,390},{7,391},{8... | collective-permute-start | bytes 3145736 | tf_op jit(solution)/shard_map/ppermute | solution.py:294
  47.1 3.1 %collective-permute-start.2 = (f32[4,256,256]{2,1,0:T(8,128)S(1)}, f32[4,256,256]{2,1,0:T(8,128)}, u32[]{:S(2)}, u32[]{:S(2)}) collective-permute-start(f32[4,256,256]{2,1,0:T(8,128)S(1)} %copy-done.10), channel_id=1, source_target_pairs={{0,256},{1,257},{2,258},{3,259},{4,260},{5,261},{6,262},{7,263},{8... | collective-permute-start | bytes 3145736 | tf_op jit(solution)/shard_map/ppermute | solution.py:294
  50.2 1.9 collective-permute-start.3
  53.5 2.4 collective-permute-start.6
  56.7 7.6 %all-to-all-start.1 = ((f32[16,4,8,128]{3,2,1,0:T(8,128)}), f32[16,4,8,128]{3,2,1,0:T(8,128)S(1)}, u32[]{:S(2)}, u32[]{:S(2)}) async-start(f32[16,4,8,128]{3,2,1,0:T(8,128)} %bitcast_add_fusion), calls=%async_computation.1 | async-start | bytes 524288 | tf_op jit(solution)/shard_map/all_to_all | solution.py:320
  64.3 4.9 %collective-permute-done.refs_1_ = f32[4,256,256]{2,1,0:T(8,128)} collective-permute-done((f32[4,256,256]{2,1,0:T(8,128)S(1)}, f32[4,256,256]{2,1,0:T(8,128)}, u32[]{:S(2)}, u32[]{:S(2)}) %collective-permute-start) | collective-permute-done | bytes 1048608 | tf_op jit(solution)/shard_map/ppermute | solution.py:294
  69.2 19.3 %collective-permute-done.1.refs_2_ = f32[4,256,256]{2,1,0:T(8,128)} collective-permute-done((f32[4,256,256]{2,1,0:T(8,128)S(1)}, f32[4,256,256]{2,1,0:T(8,128)}, u32[]{:S(2)}, u32[]{:S(2)}) %collective-permute-start.1) | collective-permute-done | bytes 1048608 | tf_op jit(solution)/shard_map/ppermute | solution.py:294
  88.5 8.1 %shard_map.46 = (f32[4,256,512]{2,1,0:T(8,128)}, bf16[4,256,512]{2,1,0:T(8,128)(2,1)S(1)}, bf16[4,256,512]{2,1,0:T(8,128)(2,1)S(1)}, bf16[4,256,1024]{2,1,0:T(8,128)(2,1)S(1)}, bf16[4,256,1024]{2,1,0:T(8,128)(2,1)S(1)}) custom-call(f32[4,256,256]{2,1,0:T(8,128)S(1)} %copy-done.10, f32[4,256,256]{2,1,0:T(8,128)} %collective-permute-done.refs_1_, ...), custom_call_target="tpu_custom_call" | custom-call | flops 3221225472 | bytes 8388608 | tf_op jit(solution)/shard_map/pallas_call | solution.py:99
  98.6 1.9 collective-permute-start.7
  100.5 7.0 %shard_map.47 = (f32[4,256,512]{2,1,0:T(8,128)}, bf16[4,256,512]{2,1,0:T(8,128)(2,1)S(1)}, bf16[4,256,512]{2,1,0:T(8,128)(2,1)S(1)}) custom-call(bf16[4,256,1024]{2,1,0:T(8,128)(2,1)S(1)} %get-tuple-element.28.bh, bf16[4,256,1024]{2,1,0:T(8,128)(2,1)S(1)} %get-tuple-element.29.bl, f32[2,256,512]{2,1,0:T(8,128)S(1)} %copy-done.9, ...), custom_call_target="tpu_custom_call" | custom-call | flops 3221225472 | bytes 8388608 | tf_op jit(solution)/shard_map/pallas_call | solution.py:99
  109.5 2.4 collective-permute-start.8
  113.6 4.6 %all-to-all-start.2 = ((f32[8,4,128,128]{3,2,1,0:T(8,128)}), f32[8,4,128,128]{3,2,1,0:T(8,128)S(1)}, u32[]{:S(2)}, u32[]{:S(2)}) async-start(f32[8,4,128,128]{3,2,1,0:T(8,128)} %broadcast_in_dim.9), calls=%async_computation.2 | async-start | bytes 4194304 | tf_op jit(solution)/shard_map/all_to_all | solution.py:324
  118.1 2.0 halves.2
  122.0 2.0 halves.3
  126.0 17.5 %all-to-all-done.2.refs_8_ = f32[8,4,128,128]{3,2,1,0:T(8,128)S(1)} async-done(((f32[8,4,128,128]{3,2,1,0:T(8,128)}), f32[8,4,128,128]{3,2,1,0:T(8,128)S(1)}, u32[]{:S(2)}, u32[]{:S(2)}) %all-to-all-start.2) | async-done | bytes 2097184 | tf_op jit(solution)/shard_map/all_to_all | solution.py:324
  143.5 4.9 %respond_far.1 = (f32[2,128,256]{2,1,0:T(8,128)S(1)}, f32[2,128,256]{2,1,0:T(8,128)S(1)}, bf16[4,512,256]{2,1,0:T(8,128)(2,1)S(1)}, bf16[4,512,256]{2,1,0:T(8,128)(2,1)S(1)}) custom-call(bf16[4,256,512]{2,1,0:T(8,128)(2,1)} %copy-done.1, bf16[4,256,512]{2,1,0:T(8,128)(2,1)} %copy-done.2, bf16[4,256,512]{2,1,0:T(8,128)(2,1)} %copy-done.5, ...), custom_call_target="tpu_custom_call" | custom-call | flops 1610612736 | bytes 8388608 | tf_op jit(solution)/shard_map/respond_far/pallas_call | solution.py:195
  148.4 3.9 %collective-permute-start.11 = (f32[2,128,256]{2,1,0:T(8,128)S(1)}, f32[2,128,256]{2,1,0:T(8,128)S(1)}, u32[]{:S(2)}, u32[]{:S(2)}) collective-permute-start(f32[2,128,256]{2,1,0:T(8,128)S(1)} %get-tuple-element.39), channel_id=1, source_target_pairs={{0,4},{1,5},{2,6},{3,7},{4,0},{5,1},{6,2},{7,3},{8,12},{9,13},{10,... | collective-permute-start | bytes 786440 | tf_op jit(solution)/shard_map/ppermute | solution.py:294
  152.3 8.4 %collective-permute-start.12 = (f32[2,128,256]{2,1,0:T(8,128)S(1)}, f32[2,128,256]{2,1,0:T(8,128)S(1)}, u32[]{:S(2)}, u32[]{:S(2)}) collective-permute-start(f32[2,128,256]{2,1,0:T(8,128)S(1)} %get-tuple-element.40), channel_id=1, source_target_pairs={{0,12},{1,13},{2,14},{3,15},{4,8},{5,9},{6,10},{7,11},{8,4},{9,5},... | collective-permute-start | bytes 786440 | tf_op jit(solution)/shard_map/ppermute | solution.py:294
  160.7 4.6 %respond_near.1 = (f32[2,128,256]{2,1,0:T(8,128)S(1)}, f32[2,128,256]{2,1,0:T(8,128)S(1)}) custom-call(bf16[4,256,512]{2,1,0:T(8,128)(2,1)} %copy-done.1, bf16[4,256,512]{2,1,0:T(8,128)(2,1)} %copy-done.2, bf16[4,256,512]{2,1,0:T(8,128)(2,1)} %copy-done.5, bf16[4,256,512]{2,1,0:T(8,128)(2,1)} %copy-done.6, bf16[4,256,512]{2,1,0:T(8,128)(2,1)} %copy-done.3, ...), custom_call_target="tpu_custom_call" | custom-call | flops 1610612736 | bytes 8388608 | tf_op jit(solution)/shard_map/respond_near/pallas_call | solution.py:216
  165.3 1.9 collective-permute-start.10
  167.2 6.5 %collective-permute-done.10 = f32[2,128,256]{2,1,0:T(8,128)S(1)} collective-permute-done((f32[2,128,256]{2,1,0:T(8,128)S(1)}, f32[2,128,256]{2,1,0:T(8,128)S(1)}, u32[]{:S(2)}, u32[]{:S(2)}) %collective-permute-start.10) | collective-permute-done | bytes 262176 | tf_op jit(solution)/shard_map/ppermute | solution.py:294
  173.8 24.6 %all_to_all.30 = f32[8,32,256]{2,1,0:T(8,128)S(1)} all-to-all(f32[8,32,256]{2,1,0:T(8,128)S(1)} %bitcast.36), channel_id=1, replica_groups={{0,16,32,48,64,80,96,112},{4,20,36,52,68,84,100,116},{8,24,40,56,72,88,..., dimensions={0} | all-to-all | bytes 524288 | tf_op jit(solution)/shard_map/all_to_all | solution.py:324
  198.4 22.7 %all_to_all.31 = f32[8,32,256]{2,1,0:T(8,128)S(1)} all-to-all(f32[8,32,256]{2,1,0:T(8,128)S(1)} %broadcast_in_dim.10), channel_id=1, replica_groups={{0,16,32,48,64,80,96,112},{4,20,36,52,68,84,100,116},{8,24,40,56,72,88,..., dimensions={0} | all-to-all | bytes 524288 | tf_op jit(solution)/shard_map/all_to_all | solution.py:324
  221.2 19.2 %all_to_all.32.parts = f32[8,128,256]{2,1,0:T(8,128)S(1)} all-to-all(f32[8,128,256]{2,1,0:T(8,128)S(1)} %bitcast.35), channel_id=1, replica_groups={{0,1,4,5,8,9,12,13},{2,3,6,7,10,11,14,15},{16,17,20,21,24,25,28,29},{18..., dimensions={0} | all-to-all | bytes 2097152 | tf_op jit(solution)/shard_map/all_to_all | solution.py:324
  (55 shorter events, 15.3 us)
Async XLA Ops:
  0.0 26.1 %copy-start = (f32[128,128]{1,0:T(8,128)S(1)}, f32[128,128]{1,0:T(8,128)}, u32[]{:S(2)}) copy-start(f32[128,128]{1,0:T(8,128)} %param.6) | copy-start | bytes 196612
  1.9 33.6 %all-to-all-start = ((f32[16,4,8,128]{3,1,2,0:T(4,128)}), f32[16,4,8,128]{3,1,2,0:T(4,128)S(1)}, u32[]{:S(2)}, u32[]{:S(2)}) async-start(f32[16,4,8,128]{3,1,2,0:T(4,128)} %bitcast.8), calls=%async_computation | async-start | bytes 524288 | tf_op jit(solution)/shard_map/all_to_all | solution.py:309
  19.3 21.8 %copy-start.10 = (f32[4,256,256]{2,1,0:T(8,128)S(1)}, f32[4,256,256]{2,1,0:T(8,128)}, u32[]{:S(2)}) copy-start(f32[4,256,256]{2,1,0:T(8,128)} %refs_0_.2) | copy-start | bytes 3145732
  19.3 30.9 %copy-start.9 = (f32[2,256,512]{2,1,0:T(8,128)S(1)}, f32[2,256,512]{2,1,0:T(8,128)}, u32[]{:S(2)}) copy-start(f32[2,256,512]{2,1,0:T(8,128)} %refs_0_.3) | copy-start | bytes 3145732
  19.3 27.7 %collective-permute-start.5 = (f32[256,512]{1,0:T(8,128)}, f32[256,512]{1,0:T(8,128)S(1)}, u32[]{:S(2)}, u32[]{:S(2)}) collective-permute-start(f32[256,512]{1,0:T(8,128)} %get-tuple-element.42), channel_id=1, source_target_pairs={{0,6},{1,7},{2,0},{3,1},{4,2},{5,3},{6,4},{7,5},{8,14},{9,15},{10,... | collective-permute-start | bytes 1572872 | tf_op jit(solution)/shard_map/ppermute | solution.py:294
  24.1 26.1 %collective-permute-start.4 = (f32[256,512]{1,0:T(8,128)}, f32[256,512]{1,0:T(8,128)S(1)}, u32[]{:S(2)}, u32[]{:S(2)}) collective-permute-start(f32[256,512]{1,0:T(8,128)} %get-tuple-element.41), channel_id=1, source_target_pairs={{0,2},{1,3},{2,4},{3,5},{4,6},{5,7},{6,0},{7,1},{8,10},{9,11},{10,... | collective-permute-start | bytes 1572872 | tf_op jit(solution)/shard_map/ppermute | solution.py:294
  36.2 17.2 %collective-permute-start.9 = (f32[16,4,8,128]{3,2,1,0:T(8,128)S(1)}, f32[16,4,8,128]{3,2,1,0:T(8,128)S(1)}, u32[]{:S(2)}, u32[]{:S(2)}) collective-permute-start(f32[16,4,8,128]{3,2,1,0:T(8,128)S(1)} %bitcast.41), channel_id=1, source_target_pairs={{0,4},{1,5},{2,6},{3,7},{4,0},{5,1},{6,2},{7,3},{8,12},{9,13},{10,... | collective-permute-start | bytes 786440 | tf_op jit(solution)/shard_map/ppermute | solution.py:294
  41.2 28.0 %collective-permute-start = (f32[4,256,256]{2,1,0:T(8,128)S(1)}, f32[4,256,256]{2,1,0:T(8,128)}, u32[]{:S(2)}, u32[]{:S(2)}) collective-permute-start(f32[4,256,256]{2,1,0:T(8,128)S(1)} %copy-done.10), channel_id=1, source_target_pairs={{0,128},{1,129},{2,130},{3,131},{4,132},{5,133},{6,134},{7,135},{8... | collective-permute-start | bytes 3145736 | tf_op jit(solution)/shard_map/ppermute | solution.py:294
  43.3 45.2 %collective-permute-start.1 = (f32[4,256,256]{2,1,0:T(8,128)S(1)}, f32[4,256,256]{2,1,0:T(8,128)}, u32[]{:S(2)}, u32[]{:S(2)}) collective-permute-start(f32[4,256,256]{2,1,0:T(8,128)S(1)} %copy-done.10), channel_id=1, source_target_pairs={{0,384},{1,385},{2,386},{3,387},{4,388},{5,389},{6,390},{7,391},{8... | collective-permute-start | bytes 3145736 | tf_op jit(solution)/shard_map/ppermute | solution.py:294
  47.0 5.1 %copy-start.11 = (f32[256,512]{1,0:T(8,128)}, f32[256,512]{1,0:T(8,128)S(1)}, u32[]{:S(2)}) copy-start(f32[256,512]{1,0:T(8,128)S(1)} %collective-permute-done.5) | copy-start | bytes 1572868
  47.1 41.5 %collective-permute-start.2 = (f32[4,256,256]{2,1,0:T(8,128)S(1)}, f32[4,256,256]{2,1,0:T(8,128)}, u32[]{:S(2)}, u32[]{:S(2)}) collective-permute-start(f32[4,256,256]{2,1,0:T(8,128)S(1)} %copy-done.10), channel_id=1, source_target_pairs={{0,256},{1,257},{2,258},{3,259},{4,260},{5,261},{6,262},{7,263},{8... | collective-permute-start | bytes 3145736 | tf_op jit(solution)/shard_map/ppermute | solution.py:294
  50.2 2.0 copy-start.12
  50.2 38.3 %collective-permute-start.3 = (f32[2,256,512]{2,1,0:T(8,128)S(1)}, f32[2,256,512]{2,1,0:T(8,128)}, u32[]{:S(2)}, u32[]{:S(2)}) collective-permute-start(f32[2,256,512]{2,1,0:T(8,128)S(1)} %copy-done.9), channel_id=1, source_target_pairs={{0,1},{1,0},{2,3},{3,2},{4,5},{5,4},{6,7},{7,6},{8,9},{9,8},{10,11... | collective-permute-start | bytes 3145736 | tf_op jit(solution)/shard_map/ppermute | solution.py:294
  53.5 35.1 %collective-permute-start.6 = (f32[2,256,512]{2,1,0:T(8,128)S(1)}, f32[2,256,512]{2,1,0:T(8,128)}, u32[]{:S(2)}, u32[]{:S(2)}) collective-permute-start(f32[2,256,512]{2,1,0:T(8,128)S(1)} %pad_maximum_fusion.refs_6_.refs_2_), channel_id=1, source_target_pairs={{0,1},{1,0},{2,3},{3,2},{4,5},{5,4},{6,7},{7,6},{8,9},{9,8},{10,11... | collective-permute-start | bytes 3145736 | tf_op jit(solution)/shard_map/ppermute | solution.py:294
  56.7 55.2 %all-to-all-start.1 = ((f32[16,4,8,128]{3,2,1,0:T(8,128)}), f32[16,4,8,128]{3,2,1,0:T(8,128)S(1)}, u32[]{:S(2)}, u32[]{:S(2)}) async-start(f32[16,4,8,128]{3,2,1,0:T(8,128)} %bitcast_add_fusion), calls=%async_computation.1 | async-start | bytes 524288 | tf_op jit(solution)/shard_map/all_to_all | solution.py:320
  96.7 1.0 copy-start.1
  97.6 1.0 copy-start.2
  98.6 19.5 %collective-permute-start.7 = (f32[4,256,512]{2,1,0:T(8,128)}, f32[4,256,512]{2,1,0:T(8,128)}, u32[]{:S(2)}, u32[]{:S(2)}) collective-permute-start(f32[4,256,512]{2,1,0:T(8,128)} %get-tuple-element.25), channel_id=1, source_target_pairs={{0,1},{1,0},{2,3},{3,2},{4,5},{5,4},{6,7},{7,6},{8,9},{9,8},{10,11... | collective-permute-start | bytes 6291464 | tf_op jit(solution)/shard_map/ppermute | solution.py:294
  107.5 1.0 copy-start.3
  108.5 1.0 copy-start.4
  109.5 12.6 %collective-permute-start.8 = (f32[4,256,512]{2,1,0:T(8,128)}, f32[4,256,512]{2,1,0:T(8,128)}, u32[]{:S(2)}, u32[]{:S(2)}) collective-permute-start(f32[4,256,512]{2,1,0:T(8,128)} %get-tuple-element.32), channel_id=1, source_target_pairs={{0,1},{1,0},{2,3},{3,2},{4,5},{5,4},{6,7},{7,6},{8,9},{9,8},{10,11... | collective-permute-start | bytes 6291464 | tf_op jit(solution)/shard_map/ppermute | solution.py:294
  113.6 29.9 %all-to-all-start.2 = ((f32[8,4,128,128]{3,2,1,0:T(8,128)}), f32[8,4,128,128]{3,2,1,0:T(8,128)S(1)}, u32[]{:S(2)}, u32[]{:S(2)}) async-start(f32[8,4,128,128]{3,2,1,0:T(8,128)} %broadcast_in_dim.9), calls=%async_computation.2 | async-start | bytes 4194304 | tf_op jit(solution)/shard_map/all_to_all | solution.py:324
  120.1 1.0 copy-start.5
  121.1 1.0 copy-start.6
  124.0 1.0 copy-start.7
  125.0 1.0 copy-start.8
  148.4 18.8 %collective-permute-start.11 = (f32[2,128,256]{2,1,0:T(8,128)S(1)}, f32[2,128,256]{2,1,0:T(8,128)S(1)}, u32[]{:S(2)}, u32[]{:S(2)}) collective-permute-start(f32[2,128,256]{2,1,0:T(8,128)S(1)} %get-tuple-element.39), channel_id=1, source_target_pairs={{0,4},{1,5},{2,6},{3,7},{4,0},{5,1},{6,2},{7,3},{8,12},{9,13},{10,... | collective-permute-start | bytes 786440 | tf_op jit(solution)/shard_map/ppermute | solution.py:294
  152.3 14.9 %collective-permute-start.12 = (f32[2,128,256]{2,1,0:T(8,128)S(1)}, f32[2,128,256]{2,1,0:T(8,128)S(1)}, u32[]{:S(2)}, u32[]{:S(2)}) collective-permute-start(f32[2,128,256]{2,1,0:T(8,128)S(1)} %get-tuple-element.40), channel_id=1, source_target_pairs={{0,12},{1,13},{2,14},{3,15},{4,8},{5,9},{6,10},{7,11},{8,4},{9,5},... | collective-permute-start | bytes 786440 | tf_op jit(solution)/shard_map/ppermute | solution.py:294
  165.3 8.4 %collective-permute-start.10 = (f32[2,128,256]{2,1,0:T(8,128)S(1)}, f32[2,128,256]{2,1,0:T(8,128)S(1)}, u32[]{:S(2)}, u32[]{:S(2)}) collective-permute-start(f32[2,128,256]{2,1,0:T(8,128)S(1)} %get-tuple-element.38), channel_id=1, source_target_pairs={{0,8},{1,9},{2,10},{3,11},{4,12},{5,13},{6,14},{7,15},{8,0},{9,1},... | collective-permute-start | bytes 786440 | tf_op jit(solution)/shard_map/ppermute | solution.py:294

commit v7 on v5

--- a/solution.py
+++ b/solution.py
@@ -24,7 +24,7 @@
 
 
 def mix_kernel(*refs):
-    slabs, pieces, (mh, ml), (b_all, x_all, bh, bl, xh, xl, sems) = refs[:4], refs[4:8], refs[8:10], refs[10:]
+    slabs, pieces, (mh, ml), (b_all, x_all, xh, xl, sems) = refs[:4], refs[4:8], refs[8:10], refs[10:]
     n_p, _, width = slabs[0].shape
     n_n = pieces[0].shape[0]
     s, k = lax.axis_index("state"), lax.axis_index("cond")
@@ -48,13 +48,10 @@
     for copy in copies[:4]:
         copy.wait()
 
-    @pl.loop(0, n_p)
-    def _(p):
-        bh[...], bl[...] = split(b_all[p])
-
-        @pl.loop(0, n_n)
-        def _(n):
-            mh[n, p], ml[n, p] = split(dot3((bh[...], bl[...]), (xh[n], xl[n])))
+    for p in range(n_p):
+        slab = split(b_all[p])
+        for n in range(n_n):
+            mh[n, p], ml[n, p] = split(dot3(slab, (xh[n], xl[n])))
 
 
 def mix(slabs, pieces):
@@ -72,8 +69,6 @@
         scratch_shapes=[
             pltpu.VMEM((n_p, rows, 4 * width), f32),
             pltpu.VMEM((4, n_n, width, cols), f32),
-            pltpu.VMEM((rows, 4 * width), bf16),
-            pltpu.VMEM((rows, 4 * width), bf16),
             pltpu.VMEM((n_n, 4 * width, cols), bf16),
             pltpu.VMEM((n_n, 4 * width, cols), bf16),
             pltpu.SemaphoreType.DMA((8,)),
@@ -91,15 +86,14 @@
 
 
 def add_products(outs, places, mh, ml, p, c_pair):
-    both = [jnp.concatenate([rows_of(m, t, p) for t in places], axis=0) for m in (mh, ml)]
-    part = dot3(both, c_pair)
-    rows = part.shape[0] // 2
-    outs[0][...] += part[:rows]
-    outs[1][...] += part[rows:]
+    part = dot3([jnp.concatenate([rows_of(m, t, p) for t in places], axis=0) for m in (mh, ml)], c_pair)
+    rows = outs[0].shape[0]
+    for i, out in enumerate(outs):
+        out[...] += part[i * rows : (i + 1) * rows]
 
 
 def far_kernel(*refs):
-    mh, ml, bands, mates, (across, diagonal, ch, cl, c_all, sems) = refs[0], refs[1], refs[2:6], refs[6:10], refs[10:]
+    mh, ml, bands, mates, (*outs, ch, cl, c_all, sems) = refs[0], refs[1], refs[2:6], refs[6:10], refs[10:]
     n_x, n_p, v1, v2 = bands[0].shape
     s, core = lax.axis_index("state"), lax.rem(lax.axis_index("cond"), 2)
     place = lax.rem(lax.axis_index("aux"), 4)
@@ -113,27 +107,25 @@
                 copies.append(pltpu.make_async_copy(band.at[x], target, sems.at[len(copies)]))
     for copy in copies:
         copy.start()
-    across[...] = jnp.zeros_like(across)
-    diagonal[...] = jnp.zeros_like(diagonal)
+    for out in outs:
+        out[...] = jnp.zeros_like(out)
     for copy in copies:
         copy.wait()
-    places = [jnp.bitwise_xor(place, 1), jnp.bitwise_xor(place, 3)]
+    places = [jnp.bitwise_xor(place, t) for t in (1, 3, 2)]
 
     @pl.loop(0, n_p)
     def _(p):
         ch[p], cl[p] = split(c_all[p])
-        add_products((across, diagonal), places, mh, ml, p, (ch[p], cl[p]))
-
-
-def near_kernel(mh, ml, ch, cl, beside, here):
+        add_products(outs, places, mh, ml, p, (ch[p], cl[p]))
+
+
+def near_kernel(mh, ml, ch, cl, here):
     place = lax.rem(lax.axis_index("aux"), 4)
-    places = [jnp.bitwise_xor(place, 2), place]
-    beside[...] = jnp.zeros_like(beside)
     here[...] = jnp.zeros_like(here)
 
     @pl.loop(0, mh.shape[1])
     def _(p):
-        add_products((beside, here), places, mh, ml, p, (ch[p], cl[p]))
+        add_products((here,), (place,), mh, ml, p, (ch[p], cl[p]))
 
 
 def respond_far(m_pair, bands, mates):
@@ -145,9 +137,9 @@
     return pl.pallas_call(
         far_kernel,
         name="respond_far",
-        out_shape=(part, part, full, full),
+        out_shape=(part, part, part, full, full),
         in_specs=[vmem] * 2 + [any_spec] * 8,
-        out_specs=(vmem,) * 4,
+        out_specs=(vmem,) * 5,
         scratch_shapes=[pltpu.VMEM((n_p, cols, cols), f32), pltpu.SemaphoreType.DMA((16,))],
         compiler_params=pltpu.CompilerParams(vmem_limit_bytes=28 << 20),
         cost_estimate=pl.CostEstimate(flops=6 * n_p * rows * cols * cols, transcendentals=0, bytes_accessed=1 << 23),
@@ -161,9 +153,9 @@
     return pl.pallas_call(
         near_kernel,
         name="respond_near",
-        out_shape=(part, part),
+        out_shape=part,
         in_specs=[vmem] * 4,
-        out_specs=(vmem, vmem),
+        out_specs=vmem,
         compiler_params=pltpu.CompilerParams(vmem_limit_bytes=28 << 20),
         cost_estimate=pl.CostEstimate(flops=6 * n_p * rows * cols * cols, transcendentals=0, bytes_accessed=1 << 23),
     )(*m_pair, *c_pair)
@@ -238,12 +230,12 @@
         mates = [send(band, to_core) for band in bands]
 
         m_pair = mix(slabs, pieces)
-        across, diagonal, *c_pair = respond_far(m_pair, bands, mates)
+        across, diagonal, beside, *c_pair = respond_far(m_pair, bands, mates)
 
         across = send(across, to_x[2])
         diagonal = send(diagonal, to_diagonal)
-        beside, here = respond_near(m_pair, c_pair)
         beside = send(beside, to_beside)
+        here = respond_near(m_pair, c_pair)
         parts = (here + beside) + (across + diagonal)
         swap = lambda value, groups: lax.all_to_all(value, "aux", 0, 0, axis_index_groups=groups)
         parts = jnp.sum(swap(parts.reshape(n_z // 2, -1, parts.shape[1]), along_fours), axis=0)

time: 250 us -> 249 us (level)
  transfers between devices with their start and end apart: 21 -> 21, of which waited for: 11 -> 12; matrix products, arithmetic and copies ran while one was open for 1% -> 2% of each run, Pallas kernels for 6% -> 5%
where the time goes in v7:
time: 249 us; the launch traced here: 246 us
  starting transfers between devices  77.6 us (31%)
  waiting for transfers between devices  72.7 us (29%)
  blocking collectives  70.1 us (28%)
  Pallas kernels  15.7 us (6%)
  local copies, waits for them, and re-layouts  5.01 us (2%)
  other arithmetic  3.2 us (1%)
    all_to_all x3, blocking collectives, per_device(): lax.all_to_all(value, 'aux', 0, 0, axis_index_groups=groups)  70.1 us
    ppermute x19, starting transfers between devices, send(): return lax.ppermute(value, AXES, pairs)  55 us
    ppermute x19, waiting for transfers between devices, send(): return lax.ppermute(value, AXES, pairs)  53.7 us
    all_to_all x1, waiting for transfers between devices, per_device(): spread = lax.all_to_all(spread, 'aux', 0, 0, axis_index_groups=along_z)  18 us
    all_to_all x1, starting transfers between devices, per_device(): spread = lax.all_to_all(spread, 'aux', 0, 0, axis_index_groups=along_z)  15.2 us
    pallas_call x1, Pallas kernels, mix(): pl.pallas_call(mix_kernel, name='mix', out_shape=(shape, shape), in_specs...  10.2 us
    all_to_all x1, starting transfers between devices, per_device(): block = lax.all_to_all(block, 'aux', 0, 0, axis_index_groups=along_z)  7.39 us
  transfers between devices with their start and end apart: 21, of which 12 were waited for; matrix products, arithmetic and copies ran while one was open for 2% of the time, Pallas kernels for 5%

profile of v7, /device:TPU:24, one launch (start us, length us, event | category | flops | bytes accessed | tf_op | source)
XLA Modules:
  0.0 245.6 jit_solution(3992266913306524551)
XLA Ops:
  1.9 15.2 %all-to-all-start = ((f32[16,4,8,128]{3,1,2,0:T(4,128)}), f32[16,4,8,128]{3,1,2,0:T(4,128)S(1)}, u32[]{:S(2)}, u32[]{:S(2)}) async-start(f32[16,4,8,128]{3,1,2,0:T(4,128)} %bitcast.8), calls=%async_computation | async-start | bytes 524288 | tf_op jit(solution)/shard_map/all_to_all | solution.py:211
  17.5 18.0 %all-to-all-done = f32[16,4,8,128]{3,1,2,0:T(4,128)S(1)} async-done(((f32[16,4,8,128]{3,1,2,0:T(4,128)}), f32[16,4,8,128]{3,1,2,0:T(4,128)S(1)}, u32[]{:S(2)}, u32[]{:S(2)}) %all-to-all-start) | async-done | bytes 262176 | tf_op jit(solution)/shard_map/all_to_all | solution.py:211
  36.2 5.1 %collective-permute-start.7 = (f32[16,4,8,128]{3,2,1,0:T(8,128)S(1)}, f32[16,4,8,128]{3,2,1,0:T(8,128)S(1)}, u32[]{:S(2)}, u32[]{:S(2)}) collective-permute-start(f32[16,4,8,128]{3,2,1,0:T(8,128)S(1)} %bitcast.50), channel_id=1, source_target_pairs={{0,4},{1,5},{2,6},{3,7},{4,0},{5,1},{6,2},{7,3},{8,12},{9,13},{10,... | collective-permute-start | bytes 786440 | tf_op jit(solution)/shard_map/ppermute | solution.py:195
  41.3 4.8 %collective-permute-done.7 = f32[16,4,8,128]{3,2,1,0:T(8,128)S(1)} collective-permute-done((f32[16,4,8,128]{3,2,1,0:T(8,128)S(1)}, f32[16,4,8,128]{3,2,1,0:T(8,128)S(1)}, u32[]{:S(2)}, u32[]{:S(2)}) %collective-permute-start.7) | collective-permute-done | bytes 262176 | tf_op jit(solution)/shard_map/ppermute | solution.py:195
  46.9 7.4 %all-to-all-start.1 = ((f32[16,4,8,128]{3,2,1,0:T(8,128)}), f32[16,4,8,128]{3,2,1,0:T(8,128)S(1)}, u32[]{:S(2)}, u32[]{:S(2)}) async-start(f32[16,4,8,128]{3,2,1,0:T(8,128)} %bitcast_add_fusion), calls=%async_computation.1 | async-start | bytes 524288 | tf_op jit(solution)/shard_map/all_to_all | solution.py:222
  55.4 4.7 %collective-permute-start.5 = (f32[256,512]{1,0:T(8,128)}, f32[256,512]{1,0:T(8,128)S(1)}, u32[]{:S(2)}, u32[]{:S(2)}) collective-permute-start(f32[256,512]{1,0:T(8,128)} %get-tuple-element.20), channel_id=1, source_target_pairs={{0,6},{1,7},{2,0},{3,1},{4,2},{5,3},{6,4},{7,5},{8,14},{9,15},{10,... | collective-permute-start | bytes 1572872 | tf_op jit(solution)/shard_map/ppermute | solution.py:195
  60.0 1.9 collective-permute-start.4
  62.0 2.1 collective-permute-start
  64.1 3.7 %collective-permute-start.1 = (f32[4,256,256]{2,1,0:T(8,128)S(1)}, f32[4,256,256]{2,1,0:T(8,128)}, u32[]{:S(2)}, u32[]{:S(2)}) collective-permute-start(f32[4,256,256]{2,1,0:T(8,128)S(1)} %copy-done.2), channel_id=1, source_target_pairs={{0,384},{1,385},{2,386},{3,387},{4,388},{5,389},{6,390},{7,391},{8... | collective-permute-start | bytes 3145736 | tf_op jit(solution)/shard_map/ppermute | solution.py:195
  67.8 3.1 %collective-permute-start.2 = (f32[4,256,256]{2,1,0:T(8,128)S(1)}, f32[4,256,256]{2,1,0:T(8,128)}, u32[]{:S(2)}, u32[]{:S(2)}) collective-permute-start(f32[4,256,256]{2,1,0:T(8,128)S(1)} %copy-done.2), channel_id=1, source_target_pairs={{0,256},{1,257},{2,258},{3,259},{4,260},{5,261},{6,262},{7,263},{8... | collective-permute-start | bytes 3145736 | tf_op jit(solution)/shard_map/ppermute | solution.py:195
  72.1 3.4 %collective-permute-start.8 = (f32[4,128,128]{2,1,0:T(8,128)S(1)}, f32[4,128,128]{2,1,0:T(8,128)S(1)}, u32[]{:S(2)}, u32[]{:S(2)}) collective-permute-start(f32[4,128,128]{2,1,0:T(8,128)S(1)} %copy_bitcast_fusion), channel_id=1, source_target_pairs={{0,2},{1,3},{2,0},{3,1},{4,6},{5,7},{6,4},{7,5},{8,10},{9,11},{10,... | collective-permute-start | bytes 786440 | tf_op jit(solution)/shard_map/ppermute | solution.py:195
  75.5 1.9 collective-permute-start.3
  81.0 1.9 collective-permute-start.6
  84.0 6.0 %collective-permute-done.refs_1_ = f32[4,256,256]{2,1,0:T(8,128)} collective-permute-done((f32[4,256,256]{2,1,0:T(8,128)S(1)}, f32[4,256,256]{2,1,0:T(8,128)}, u32[]{:S(2)}, u32[]{:S(2)}) %collective-permute-start) | collective-permute-done | bytes 1048608 | tf_op jit(solution)/shard_map/ppermute | solution.py:195
  90.0 2.2 collective-permute-start.9
  92.2 18.4 %collective-permute-done.1.refs_2_ = f32[4,256,256]{2,1,0:T(8,128)} collective-permute-done((f32[4,256,256]{2,1,0:T(8,128)S(1)}, f32[4,256,256]{2,1,0:T(8,128)}, u32[]{:S(2)}, u32[]{:S(2)}) %collective-permute-start.1) | collective-permute-done | bytes 1048608 | tf_op jit(solution)/shard_map/ppermute | solution.py:195
  110.6 1.9 collective-permute-start.10
  112.5 3.1 %collective-permute-done.2.refs_3_ = f32[4,256,256]{2,1,0:T(8,128)} collective-permute-done((f32[4,256,256]{2,1,0:T(8,128)S(1)}, f32[4,256,256]{2,1,0:T(8,128)}, u32[]{:S(2)}, u32[]{:S(2)}) %collective-permute-start.2) | collective-permute-done | bytes 1048608 | tf_op jit(solution)/shard_map/ppermute | solution.py:195
  115.7 4.2 %collective-permute-start.11 = (f32[2,4,128,128]{3,2,1,0:T(8,128)S(1)}, f32[2,4,128,128]{3,2,1,0:T(8,128)S(1)}, u32[]{:S(2)}, u32[]{:S(2)}) collective-permute-start(f32[2,4,128,128]{3,2,1,0:T(8,128)S(1)} %pad_maximum_fusion.1.refs_2_), channel_id=1, source_target_pairs={{0,256},{1,257},{2,258},{3,259},{4,260},{5,261},{6,262},{7,263},{8... | collective-permute-start | bytes 1572872 | tf_op jit(solution)/shard_map/ppermute | solution.py:195
  119.9 1.9 collective-permute-start.12
  125.5 9.8 %collective-permute-done.10.refs_4_ = f32[2,4,128,128]{3,2,1,0:T(8,128)S(1)} collective-permute-done((f32[2,4,128,128]{3,2,1,0:T(8,128)S(1)}, f32[2,4,128,128]{3,2,1,0:T(8,128)S(1)}, u32[]{:S(2)}, u32[]{:S(2)}) %collective-permute-start.10) | collective-permute-done | bytes 524320 | tf_op jit(solution)/shard_map/ppermute | solution.py:195
  137.3 2.4 collective-permute-start.15
  139.7 10.2 %mix.1 = (bf16[2,4,256,512]{3,2,1,0:T(8,128)(2,1)S(1)}, bf16[2,4,256,512]{3,2,1,0:T(8,128)(2,1)S(1)}) custom-call(f32[4,256,256]{2,1,0:T(8,128)S(1)} %copy-done.2, f32[4,256,256]{2,1,0:T(8,128)} %collective-permute-done.refs_1_, f32[4,256,256]{2,1,0:T(8,128)} %collective-permute-done.1.refs_2_, f32[4,256,256]{2,1,0:T(8,128)} %collective-permute-done.2.refs_3_, ...), custom_call_target="tpu_custom_call" | custom-call | flops 6442450944 | bytes 16777216 | tf_op jit(solution)/shard_map/mix/pallas_call | solution.py:63
  149.9 4.0 %respond_far.1 = (f32[128,512]{1,0:T(8,128)S(1)}, f32[128,512]{1,0:T(8,128)S(1)}, f32[128,512]{1,0:T(8,128)S(1)}, bf16[4,512,512]{2,1,0:T(8,128)(2,1)S(1)}, bf16[4,512,512]{2,1,0:T(8,128)(2,1)S(1)}) custom-call(bf16[2,4,256,512]{3,2,1,0:T(8,128)(2,1)S(1)} %get-tuple-element.12.refs_0_.mh, bf16[2,4,256,512]{3,2,1,0:T(8,128)(2,1)S(1)} %get-tuple-element.13.refs_1_.ml, ...), custom_call_target="tpu_custom_call" | custom-call | flops 1610612736 | bytes 8388608 | tf_op jit(solution)/shard_map/respond_far/pallas_call | solution.py:137
  154.0 3.9 %collective-permute-start.17 = (f32[128,512]{1,0:T(8,128)S(1)}, f32[128,512]{1,0:T(8,128)S(1)}, u32[]{:S(2)}, u32[]{:S(2)}) collective-permute-start(f32[128,512]{1,0:T(8,128)S(1)} %get-tuple-element.17), channel_id=1, source_target_pairs={{0,4},{1,5},{2,6},{3,7},{4,0},{5,1},{6,2},{7,3},{8,12},{9,13},{10,... | collective-permute-start | bytes 786440 | tf_op jit(solution)/shard_map/ppermute | solution.py:195
  157.9 4.5 %collective-permute-start.18 = (f32[128,512]{1,0:T(8,128)S(1)}, f32[128,512]{1,0:T(8,128)S(1)}, u32[]{:S(2)}, u32[]{:S(2)}) collective-permute-start(f32[128,512]{1,0:T(8,128)S(1)} %get-tuple-element.18), channel_id=1, source_target_pairs={{0,12},{1,13},{2,14},{3,15},{4,8},{5,9},{6,10},{7,11},{8,4},{9,5},... | collective-permute-start | bytes 786440 | tf_op jit(solution)/shard_map/ppermute | solution.py:195
  162.4 2.3 collective-permute-start.16
  166.2 4.8 %collective-permute-done.17 = f32[128,512]{1,0:T(8,128)S(1)} collective-permute-done((f32[128,512]{1,0:T(8,128)S(1)}, f32[128,512]{1,0:T(8,128)S(1)}, u32[]{:S(2)}, u32[]{:S(2)}) %collective-permute-start.17) | collective-permute-done | bytes 262176 | tf_op jit(solution)/shard_map/ppermute | solution.py:195
  171.3 3.0 %collective-permute-done.16 = f32[128,512]{1,0:T(8,128)S(1)} collective-permute-done((f32[128,512]{1,0:T(8,128)S(1)}, f32[128,512]{1,0:T(8,128)S(1)}, u32[]{:S(2)}, u32[]{:S(2)}) %collective-permute-start.16) | collective-permute-done | bytes 262176 | tf_op jit(solution)/shard_map/ppermute | solution.py:195
  174.4 31.4 %all_to_all.25 = f32[8,16,512]{2,1,0:T(8,128)S(1)} all-to-all(f32[8,16,512]{2,1,0:T(8,128)S(1)} %bitcast.45), channel_id=1, replica_groups={{0,16,32,48,64,80,96,112},{4,20,36,52,68,84,100,116},{8,24,40,56,72,88,..., dimensions={0} | all-to-all | bytes 524288 | tf_op jit(solution)/shard_map/all_to_all | solution.py:240
  205.9 22.7 %all_to_all.26 = f32[8,16,512]{2,1,0:T(8,128)S(1)} all-to-all(f32[8,16,512]{2,1,0:T(8,128)S(1)} %broadcast_in_dim.6), channel_id=1, replica_groups={{0,16,32,48,64,80,96,112},{4,20,36,52,68,84,100,116},{8,24,40,56,72,88,..., dimensions={0} | all-to-all | bytes 524288 | tf_op jit(solution)/shard_map/all_to_all | solution.py:240
  228.8 15.9 %all_to_all.27 = f32[4,128,512]{2,1,0:T(8,128)S(1)} all-to-all(f32[4,128,512]{2,1,0:T(8,128)S(1)} %broadcast_in_dim.7), channel_id=1, replica_groups={{0,4,8,12},{16,20,24,28},{32,36,40,44},{48,52,56,60},{64,68,72,76},{80,..., dimensions={0} | all-to-all | bytes 2097152 | tf_op jit(solution)/shard_map/all_to_all | solution.py:240
  (49 shorter events, 19.2 us)
Async XLA Ops:
  0.0 17.1 %copy-start = (f32[128,128]{1,0:T(8,128)S(1)}, f32[128,128]{1,0:T(8,128)}, u32[]{:S(2)}) copy-start(f32[128,128]{1,0:T(8,128)} %param.6) | copy-start | bytes 196612
  1.9 33.6 %all-to-all-start = ((f32[16,4,8,128]{3,1,2,0:T(4,128)}), f32[16,4,8,128]{3,1,2,0:T(4,128)S(1)}, u32[]{:S(2)}, u32[]{:S(2)}) async-start(f32[16,4,8,128]{3,1,2,0:T(4,128)} %bitcast.8), calls=%async_computation | async-start | bytes 524288 | tf_op jit(solution)/shard_map/all_to_all | solution.py:211
  17.5 36.8 %copy-start.1 = (f32[2,256,512]{2,1,0:T(8,128)S(1)}, f32[2,256,512]{2,1,0:T(8,128)}, u32[]{:S(2)}) copy-start(f32[2,256,512]{2,1,0:T(8,128)} %refs_4_.1) | copy-start | bytes 3145732
  36.1 25.8 %copy-start.2 = (f32[4,256,256]{2,1,0:T(8,128)S(1)}, f32[4,256,256]{2,1,0:T(8,128)}, u32[]{:S(2)}) copy-start(f32[4,256,256]{2,1,0:T(8,128)} %refs_0_.1) | copy-start | bytes 3145732
  36.2 9.9 %collective-permute-start.7 = (f32[16,4,8,128]{3,2,1,0:T(8,128)S(1)}, f32[16,4,8,128]{3,2,1,0:T(8,128)S(1)}, u32[]{:S(2)}, u32[]{:S(2)}) collective-permute-start(f32[16,4,8,128]{3,2,1,0:T(8,128)S(1)} %bitcast.50), channel_id=1, source_target_pairs={{0,4},{1,5},{2,6},{3,7},{4,0},{5,1},{6,2},{7,3},{8,12},{9,13},{10,... | collective-permute-start | bytes 786440 | tf_op jit(solution)/shard_map/ppermute | solution.py:195
  46.9 25.1 %all-to-all-start.1 = ((f32[16,4,8,128]{3,2,1,0:T(8,128)}), f32[16,4,8,128]{3,2,1,0:T(8,128)S(1)}, u32[]{:S(2)}, u32[]{:S(2)}) async-start(f32[16,4,8,128]{3,2,1,0:T(8,128)} %bitcast_add_fusion), calls=%async_computation.1 | async-start | bytes 524288 | tf_op jit(solution)/shard_map/all_to_all | solution.py:222
  55.4 16.7 %collective-permute-start.5 = (f32[256,512]{1,0:T(8,128)}, f32[256,512]{1,0:T(8,128)S(1)}, u32[]{:S(2)}, u32[]{:S(2)}) collective-permute-start(f32[256,512]{1,0:T(8,128)} %get-tuple-element.20), channel_id=1, source_target_pairs={{0,6},{1,7},{2,0},{3,1},{4,2},{5,3},{6,4},{7,5},{8,14},{9,15},{10,... | collective-permute-start | bytes 1572872 | tf_op jit(solution)/shard_map/ppermute | solution.py:195
  60.0 15.5 %collective-permute-start.4 = (f32[256,512]{1,0:T(8,128)}, f32[256,512]{1,0:T(8,128)S(1)}, u32[]{:S(2)}, u32[]{:S(2)}) collective-permute-start(f32[256,512]{1,0:T(8,128)} %get-tuple-element.19), channel_id=1, source_target_pairs={{0,2},{1,3},{2,4},{3,5},{4,6},{5,7},{6,0},{7,1},{8,10},{9,11},{10,... | collective-permute-start | bytes 1572872 | tf_op jit(solution)/shard_map/ppermute | solution.py:195
  62.0 28.0 %collective-permute-start = (f32[4,256,256]{2,1,0:T(8,128)S(1)}, f32[4,256,256]{2,1,0:T(8,128)}, u32[]{:S(2)}, u32[]{:S(2)}) collective-permute-start(f32[4,256,256]{2,1,0:T(8,128)S(1)} %copy-done.2), channel_id=1, source_target_pairs={{0,128},{1,129},{2,130},{3,131},{4,132},{5,133},{6,134},{7,135},{8... | collective-permute-start | bytes 3145736 | tf_op jit(solution)/shard_map/ppermute | solution.py:195
  64.1 46.6 %collective-permute-start.1 = (f32[4,256,256]{2,1,0:T(8,128)S(1)}, f32[4,256,256]{2,1,0:T(8,128)}, u32[]{:S(2)}, u32[]{:S(2)}) collective-permute-start(f32[4,256,256]{2,1,0:T(8,128)S(1)} %copy-done.2), channel_id=1, source_target_pairs={{0,384},{1,385},{2,386},{3,387},{4,388},{5,389},{6,390},{7,391},{8... | collective-permute-start | bytes 3145736 | tf_op jit(solution)/shard_map/ppermute | solution.py:195
  67.8 47.8 %collective-permute-start.2 = (f32[4,256,256]{2,1,0:T(8,128)S(1)}, f32[4,256,256]{2,1,0:T(8,128)}, u32[]{:S(2)}, u32[]{:S(2)}) collective-permute-start(f32[4,256,256]{2,1,0:T(8,128)S(1)} %copy-done.2), channel_id=1, source_target_pairs={{0,256},{1,257},{2,258},{3,259},{4,260},{5,261},{6,262},{7,263},{8... | collective-permute-start | bytes 3145736 | tf_op jit(solution)/shard_map/ppermute | solution.py:195
  72.1 5.4 %copy-start.3 = (f32[256,512]{1,0:T(8,128)}, f32[256,512]{1,0:T(8,128)S(1)}, u32[]{:S(2)}) copy-start(f32[256,512]{1,0:T(8,128)S(1)} %collective-permute-done.5) | copy-start | bytes 1572868
  72.1 8.3 %collective-permute-start.8 = (f32[4,128,128]{2,1,0:T(8,128)S(1)}, f32[4,128,128]{2,1,0:T(8,128)S(1)}, u32[]{:S(2)}, u32[]{:S(2)}) collective-permute-start(f32[4,128,128]{2,1,0:T(8,128)S(1)} %copy_bitcast_fusion), channel_id=1, source_target_pairs={{0,2},{1,3},{2,0},{3,1},{4,6},{5,7},{6,4},{7,5},{8,10},{9,11},{10,... | collective-permute-start | bytes 786440 | tf_op jit(solution)/shard_map/ppermute | solution.py:195
  75.5 1.9 copy-start.4
  75.5 44.3 %collective-permute-start.3 = (f32[2,256,512]{2,1,0:T(8,128)S(1)}, f32[2,256,512]{2,1,0:T(8,128)}, u32[]{:S(2)}, u32[]{:S(2)}) collective-permute-start(f32[2,256,512]{2,1,0:T(8,128)S(1)} %copy-done.1), channel_id=1, source_target_pairs={{0,1},{1,0},{2,3},{3,2},{4,5},{5,4},{6,7},{7,6},{8,9},{9,8},{10,11... | collective-permute-start | bytes 3145736 | tf_op jit(solution)/shard_map/ppermute | solution.py:195
  80.3 0.7 copy-start.5
  81.0 58.6 %collective-permute-start.6 = (f32[2,256,512]{2,1,0:T(8,128)S(1)}, f32[2,256,512]{2,1,0:T(8,128)}, u32[]{:S(2)}, u32[]{:S(2)}) collective-permute-start(f32[2,256,512]{2,1,0:T(8,128)S(1)} %pad_maximum_fusion.refs_6_), channel_id=1, source_target_pairs={{0,1},{1,0},{2,3},{3,2},{4,5},{5,4},{6,7},{7,6},{8,9},{9,8},{10,11... | collective-permute-start | bytes 3145736 | tf_op jit(solution)/shard_map/ppermute | solution.py:195
  90.0 33.6 %collective-permute-start.9 = (f32[2,4,128,128]{3,2,1,0:T(8,128)S(1)}, f32[2,4,128,128]{3,2,1,0:T(8,128)S(1)}, u32[]{:S(2)}, u32[]{:S(2)}) collective-permute-start(f32[2,4,128,128]{3,2,1,0:T(8,128)S(1)} %pad_maximum_fusion.1.refs_2_), channel_id=1, source_target_pairs={{0,128},{1,129},{2,130},{3,131},{4,132},{5,133},{6,134},{7,135},{8... | collective-permute-start | bytes 1572872 | tf_op jit(solution)/shard_map/ppermute | solution.py:195
  110.6 24.7 %collective-permute-start.10 = (f32[2,4,128,128]{3,2,1,0:T(8,128)S(1)}, f32[2,4,128,128]{3,2,1,0:T(8,128)S(1)}, u32[]{:S(2)}, u32[]{:S(2)}) collective-permute-start(f32[2,4,128,128]{3,2,1,0:T(8,128)S(1)} %pad_maximum_fusion.1.refs_2_), channel_id=1, source_target_pairs={{0,384},{1,385},{2,386},{3,387},{4,388},{5,389},{6,390},{7,391},{8... | collective-permute-start | bytes 1572872 | tf_op jit(solution)/shard_map/ppermute | solution.py:195
  115.7 21.6 %collective-permute-start.11 = (f32[2,4,128,128]{3,2,1,0:T(8,128)S(1)}, f32[2,4,128,128]{3,2,1,0:T(8,128)S(1)}, u32[]{:S(2)}, u32[]{:S(2)}) collective-permute-start(f32[2,4,128,128]{3,2,1,0:T(8,128)S(1)} %pad_maximum_fusion.1.refs_2_), channel_id=1, source_target_pairs={{0,256},{1,257},{2,258},{3,259},{4,260},{5,261},{6,262},{7,263},{8... | collective-permute-start | bytes 1572872 | tf_op jit(solution)/shard_map/ppermute | solution.py:195
  119.9 30.0 %collective-permute-start.12 = (f32[2,4,128,128]{3,2,1,0:T(8,128)S(1)}, f32[2,4,128,128]{3,2,1,0:T(8,128)S(1)}, u32[]{:S(2)}, u32[]{:S(2)}) collective-permute-start(f32[2,4,128,128]{3,2,1,0:T(8,128)S(1)} %pad_maximum_fusion.1.refs_2_), channel_id=1, source_target_pairs={{0,1},{1,0},{2,3},{3,2},{4,5},{5,4},{6,7},{7,6},{8,9},{9,8},{10,11... | collective-permute-start | bytes 1572872 | tf_op jit(solution)/shard_map/ppermute | solution.py:195
  123.6 26.3 %collective-permute-start.13 = (f32[2,4,128,128]{3,2,1,0:T(8,128)S(1)}, f32[2,4,128,128]{3,2,1,0:T(8,128)S(1)}, u32[]{:S(2)}, u32[]{:S(2)}) collective-permute-start(f32[2,4,128,128]{3,2,1,0:T(8,128)S(1)} %collective-permute-done.9.refs_3_), channel_id=1, source_target_pairs={{0,1},{1,0},{2,3},{3,2},{4,5},{5,4},{6,7},{7,6},{8,9},{9,8},{10,11... | collective-permute-start | bytes 1572872 | tf_op jit(solution)/shard_map/ppermute | solution.py:195
  135.3 14.6 %collective-permute-start.14 = (f32[2,4,128,128]{3,2,1,0:T(8,128)S(1)}, f32[2,4,128,128]{3,2,1,0:T(8,128)S(1)}, u32[]{:S(2)}, u32[]{:S(2)}) collective-permute-start(f32[2,4,128,128]{3,2,1,0:T(8,128)S(1)} %collective-permute-done.10.refs_4_), channel_id=1, source_target_pairs={{0,1},{1,0},{2,3},{3,2},{4,5},{5,4},{6,7},{7,6},{8,9},{9,8},{10,11... | collective-permute-start | bytes 1572872 | tf_op jit(solution)/shard_map/ppermute | solution.py:195
  137.3 12.7 %collective-permute-start.15 = (f32[2,4,128,128]{3,2,1,0:T(8,128)S(1)}, f32[2,4,128,128]{3,2,1,0:T(8,128)S(1)}, u32[]{:S(2)}, u32[]{:S(2)}) collective-permute-start(f32[2,4,128,128]{3,2,1,0:T(8,128)S(1)} %collective-permute-done.11.refs_5_), channel_id=1, source_target_pairs={{0,1},{1,0},{2,3},{3,2},{4,5},{5,4},{6,7},{7,6},{8,9},{9,8},{10,11... | collective-permute-start | bytes 1572872 | tf_op jit(solution)/shard_map/ppermute | solution.py:195
  154.0 17.1 %collective-permute-start.17 = (f32[128,512]{1,0:T(8,128)S(1)}, f32[128,512]{1,0:T(8,128)S(1)}, u32[]{:S(2)}, u32[]{:S(2)}) collective-permute-start(f32[128,512]{1,0:T(8,128)S(1)} %get-tuple-element.17), channel_id=1, source_target_pairs={{0,4},{1,5},{2,6},{3,7},{4,0},{5,1},{6,2},{7,3},{8,12},{9,13},{10,... | collective-permute-start | bytes 786440 | tf_op jit(solution)/shard_map/ppermute | solution.py:195
  157.9 13.5 %collective-permute-start.18 = (f32[128,512]{1,0:T(8,128)S(1)}, f32[128,512]{1,0:T(8,128)S(1)}, u32[]{:S(2)}, u32[]{:S(2)}) collective-permute-start(f32[128,512]{1,0:T(8,128)S(1)} %get-tuple-element.18), channel_id=1, source_target_pairs={{0,12},{1,13},{2,14},{3,15},{4,8},{5,9},{6,10},{7,11},{8,4},{9,5},... | collective-permute-start | bytes 786440 | tf_op jit(solution)/shard_map/ppermute | solution.py:195
  162.4 12.0 %collective-permute-start.16 = (f32[128,512]{1,0:T(8,128)S(1)}, f32[128,512]{1,0:T(8,128)S(1)}, u32[]{:S(2)}, u32[]{:S(2)}) collective-permute-start(f32[128,512]{1,0:T(8,128)S(1)} %get-tuple-element.16), channel_id=1, source_target_pairs={{0,8},{1,9},{2,10},{3,11},{4,12},{5,13},{6,14},{7,15},{8,0},{9,1},... | collective-permute-start | bytes 786440 | tf_op jit(solution)/shard_map/ppermute | solution.py:195

commit v8 on v5

--- a/solution.py
+++ b/solution.py
@@ -169,6 +169,28 @@
     )(*m_pair, *c_pair)
 
 
+def deal_kernel(blocks, out, sems):
+    copies = [pltpu.make_async_copy(blocks.at[q], out.at[:, q], sems.at[q]) for q in range(blocks.shape[0])]
+    for copy in copies:
+        copy.start()
+    for copy in copies:
+        copy.wait()
+
+
+def deal(blocks):
+    n_q, n, rows, cols = blocks.shape
+    return pl.pallas_call(
+        deal_kernel,
+        name="deal",
+        out_shape=jax.ShapeDtypeStruct((n, n_q, rows, cols), f32),
+        in_specs=[pl.BlockSpec(memory_space=pl.ANY)],
+        out_specs=pl.BlockSpec(memory_space=pl.ANY),
+        scratch_shapes=[pltpu.SemaphoreType.DMA((n_q,))],
+        compiler_params=pltpu.CompilerParams(vmem_limit_bytes=2 << 20),
+        cost_estimate=pl.CostEstimate(flops=0, transcendentals=0, bytes_accessed=8 * blocks.size),
+    )(blocks)
+
+
 def moves(mesh, step):
     n_state, n_aux, n_cond = (mesh.shape[name] for name in AXES)
 
@@ -215,7 +237,7 @@
         pieces.append(send(far, to_core))
 
         qb, v1, v2 = val_pairs.shape
-        spread = val_pairs.reshape(qb, n_z, v1 // n_z, v2).transpose(1, 0, 2, 3)
+        spread = deal(val_pairs.reshape(qb, n_z, v1 // n_z, v2))
         spread = lax.all_to_all(spread, "aux", 0, 0, axis_index_groups=along_z)
         n_q = screened.shape[0]
         q = lax.broadcasted_iota(jnp.int32, (n_q, n_q // 2), 0)

time: 250 us -> 250 us (level)
  no operation moved by 1% of the time
where the time goes in v8:
time: 250 us; the launch traced here: 247 us
  starting transfers between devices  77.6 us (31%)
  waiting for transfers between devices  71.9 us (29%)
  blocking collectives  70.2 us (28%)
  Pallas kernels  18.2 us (7%)
  local copies, waits for them, and re-layouts  4.09 us (2%)
  other arithmetic  3.22 us (1%)
    all_to_all x3, blocking collectives, per_device(): lax.all_to_all(value, 'aux', 0, 0, axis_index_groups=groups)  70.2 us
    ppermute x19, starting transfers between devices, send(): return lax.ppermute(value, AXES, pairs)  55 us
    ppermute x19, waiting for transfers between devices, send(): return lax.ppermute(value, AXES, pairs)  52.9 us
    all_to_all x1, waiting for transfers between devices, per_device(): spread = lax.all_to_all(spread, 'aux', 0, 0, axis_index_groups=along_z)  18 us
    all_to_all x1, starting transfers between devices, per_device(): spread = lax.all_to_all(spread, 'aux', 0, 0, axis_index_groups=along_z)  15.2 us
    pallas_call x1, Pallas kernels, mix(): pl.pallas_call(mix_kernel, name='mix', out_shape=(shape, shape), in_specs...  11.9 us
    all_to_all x1, starting transfers between devices, per_device(): block = lax.all_to_all(block, 'aux', 0, 0, axis_index_groups=along_z)  7.38 us
  transfers between devices with their start and end apart: 21, of which 11 were waited for; matrix products, arithmetic and copies ran while one was open for 1% of the time, Pallas kernels for 6%

profile of v8, /device:TPU:24, one launch (start us, length us, event | category | flops | bytes accessed | tf_op | source)
XLA Modules:
  0.0 246.6 jit_solution(9755042528743458201)
XLA Ops:
  1.7 15.2 %all-to-all-start = ((f32[16,4,8,128]{3,2,1,0:T(8,128)}), f32[16,4,8,128]{3,2,1,0:T(8,128)S(1)}, u32[]{:S(2)}, u32[]{:S(2)}) async-start(f32[16,4,8,128]{3,2,1,0:T(8,128)} %deal.1), calls=%async_computation | async-start | bytes 524288 | tf_op jit(solution)/shard_map/all_to_all | solution.py:241
  17.4 18.0 %all-to-all-done = f32[16,4,8,128]{3,2,1,0:T(8,128)S(1)} async-done(((f32[16,4,8,128]{3,2,1,0:T(8,128)}), f32[16,4,8,128]{3,2,1,0:T(8,128)S(1)}, u32[]{:S(2)}, u32[]{:S(2)}) %all-to-all-start) | async-done | bytes 262176 | tf_op jit(solution)/shard_map/all_to_all | solution.py:241
  36.1 5.1 %collective-permute-start.7 = (f32[16,4,8,128]{3,2,1,0:T(8,128)S(1)}, f32[16,4,8,128]{3,2,1,0:T(8,128)S(1)}, u32[]{:S(2)}, u32[]{:S(2)}) collective-permute-start(f32[16,4,8,128]{3,2,1,0:T(8,128)S(1)} %bitcast.46), channel_id=1, source_target_pairs={{0,4},{1,5},{2,6},{3,7},{4,0},{5,1},{6,2},{7,3},{8,12},{9,13},{10,... | collective-permute-start | bytes 786440 | tf_op jit(solution)/shard_map/ppermute | solution.py:225
  41.1 4.8 %collective-permute-done.7 = f32[16,4,8,128]{3,2,1,0:T(8,128)S(1)} collective-permute-done((f32[16,4,8,128]{3,2,1,0:T(8,128)S(1)}, f32[16,4,8,128]{3,2,1,0:T(8,128)S(1)}, u32[]{:S(2)}, u32[]{:S(2)}) %collective-permute-start.7) | collective-permute-done | bytes 262176 | tf_op jit(solution)/shard_map/ppermute | solution.py:225
  46.8 7.4 %all-to-all-start.1 = ((f32[16,4,8,128]{3,2,1,0:T(8,128)}), f32[16,4,8,128]{3,2,1,0:T(8,128)S(1)}, u32[]{:S(2)}, u32[]{:S(2)}) async-start(f32[16,4,8,128]{3,2,1,0:T(8,128)} %bitcast_add_fusion), calls=%async_computation.1 | async-start | bytes 524288 | tf_op jit(solution)/shard_map/all_to_all | solution.py:252
  55.2 4.7 %collective-permute-start.5 = (f32[256,512]{1,0:T(8,128)}, f32[256,512]{1,0:T(8,128)S(1)}, u32[]{:S(2)}, u32[]{:S(2)}) collective-permute-start(f32[256,512]{1,0:T(8,128)} %get-tuple-element.22), channel_id=1, source_target_pairs={{0,6},{1,7},{2,0},{3,1},{4,2},{5,3},{6,4},{7,5},{8,14},{9,15},{10,... | collective-permute-start | bytes 1572872 | tf_op jit(solution)/shard_map/ppermute | solution.py:225
  59.8 1.9 collective-permute-start.4
  61.8 2.1 collective-permute-start
  63.9 3.7 %collective-permute-start.1 = (f32[4,256,256]{2,1,0:T(8,128)S(1)}, f32[4,256,256]{2,1,0:T(8,128)}, u32[]{:S(2)}, u32[]{:S(2)}) collective-permute-start(f32[4,256,256]{2,1,0:T(8,128)S(1)} %copy-done.3), channel_id=1, source_target_pairs={{0,384},{1,385},{2,386},{3,387},{4,388},{5,389},{6,390},{7,391},{8... | collective-permute-start | bytes 3145736 | tf_op jit(solution)/shard_map/ppermute | solution.py:225
  67.6 3.1 %collective-permute-start.2 = (f32[4,256,256]{2,1,0:T(8,128)S(1)}, f32[4,256,256]{2,1,0:T(8,128)}, u32[]{:S(2)}, u32[]{:S(2)}) collective-permute-start(f32[4,256,256]{2,1,0:T(8,128)S(1)} %copy-done.3), channel_id=1, source_target_pairs={{0,256},{1,257},{2,258},{3,259},{4,260},{5,261},{6,262},{7,263},{8... | collective-permute-start | bytes 3145736 | tf_op jit(solution)/shard_map/ppermute | solution.py:225
  71.9 3.4 %collective-permute-start.8 = (f32[4,128,128]{2,1,0:T(8,128)S(1)}, f32[4,128,128]{2,1,0:T(8,128)S(1)}, u32[]{:S(2)}, u32[]{:S(2)}) collective-permute-start(f32[4,128,128]{2,1,0:T(8,128)S(1)} %copy_bitcast_fusion), channel_id=1, source_target_pairs={{0,2},{1,3},{2,0},{3,1},{4,6},{5,7},{6,4},{7,5},{8,10},{9,11},{10,... | collective-permute-start | bytes 786440 | tf_op jit(solution)/shard_map/ppermute | solution.py:225
  75.3 1.9 collective-permute-start.3
  80.9 1.9 collective-permute-start.6
  83.8 6.0 %collective-permute-done.refs_1_ = f32[4,256,256]{2,1,0:T(8,128)} collective-permute-done((f32[4,256,256]{2,1,0:T(8,128)S(1)}, f32[4,256,256]{2,1,0:T(8,128)}, u32[]{:S(2)}, u32[]{:S(2)}) %collective-permute-start) | collective-permute-done | bytes 1048608 | tf_op jit(solution)/shard_map/ppermute | solution.py:225
  89.8 2.2 collective-permute-start.9
  92.0 18.4 %collective-permute-done.1.refs_2_ = f32[4,256,256]{2,1,0:T(8,128)} collective-permute-done((f32[4,256,256]{2,1,0:T(8,128)S(1)}, f32[4,256,256]{2,1,0:T(8,128)}, u32[]{:S(2)}, u32[]{:S(2)}) %collective-permute-start.1) | collective-permute-done | bytes 1048608 | tf_op jit(solution)/shard_map/ppermute | solution.py:225
  112.4 3.1 %collective-permute-done.2.refs_3_ = f32[4,256,256]{2,1,0:T(8,128)} collective-permute-done((f32[4,256,256]{2,1,0:T(8,128)S(1)}, f32[4,256,256]{2,1,0:T(8,128)}, u32[]{:S(2)}, u32[]{:S(2)}) %collective-permute-start.2) | collective-permute-done | bytes 1048608 | tf_op jit(solution)/shard_map/ppermute | solution.py:225
  115.5 4.2 %collective-permute-start.11 = (f32[2,4,128,128]{3,2,1,0:T(8,128)S(1)}, f32[2,4,128,128]{3,2,1,0:T(8,128)S(1)}, u32[]{:S(2)}, u32[]{:S(2)}) collective-permute-start(f32[2,4,128,128]{3,2,1,0:T(8,128)S(1)} %pad_maximum_fusion.1.refs_2_), channel_id=1, source_target_pairs={{0,256},{1,257},{2,258},{3,259},{4,260},{5,261},{6,262},{7,263},{8... | collective-permute-start | bytes 1572872 | tf_op jit(solution)/shard_map/ppermute | solution.py:225
  119.7 1.9 collective-permute-start.12
  125.4 9.8 %collective-permute-done.10.refs_4_ = f32[2,4,128,128]{3,2,1,0:T(8,128)S(1)} collective-permute-done((f32[2,4,128,128]{3,2,1,0:T(8,128)S(1)}, f32[2,4,128,128]{3,2,1,0:T(8,128)S(1)}, u32[]{:S(2)}, u32[]{:S(2)}) %collective-permute-start.10) | collective-permute-done | bytes 524320 | tf_op jit(solution)/shard_map/ppermute | solution.py:225
  137.1 2.4 collective-permute-start.15
  139.5 11.9 %mix.1 = (bf16[2,4,256,512]{3,2,1,0:T(8,128)(2,1)S(1)}, bf16[2,4,256,512]{3,2,1,0:T(8,128)(2,1)S(1)}) custom-call(f32[4,256,256]{2,1,0:T(8,128)S(1)} %copy-done.3, f32[4,256,256]{2,1,0:T(8,128)} %collective-permute-done.refs_1_, f32[4,256,256]{2,1,0:T(8,128)} %collective-permute-done.1.refs_2_, f32[4,256,256]{2,1,0:T(8,128)} %collective-permute-done.2.refs_3_, ...), custom_call_target="tpu_custom_call" | custom-call | flops 6442450944 | bytes 16777216 | tf_op jit(solution)/shard_map/mix/pallas_call | solution.py:66
  151.5 3.2 %respond_far.1 = (f32[128,512]{1,0:T(8,128)S(1)}, f32[128,512]{1,0:T(8,128)S(1)}, bf16[4,512,512]{2,1,0:T(8,128)(2,1)S(1)}, bf16[4,512,512]{2,1,0:T(8,128)(2,1)S(1)}) custom-call(bf16[2,4,256,512]{3,2,1,0:T(8,128)(2,1)S(1)} %get-tuple-element.13.refs_0_.mh, bf16[2,4,256,512]{3,2,1,0:T(8,128)(2,1)S(1)} %get-tuple-element.14.refs_1_.ml, ...), custom_call_target="tpu_custom_call" | custom-call | flops 1610612736 | bytes 8388608 | tf_op jit(solution)/shard_map/respond_far/pallas_call | solution.py:145
  154.8 3.9 %collective-permute-start.17 = (f32[128,512]{1,0:T(8,128)S(1)}, f32[128,512]{1,0:T(8,128)S(1)}, u32[]{:S(2)}, u32[]{:S(2)}) collective-permute-start(f32[128,512]{1,0:T(8,128)S(1)} %get-tuple-element.19), channel_id=1, source_target_pairs={{0,4},{1,5},{2,6},{3,7},{4,0},{5,1},{6,2},{7,3},{8,12},{9,13},{10,... | collective-permute-start | bytes 786440 | tf_op jit(solution)/shard_map/ppermute | solution.py:225
  158.7 4.5 %collective-permute-start.18 = (f32[128,512]{1,0:T(8,128)S(1)}, f32[128,512]{1,0:T(8,128)S(1)}, u32[]{:S(2)}, u32[]{:S(2)}) collective-permute-start(f32[128,512]{1,0:T(8,128)S(1)} %get-tuple-element.20), channel_id=1, source_target_pairs={{0,12},{1,13},{2,14},{3,15},{4,8},{5,9},{6,10},{7,11},{8,4},{9,5},... | collective-permute-start | bytes 786440 | tf_op jit(solution)/shard_map/ppermute | solution.py:225
  163.2 2.3 respond_near.1
  165.5 2.3 collective-permute-start.16
  167.8 4.2 %collective-permute-done.17 = f32[128,512]{1,0:T(8,128)S(1)} collective-permute-done((f32[128,512]{1,0:T(8,128)S(1)}, f32[128,512]{1,0:T(8,128)S(1)}, u32[]{:S(2)}, u32[]{:S(2)}) %collective-permute-start.17) | collective-permute-done | bytes 262176 | tf_op jit(solution)/shard_map/ppermute | solution.py:225
  172.0 3.1 %collective-permute-done.16 = f32[128,512]{1,0:T(8,128)S(1)} collective-permute-done((f32[128,512]{1,0:T(8,128)S(1)}, f32[128,512]{1,0:T(8,128)S(1)}, u32[]{:S(2)}, u32[]{:S(2)}) %collective-permute-start.16) | collective-permute-done | bytes 262176 | tf_op jit(solution)/shard_map/ppermute | solution.py:225
  175.2 31.5 %all_to_all.25 = f32[8,16,512]{2,1,0:T(8,128)S(1)} all-to-all(f32[8,16,512]{2,1,0:T(8,128)S(1)} %bitcast.41), channel_id=1, replica_groups={{0,16,32,48,64,80,96,112},{4,20,36,52,68,84,100,116},{8,24,40,56,72,88,..., dimensions={0} | all-to-all | bytes 524288 | tf_op jit(solution)/shard_map/all_to_all | solution.py:270
  206.8 22.5 %all_to_all.26 = f32[8,16,512]{2,1,0:T(8,128)S(1)} all-to-all(f32[8,16,512]{2,1,0:T(8,128)S(1)} %broadcast_in_dim.6), channel_id=1, replica_groups={{0,16,32,48,64,80,96,112},{4,20,36,52,68,84,100,116},{8,24,40,56,72,88,..., dimensions={0} | all-to-all | bytes 524288 | tf_op jit(solution)/shard_map/all_to_all | solution.py:270
  229.4 16.2 %all_to_all.27 = f32[4,128,512]{2,1,0:T(8,128)S(1)} all-to-all(f32[4,128,512]{2,1,0:T(8,128)S(1)} %broadcast_in_dim.7), channel_id=1, replica_groups={{0,4,8,12},{16,20,24,28},{32,36,40,44},{48,52,56,60},{64,68,72,76},{80,..., dimensions={0} | all-to-all | bytes 2097152 | tf_op jit(solution)/shard_map/all_to_all | solution.py:270
  (50 shorter events, 19.1 us)
Async XLA Ops:
  0.0 17.0 %copy-start = (f32[128,128]{1,0:T(8,128)S(1)}, f32[128,128]{1,0:T(8,128)}, u32[]{:S(2)}) copy-start(f32[128,128]{1,0:T(8,128)} %param.6) | copy-start | bytes 196612
  0.0 1.0 copy-start.2
  1.7 33.6 %all-to-all-start = ((f32[16,4,8,128]{3,2,1,0:T(8,128)}), f32[16,4,8,128]{3,2,1,0:T(8,128)S(1)}, u32[]{:S(2)}, u32[]{:S(2)}) async-start(f32[16,4,8,128]{3,2,1,0:T(8,128)} %deal.1), calls=%async_computation | async-start | bytes 524288 | tf_op jit(solution)/shard_map/all_to_all | solution.py:241
  16.9 37.2 %copy-start.1 = (f32[2,256,512]{2,1,0:T(8,128)S(1)}, f32[2,256,512]{2,1,0:T(8,128)}, u32[]{:S(2)}) copy-start(f32[2,256,512]{2,1,0:T(8,128)} %refs_4_.1) | copy-start | bytes 3145732
  35.9 25.8 %copy-start.3 = (f32[4,256,256]{2,1,0:T(8,128)S(1)}, f32[4,256,256]{2,1,0:T(8,128)}, u32[]{:S(2)}) copy-start(f32[4,256,256]{2,1,0:T(8,128)} %refs_0_.1) | copy-start | bytes 3145732
  36.1 9.9 %collective-permute-start.7 = (f32[16,4,8,128]{3,2,1,0:T(8,128)S(1)}, f32[16,4,8,128]{3,2,1,0:T(8,128)S(1)}, u32[]{:S(2)}, u32[]{:S(2)}) collective-permute-start(f32[16,4,8,128]{3,2,1,0:T(8,128)S(1)} %bitcast.46), channel_id=1, source_target_pairs={{0,4},{1,5},{2,6},{3,7},{4,0},{5,1},{6,2},{7,3},{8,12},{9,13},{10,... | collective-permute-start | bytes 786440 | tf_op jit(solution)/shard_map/ppermute | solution.py:225
  46.8 25.1 %all-to-all-start.1 = ((f32[16,4,8,128]{3,2,1,0:T(8,128)}), f32[16,4,8,128]{3,2,1,0:T(8,128)S(1)}, u32[]{:S(2)}, u32[]{:S(2)}) async-start(f32[16,4,8,128]{3,2,1,0:T(8,128)} %bitcast_add_fusion), calls=%async_computation.1 | async-start | bytes 524288 | tf_op jit(solution)/shard_map/all_to_all | solution.py:252
  55.2 16.7 %collective-permute-start.5 = (f32[256,512]{1,0:T(8,128)}, f32[256,512]{1,0:T(8,128)S(1)}, u32[]{:S(2)}, u32[]{:S(2)}) collective-permute-start(f32[256,512]{1,0:T(8,128)} %get-tuple-element.22), channel_id=1, source_target_pairs={{0,6},{1,7},{2,0},{3,1},{4,2},{5,3},{6,4},{7,5},{8,14},{9,15},{10,... | collective-permute-start | bytes 1572872 | tf_op jit(solution)/shard_map/ppermute | solution.py:225
  59.8 15.5 %collective-permute-start.4 = (f32[256,512]{1,0:T(8,128)}, f32[256,512]{1,0:T(8,128)S(1)}, u32[]{:S(2)}, u32[]{:S(2)}) collective-permute-start(f32[256,512]{1,0:T(8,128)} %get-tuple-element.21), channel_id=1, source_target_pairs={{0,2},{1,3},{2,4},{3,5},{4,6},{5,7},{6,0},{7,1},{8,10},{9,11},{10,... | collective-permute-start | bytes 1572872 | tf_op jit(solution)/shard_map/ppermute | solution.py:225
  61.8 28.0 %collective-permute-start = (f32[4,256,256]{2,1,0:T(8,128)S(1)}, f32[4,256,256]{2,1,0:T(8,128)}, u32[]{:S(2)}, u32[]{:S(2)}) collective-permute-start(f32[4,256,256]{2,1,0:T(8,128)S(1)} %copy-done.3), channel_id=1, source_target_pairs={{0,128},{1,129},{2,130},{3,131},{4,132},{5,133},{6,134},{7,135},{8... | collective-permute-start | bytes 3145736 | tf_op jit(solution)/shard_map/ppermute | solution.py:225
  63.9 46.5 %collective-permute-start.1 = (f32[4,256,256]{2,1,0:T(8,128)S(1)}, f32[4,256,256]{2,1,0:T(8,128)}, u32[]{:S(2)}, u32[]{:S(2)}) collective-permute-start(f32[4,256,256]{2,1,0:T(8,128)S(1)} %copy-done.3), channel_id=1, source_target_pairs={{0,384},{1,385},{2,386},{3,387},{4,388},{5,389},{6,390},{7,391},{8... | collective-permute-start | bytes 3145736 | tf_op jit(solution)/shard_map/ppermute | solution.py:225
  67.6 47.8 %collective-permute-start.2 = (f32[4,256,256]{2,1,0:T(8,128)S(1)}, f32[4,256,256]{2,1,0:T(8,128)}, u32[]{:S(2)}, u32[]{:S(2)}) collective-permute-start(f32[4,256,256]{2,1,0:T(8,128)S(1)} %copy-done.3), channel_id=1, source_target_pairs={{0,256},{1,257},{2,258},{3,259},{4,260},{5,261},{6,262},{7,263},{8... | collective-permute-start | bytes 3145736 | tf_op jit(solution)/shard_map/ppermute | solution.py:225
  71.9 5.4 %copy-start.4 = (f32[256,512]{1,0:T(8,128)}, f32[256,512]{1,0:T(8,128)S(1)}, u32[]{:S(2)}) copy-start(f32[256,512]{1,0:T(8,128)S(1)} %collective-permute-done.5) | copy-start | bytes 1572868
  71.9 8.3 %collective-permute-start.8 = (f32[4,128,128]{2,1,0:T(8,128)S(1)}, f32[4,128,128]{2,1,0:T(8,128)S(1)}, u32[]{:S(2)}, u32[]{:S(2)}) collective-permute-start(f32[4,128,128]{2,1,0:T(8,128)S(1)} %copy_bitcast_fusion), channel_id=1, source_target_pairs={{0,2},{1,3},{2,0},{3,1},{4,6},{5,7},{6,4},{7,5},{8,10},{9,11},{10,... | collective-permute-start | bytes 786440 | tf_op jit(solution)/shard_map/ppermute | solution.py:225
  75.3 1.9 copy-start.5
  75.3 44.3 %collective-permute-start.3 = (f32[2,256,512]{2,1,0:T(8,128)S(1)}, f32[2,256,512]{2,1,0:T(8,128)}, u32[]{:S(2)}, u32[]{:S(2)}) collective-permute-start(f32[2,256,512]{2,1,0:T(8,128)S(1)} %copy-done.1), channel_id=1, source_target_pairs={{0,1},{1,0},{2,3},{3,2},{4,5},{5,4},{6,7},{7,6},{8,9},{9,8},{10,11... | collective-permute-start | bytes 3145736 | tf_op jit(solution)/shard_map/ppermute | solution.py:225
  80.2 0.7 copy-start.6
  80.9 58.6 %collective-permute-start.6 = (f32[2,256,512]{2,1,0:T(8,128)S(1)}, f32[2,256,512]{2,1,0:T(8,128)}, u32[]{:S(2)}, u32[]{:S(2)}) collective-permute-start(f32[2,256,512]{2,1,0:T(8,128)S(1)} %pad_maximum_fusion.refs_6_), channel_id=1, source_target_pairs={{0,1},{1,0},{2,3},{3,2},{4,5},{5,4},{6,7},{7,6},{8,9},{9,8},{10,11... | collective-permute-start | bytes 3145736 | tf_op jit(solution)/shard_map/ppermute | solution.py:225
  89.8 33.6 %collective-permute-start.9 = (f32[2,4,128,128]{3,2,1,0:T(8,128)S(1)}, f32[2,4,128,128]{3,2,1,0:T(8,128)S(1)}, u32[]{:S(2)}, u32[]{:S(2)}) collective-permute-start(f32[2,4,128,128]{3,2,1,0:T(8,128)S(1)} %pad_maximum_fusion.1.refs_2_), channel_id=1, source_target_pairs={{0,128},{1,129},{2,130},{3,131},{4,132},{5,133},{6,134},{7,135},{8... | collective-permute-start | bytes 1572872 | tf_op jit(solution)/shard_map/ppermute | solution.py:225
  110.5 24.7 %collective-permute-start.10 = (f32[2,4,128,128]{3,2,1,0:T(8,128)S(1)}, f32[2,4,128,128]{3,2,1,0:T(8,128)S(1)}, u32[]{:S(2)}, u32[]{:S(2)}) collective-permute-start(f32[2,4,128,128]{3,2,1,0:T(8,128)S(1)} %pad_maximum_fusion.1.refs_2_), channel_id=1, source_target_pairs={{0,384},{1,385},{2,386},{3,387},{4,388},{5,389},{6,390},{7,391},{8... | collective-permute-start | bytes 1572872 | tf_op jit(solution)/shard_map/ppermute | solution.py:225
  115.5 21.6 %collective-permute-start.11 = (f32[2,4,128,128]{3,2,1,0:T(8,128)S(1)}, f32[2,4,128,128]{3,2,1,0:T(8,128)S(1)}, u32[]{:S(2)}, u32[]{:S(2)}) collective-permute-start(f32[2,4,128,128]{3,2,1,0:T(8,128)S(1)} %pad_maximum_fusion.1.refs_2_), channel_id=1, source_target_pairs={{0,256},{1,257},{2,258},{3,259},{4,260},{5,261},{6,262},{7,263},{8... | collective-permute-start | bytes 1572872 | tf_op jit(solution)/shard_map/ppermute | solution.py:225
  119.7 31.8 %collective-permute-start.12 = (f32[2,4,128,128]{3,2,1,0:T(8,128)S(1)}, f32[2,4,128,128]{3,2,1,0:T(8,128)S(1)}, u32[]{:S(2)}, u32[]{:S(2)}) collective-permute-start(f32[2,4,128,128]{3,2,1,0:T(8,128)S(1)} %pad_maximum_fusion.1.refs_2_), channel_id=1, source_target_pairs={{0,1},{1,0},{2,3},{3,2},{4,5},{5,4},{6,7},{7,6},{8,9},{9,8},{10,11... | collective-permute-start | bytes 1572872 | tf_op jit(solution)/shard_map/ppermute | solution.py:225
  123.5 28.0 %collective-permute-start.13 = (f32[2,4,128,128]{3,2,1,0:T(8,128)S(1)}, f32[2,4,128,128]{3,2,1,0:T(8,128)S(1)}, u32[]{:S(2)}, u32[]{:S(2)}) collective-permute-start(f32[2,4,128,128]{3,2,1,0:T(8,128)S(1)} %collective-permute-done.9.refs_3_), channel_id=1, source_target_pairs={{0,1},{1,0},{2,3},{3,2},{4,5},{5,4},{6,7},{7,6},{8,9},{9,8},{10,11... | collective-permute-start | bytes 1572872 | tf_op jit(solution)/shard_map/ppermute | solution.py:225
  135.2 16.3 %collective-permute-start.14 = (f32[2,4,128,128]{3,2,1,0:T(8,128)S(1)}, f32[2,4,128,128]{3,2,1,0:T(8,128)S(1)}, u32[]{:S(2)}, u32[]{:S(2)}) collective-permute-start(f32[2,4,128,128]{3,2,1,0:T(8,128)S(1)} %collective-permute-done.10.refs_4_), channel_id=1, source_target_pairs={{0,1},{1,0},{2,3},{3,2},{4,5},{5,4},{6,7},{7,6},{8,9},{9,8},{10,11... | collective-permute-start | bytes 1572872 | tf_op jit(solution)/shard_map/ppermute | solution.py:225
  137.1 14.4 %collective-permute-start.15 = (f32[2,4,128,128]{3,2,1,0:T(8,128)S(1)}, f32[2,4,128,128]{3,2,1,0:T(8,128)S(1)}, u32[]{:S(2)}, u32[]{:S(2)}) collective-permute-start(f32[2,4,128,128]{3,2,1,0:T(8,128)S(1)} %collective-permute-done.11.refs_5_), channel_id=1, source_target_pairs={{0,1},{1,0},{2,3},{3,2},{4,5},{5,4},{6,7},{7,6},{8,9},{9,8},{10,11... | collective-permute-start | bytes 1572872 | tf_op jit(solution)/shard_map/ppermute | solution.py:225
  154.8 17.2 %collective-permute-start.17 = (f32[128,512]{1,0:T(8,128)S(1)}, f32[128,512]{1,0:T(8,128)S(1)}, u32[]{:S(2)}, u32[]{:S(2)}) collective-permute-start(f32[128,512]{1,0:T(8,128)S(1)} %get-tuple-element.19), channel_id=1, source_target_pairs={{0,4},{1,5},{2,6},{3,7},{4,0},{5,1},{6,2},{7,3},{8,12},{9,13},{10,... | collective-permute-start | bytes 786440 | tf_op jit(solution)/shard_map/ppermute | solution.py:225
  158.7 13.3 %collective-permute-start.18 = (f32[128,512]{1,0:T(8,128)S(1)}, f32[128,512]{1,0:T(8,128)S(1)}, u32[]{:S(2)}, u32[]{:S(2)}) collective-permute-start(f32[128,512]{1,0:T(8,128)S(1)} %get-tuple-element.20), channel_id=1, source_target_pairs={{0,12},{1,13},{2,14},{3,15},{4,8},{5,9},{6,10},{7,11},{8,4},{9,5},... | collective-permute-start | bytes 786440 | tf_op jit(solution)/shard_map/ppermute | solution.py:225
  165.5 9.6 %collective-permute-start.16 = (f32[128,512]{1,0:T(8,128)S(1)}, f32[128,512]{1,0:T(8,128)S(1)}, u32[]{:S(2)}, u32[]{:S(2)}) collective-permute-start(f32[128,512]{1,0:T(8,128)S(1)} %get-tuple-element.18), channel_id=1, source_target_pairs={{0,8},{1,9},{2,10},{3,11},{4,12},{5,13},{6,14},{7,15},{8,0},{9,1},... | collective-permute-start | bytes 786440 | tf_op jit(solution)/shard_map/ppermute | solution.py:225
